TPU v7x, 32 devices: a whole 2x2x4 slice. The times are simulated.
32 devices in a mesh: row: 8 (over y, x, core), col: 4 (over z).
Axes of the slice: x: 2, y: 2, z: 4, core: 2. Of those that a mesh axis runs over, the one named last changes fastest.
Arguments:
- block_vecs: float32 [16, 16384], P(None, ('col', 'row')), may hold values from -130 to 130
- direction: float32 [16, 16384], P(None, ('col', 'row')), may hold values from -130 to 130
- blocks: bfloat16 [128, 16, 128, 128], P('col', 'row'), may hold values from 0 to 4
- block_cols: int32 [128, 16], P('col', 'row'), may hold values from 0 to 127, as said below
- live_counts: int32 [128, 8], P('col', 'row'), may hold values from 1 to 2, as said below
Outputs:
- x_next: float32 [16, 16384], P(None, ('col', 'row'))
- reduced: float32 [48, 48], replicated
- residual: float32 [16, 16384], P(None, ('col', 'row'))
Inputs may be any that keep to these rules, and one draw needn't show every extreme that they name: `block_cols`: A block column index g in slots 2 * r to 2 * r + 1 of any block row satisfies (g // 4) mod 8 == r. `live_counts`: every block row has 2 live slots in at least one segment.
All inputs are finite; a program needn't handle non-finite values.
Results may differ from a plain program's by a relative error of at most 0.0003.
Values sent between devices are 32-bit elements; how exact they have to be, the bound alone decides.
No kernel may reach another device: no remote copies, remote signals or barrier semaphores. Data moves between devices by JAX's collectives and lax.ppermute only.
A program may use at most 64 MiB of HBM per device.

v0:
```python
import math

import jax
import jax.numpy as jnp
from jax import lax
from jax.sharding import PartitionSpec as P

highest = lax.Precision.HIGHEST


def outer(left, right):
    return jnp.dot(left, right.T, precision=highest, preferred_element_type=jnp.float32)


def cholesky_lower(matrix):
    order_small = matrix.shape[0]
    places = jnp.arange(order_small, dtype=jnp.int32)

    def column_step(step, lower):
        pick = (places == step).astype(jnp.float32)
        row_now = jnp.sum(lower * pick[:, None], axis=0)
        column_now = jnp.sum(matrix * pick[None, :], axis=1)
        pivot = jnp.sum(column_now * pick) - jnp.sum(row_now * row_now)
        pivot_root = jnp.sqrt(pivot)
        below = (column_now - jnp.sum(lower * row_now[None, :], axis=1)) / pivot_root
        values = jnp.where(places > step, below, jnp.where(places == step, pivot_root, 0.0))
        return lower + values[:, None] * pick[None, :]

    return lax.fori_loop(0, order_small, column_step, jnp.zeros_like(matrix))


def solve_lower(lower, right):
    order_small = lower.shape[0]
    places = jnp.arange(order_small, dtype=jnp.int32)

    def row_step(step, solved):
        pick = (places == step).astype(jnp.float32)
        row_now = jnp.sum(lower * pick[:, None], axis=0)
        pivot = jnp.sum(row_now * pick)
        right_row = jnp.sum(right * pick[:, None], axis=0)
        value = (right_row - jnp.sum(row_now[:, None] * solved, axis=0)) / pivot
        return solved + pick[:, None] * value[None, :]

    return lax.fori_loop(0, order_small, row_step, jnp.zeros_like(right))


def solve_upper_t(lower, right):
    order_small = lower.shape[0]
    places = jnp.arange(order_small, dtype=jnp.int32)

    def row_step(count, solved):
        step = order_small - 1 - count
        pick = (places == step).astype(jnp.float32)
        column_now = jnp.sum(lower * pick[None, :], axis=1)
        pivot = jnp.sum(column_now * pick)
        right_row = jnp.sum(right * pick[:, None], axis=0)
        value = (right_row - jnp.sum(column_now[:, None] * solved, axis=0)) / pivot
        return solved + pick[:, None] * value[None, :]

    return lax.fori_loop(0, order_small, row_step, jnp.zeros_like(right))


def local_layout(block_cols, live_counts, span_rows, block_size, row_count):
    per_span = span_rows // block_size
    span_index = block_cols // per_span
    local_cols = span_index // row_count * per_span + block_cols % per_span
    slot_count = block_cols.shape[1]
    live_mask = (jnp.arange(slot_count, dtype=jnp.int32)[None, :] < live_counts).astype(jnp.float32)
    return (local_cols, live_mask)


def forward_part(col_panel, blocks, local_cols, live_mask):
    vec_width = col_panel.shape[0]
    block_size = blocks.shape[2]
    col_blocks = col_panel.reshape(vec_width, -1, block_size)
    picked = col_blocks[:, local_cols, :] * live_mask[None, :, :, None]
    forward = jnp.einsum(
        "vbkj,bkij->vbi", picked, blocks, precision=highest, preferred_element_type=jnp.float32
    )
    return 0.5 * forward.reshape(vec_width, -1)


def backward_part(row_panel, col_length, blocks, local_cols, live_mask):
    vec_width = row_panel.shape[0]
    block_size = blocks.shape[2]
    row_blocks = row_panel.reshape(vec_width, -1, block_size)
    backward = (
        jnp.einsum(
            "vbi,bkij->vbkj",
            row_blocks,
            blocks,
            precision=highest,
            preferred_element_type=jnp.float32,
        )
        * live_mask[None, :, :, None]
    )
    spread = jnp.zeros((vec_width, col_length // block_size, block_size), jnp.float32)
    spread = spread.at[:, local_cols.reshape(-1), :].add(
        backward.reshape(vec_width, -1, block_size)
    )
    return 0.5 * spread.reshape(vec_width, -1)


def per_device(block_vecs, direction, blocks, block_cols, live_counts):
    row_count = lax.axis_size("row")
    col_count = lax.axis_size("col")
    vec_width = block_vecs.shape[0]
    span_rows = block_vecs.shape[1]
    order_total = span_rows * row_count * col_count
    col_length = span_rows * col_count
    block_size = blocks.shape[2]
    local_cols, live_mask = local_layout(block_cols, live_counts, span_rows, block_size, row_count)
    paired = jnp.concatenate([block_vecs, direction], axis=0)
    pair_cols = lax.all_gather(paired, "col", axis=1, tiled=True)
    pair_rows = lax.all_gather(paired, "row", axis=1, tiled=True)
    forward = forward_part(pair_cols, blocks, local_cols, live_mask)
    backward = backward_part(pair_rows, col_length, blocks, local_cols, live_mask)
    image_pair = lax.psum_scatter(
        forward, "row", scatter_dimension=1, tiled=True
    ) + lax.psum_scatter(backward, "col", scatter_dimension=1, tiled=True)
    image_x = image_pair[:vec_width]
    image_p = image_pair[vec_width:]
    gram_x, cross_x = lax.psum(
        (outer(block_vecs, block_vecs), outer(block_vecs, image_x)), ("row", "col")
    )
    factor_x = cholesky_lower(gram_x)
    coefficient = solve_upper_t(factor_x, solve_lower(factor_x, cross_x))
    resid = image_x - jnp.dot(
        coefficient.T, block_vecs, precision=highest, preferred_element_type=jnp.float32
    )
    basis = jnp.concatenate([block_vecs, resid, direction], axis=0)
    resid_cols = lax.all_gather(resid, "col", axis=1, tiled=True)
    resid_rows = lax.all_gather(resid, "row", axis=1, tiled=True)
    forward_r = forward_part(resid_cols, blocks, local_cols, live_mask)
    column_x = outer(basis, image_x)
    column_p = outer(basis, image_p)
    backward_r = backward_part(resid_rows, col_length, blocks, local_cols, live_mask)
    image_r = lax.psum_scatter(
        forward_r, "row", scatter_dimension=1, tiled=True
    ) + lax.psum_scatter(backward_r, "col", scatter_dimension=1, tiled=True)
    column_r = outer(basis, image_r)
    gram_apply = jnp.concatenate([column_x, column_r, column_p], axis=1)
    gram_basis, gram_apply = lax.psum((outer(basis, basis), gram_apply), ("row", "col"))
    factor = cholesky_lower(gram_basis)
    halfway = solve_lower(factor, 0.5 * (gram_apply + gram_apply.T))
    reduced = solve_lower(factor, halfway.T)
    shifted = reduced + 3.0 * jnp.eye(3 * vec_width, dtype=jnp.float32)
    target = jnp.dot(
        shifted, shifted[:, :vec_width], precision=highest, preferred_element_type=jnp.float32
    )
    mixing = solve_upper_t(factor, target)
    fresh = jnp.dot(mixing.T, basis, precision=highest, preferred_element_type=jnp.float32)
    gram_fresh = jnp.dot(target.T, target, precision=highest, preferred_element_type=jnp.float32)
    factor_fresh = cholesky_lower(gram_fresh)
    x_next = math.sqrt(order_total) * solve_lower(factor_fresh, fresh)
    return (x_next, reduced, resid)


def solution(mesh):
    return jax.shard_map(
        per_device,
        mesh=mesh,
        in_specs=(
            P(None, ("col", "row")),
            P(None, ("col", "row")),
            P("col", "row", None, None),
            P("col", "row"),
            P("col", "row"),
        ),
        out_specs=(P(None, ("col", "row")), P(), P(None, ("col", "row"))),
        check_vma=False,
    )
```

profile of v0, /device:TPU:0, one launch (start us, length us, event | category | flops | bytes accessed | tf_op | source)
XLA Modules:
  0.0 742.8 jit_solution(14944574673817787883)
XLA Ops:
  7.2 0.9 fusion.58
  8.1 0.8 constant_dynamic-update-slice_fusion.1
  9.6 11.3 %all_gather.13 = f32[32,4096]{1,0:T(8,128)S(1)} all-gather(f32[32,512]{1,0:T(8,128)S(1)} %constant_dynamic-update-slice_fusion), channel_id=1, replica_groups=mesh['row'=8,'col'=4] {'row'}, dimensions={1}, use_global_device_ids=true | all-gather | bytes 589824 | tf_op jit(solution)/shard_map/all_gather | solution.py:115
  20.9 0.9 copy.56
  22.7 2.2 convolution_multiply_fusion
  25.0 3.2 scatter_fusion
  28.4 0.8 copy.71
  29.4 15.4 %all_gather.12 = f32[32,2048]{1,0:T(8,128)S(1)} all-gather(f32[32,512]{1,0:T(8,128)S(1)} %constant_dynamic-update-slice_fusion), channel_id=1, replica_groups=mesh['row'=8,'col'=4] {'col'}, dimensions={1}, use_global_device_ids=true | all-gather | bytes 327680 | tf_op jit(solution)/shard_map/all_gather | solution.py:114
  45.5 2.2 fusion.37
  47.7 0.8 copy.70
  48.8 1.5 reduce-scatter.7.cloned.1.call-done
  50.3 35.9 %reduce-scatter.5.cloned.1.call-done = f32[32,512]{1,0:T(8,128)} async-done(((f32[32,4096]{1,0:T(8,128)}), f32[32,512]{1,0:T(8,128)}) %reduce-scatter.5.cloned.1.call-update) | async-done | bytes 65552 | tf_op jit(solution)/shard_map/reduce_scatter | solution.py:118
  86.2 0.9 add.269
  87.3 39.4 %all-reduce.1 = (f32[16,16]{0,1:T(8,128)S(1)}, f32[16,16]{1,0:T(8,128)S(1)}) all-reduce(f32[16,16]{0,1:T(8,128)S(1)} %convolution_bitcast_fusion.2, f32[16,16]{1,0:T(8,128)S(1)} %fusion.64), channel_id=1, replica_groups=mesh['row'=8,'col'=4] {'row','col'}, use_global_device_ids=true, to_apply=%region_11.12 | all-reduce | flops 512 | bytes 4096 | tf_op jit(solution)/shard_map/psum | solution.py:123
  126.7 37.0 %while.135 = (s32[]{:T(128)}, f32[16,16]{1,0:T(8,128)S(1)}, f32[16,16]{1,0:T(8,128)S(1)}, s32[]{:T(128)}, s32[]{:T(128)}) while((s32[]{:T(128)}, f32[16,16]{1,0:T(8,128)S(1)}, f32[16,16]{1,0:T(8,128)S(1)}, s32[]{:T(128)}, s32[]{:T(128)}) %tuple.302), condition=%wide.region_10.11_spmd.clone.clone, body=%wide.region_4.10_spmd.clone.clone.sunk | while | flops 2978 | bytes 6069 | solution.py:29
  163.8 26.3 %while.129 = (s32[]{:T(128)}, f32[16,16]{1,0:T(8,128)S(1)}, f32[16,16]{1,0:T(8,128)S(1)}, f32[16,16]{1,0:T(8,128)S(1)}, s32[]{:T(128)}, /*index=5*/s32[]{:T(128)}) while((s32[]{:T(128)}, f32[16,16]{1,0:T(8,128)S(1)}, f32[16,16]{1,0:T(8,128)S(1)}, f32[16,16]{1,0:T(8,128)S(1)}, s32[]{:T(128)}, /*index=5*/s32[]{:T(128)}) %tuple.305), condition=%wide.region_17.18_spmd.clone, body=%wide.region_12.17_spmd.clone.sunk | while | flops 2626 | bytes 5984 | solution.py:44
  190.0 26.8 %while.130 = (s32[]{:T(128)}, f32[16,16]{1,0:T(8,128)S(1)}, f32[16,16]{1,0:T(8,128)S(1)}, f32[16,16]{1,0:T(8,128)S(1)}, s32[]{:T(128)}, /*index=5*/s32[]{:T(128)}, s32[]{:T(128)}) while((s32[]{:T(128)}, f32[16,16]{1,0:T(8,128)S(1)}, f32[16,16]{1,0:T(8,128)S(1)}, f32[16,16]{1,0:T(8,128)S(1)}, s32[]{:T(128)}, ...), condition=%wide.region_23.24_spmd.clone, body=%wide.region_18.23_spmd.clone.sunk | while | flops 2627 | bytes 6004 | solution.py:60
  217.0 10.1 %all_gather.15 = f32[16,4096]{1,0:T(8,128)S(1)} all-gather(f32[16,512]{1,0:T(8,128)S(1)} %convolution_subtract_fusion), channel_id=1, replica_groups=mesh['row'=8,'col'=4] {'row'}, dimensions={1}, use_global_device_ids=true | all-gather | bytes 294912 | tf_op jit(solution)/shard_map/all_gather | solution.py:133
  227.2 13.4 %all_gather.14 = f32[16,2048]{1,0:T(8,128)S(1)} all-gather(f32[16,512]{1,0:T(8,128)S(1)} %convolution_subtract_fusion), channel_id=1, replica_groups=mesh['row'=8,'col'=4] {'col'}, dimensions={1}, use_global_device_ids=true | all-gather | bytes 163840 | tf_op jit(solution)/shard_map/all_gather | solution.py:132
  240.6 1.0 convolution_multiply_fusion.1
  241.7 2.9 scatter_fusion.1
  246.0 1.8 fusion.39
  249.1 14.7 %reduce-scatter.11.cloned.1.call-done = f32[16,512]{1,0:T(8,128)} async-done(((f32[16,2048]{1,0:T(8,128)}), f32[16,512]{1,0:T(8,128)}) %reduce-scatter.11.cloned.1.call-update) | async-done | bytes 32784 | tf_op jit(solution)/shard_map/reduce_scatter | solution.py:140
  263.9 34.8 %reduce-scatter.9.cloned.1.call-done = f32[16,512]{1,0:T(8,128)} async-done(((f32[16,4096]{1,0:T(8,128)}), f32[16,512]{1,0:T(8,128)}) %reduce-scatter.9.cloned.1.call-update) | async-done | bytes 32784 | tf_op jit(solution)/shard_map/reduce_scatter | solution.py:138
  298.6 0.9 fusion.50
  299.6 39.9 %all-reduce = (f32[48,48]{0,1:T(8,128)S(1)}, f32[48,48]{1,0:T(8,128)S(1)}) all-reduce(f32[48,48]{0,1:T(8,128)S(1)} %pad_maximum_fusion.1, f32[48,48]{1,0:T(8,128)S(1)} %fusion.62), channel_id=1, replica_groups=mesh['row'=8,'col'=4] {'row','col'}, use_global_device_ids=true, to_apply=%region_35.36 | all-reduce | flops 4608 | bytes 36864 | tf_op jit(solution)/shard_map/psum | solution.py:143
  339.7 109.8 %while.136 = (s32[]{:T(128)}, f32[48,48]{1,0:T(8,128)S(1)}, f32[48,48]{1,0:T(8,128)S(1)}, s32[]{:T(128)}, s32[]{:T(128)}) while((s32[]{:T(128)}, f32[48,48]{1,0:T(8,128)S(1)}, f32[48,48]{1,0:T(8,128)S(1)}, s32[]{:T(128)}, s32[]{:T(128)}) %tuple.311), condition=%wide.region_31.32_spmd.clone.clone, body=%wide.region_25.31_spmd.clone.clone.sunk | while | flops 25826 | bytes 48693 | solution.py:29
  449.5 73.5 %while.131 = (s32[]{:T(128)}, f32[48,48]{1,0:T(8,128)S(1)}, f32[48,48]{1,0:T(8,128)S(1)}, f32[48,48]{1,0:T(8,128)S(1)}, s32[]{:T(128)}, /*index=5*/s32[]{:T(128)}) while((s32[]{:T(128)}, f32[48,48]{1,0:T(8,128)S(1)}, f32[48,48]{1,0:T(8,128)S(1)}, f32[48,48]{1,0:T(8,128)S(1)}, s32[]{:T(128)}, /*index=5*/s32[]{:T(128)}) %tuple.314), condition=%wide.region_41.42_spmd.clone, body=%wide.region_36.41_spmd.clone.sunk | while | flops 23234 | bytes 48480 | solution.py:44
  523.0 73.5 %while.132 = (s32[]{:T(128)}, f32[48,48]{1,0:T(8,128)S(1)}, f32[48,48]{1,0:T(8,128)S(1)}, f32[48,48]{1,0:T(8,128)S(1)}, s32[]{:T(128)}, /*index=5*/s32[]{:T(128)}) while((s32[]{:T(128)}, f32[48,48]{1,0:T(8,128)S(1)}, f32[48,48]{1,0:T(8,128)S(1)}, f32[48,48]{1,0:T(8,128)S(1)}, s32[]{:T(128)}, /*index=5*/s32[]{:T(128)}) %tuple.340), condition=%wide.region_47.48_spmd.clone, body=%wide.region_42.47_spmd.clone.sunk | while | flops 23234 | bytes 48480 | solution.py:44
  596.9 75.8 %while.133 = (s32[]{:T(128)}, f32[48,16]{0,1:T(8,128)S(1)}, f32[48,16]{0,1:T(8,128)S(1)}, f32[48,48]{1,0:T(8,128)S(1)}, s32[]{:T(128)}, /*index=5*/s32[]{:T(128)}, s32[]{:T(128)}) while((s32[]{:T(128)}, f32[48,16]{0,1:T(8,128)S(1)}, f32[48,16]{0,1:T(8,128)S(1)}, f32[48,48]{1,0:T(8,128)S(1)}, s32[]{:T(128)}, ...), condition=%wide.region_60.61_spmd.clone, body=%wide.region_55.60_spmd.clone.sunk | while | flops 10947 | bytes 23348 | solution.py:60
  672.8 38.5 %while.137 = (s32[]{:T(128)}, f32[16,16]{1,0:T(8,128)S(1)}, f32[16,16]{1,0:T(8,128)S(1)}, s32[]{:T(128)}, s32[]{:T(128)}) while((s32[]{:T(128)}, f32[16,16]{1,0:T(8,128)S(1)}, f32[16,16]{1,0:T(8,128)S(1)}, s32[]{:T(128)}, s32[]{:T(128)}) %tuple.323), condition=%wide.region_54.55_spmd.clone.clone, body=%wide.region_48.54_spmd.clone.clone.sunk | while | flops 2978 | bytes 6069 | solution.py:29
  711.3 24.3 %while.134 = (s32[]{:T(128)}, f32[16,512]{1,0:T(8,128)S(1)}, f32[16,512]{1,0:T(8,128)S(1)}, f32[16,16]{1,0:T(8,128)S(1)}, s32[]{:T(128)}, /*index=5*/s32[]{:T(128)}) while((s32[]{:T(128)}, f32[16,512]{1,0:T(8,128)S(1)}, f32[16,512]{1,0:T(8,128)S(1)}, f32[16,16]{1,0:T(8,128)S(1)}, s32[]{:T(128)}, /*index=5*/s32[]{:T(128)}) %tuple.326), condition=%wide.region_66.67_spmd.clone, body=%wide.region_61.66_spmd.clone.sunk | while | flops 66114 | bytes 144928 | solution.py:44
  (1706 shorter events, 382.3 us)
Async XLA Ops:
  7.2 15.6 %copy-start = (bf16[32,2,128,128]{3,2,1,0:T(8,128)(2,1)S(1)}, bf16[32,2,128,128]{3,2,1,0:T(8,128)(2,1)}, u32[]{:S(2)}) copy-start(bf16[32,2,128,128]{3,2,1,0:T(8,128)(2,1)} %param.25) | copy-start | bytes 6291460
  7.2 43.1 %reduce-scatter.7.cloned.1.call-start = ((), (), s32[]{:S(2)}) async-start(), calls=%async_computation.5 | async-start | bytes 327680 | tf_op jit(solution)/shard_map/reduce_scatter | solution.py:120
  8.1 37.4 %copy-start.5 = (f32[32,2]{1,0:T(8,128)}, f32[32,2]{1,0:T(8,128)S(1)}, u32[]{:S(2)}) copy-start(f32[32,2]{1,0:T(8,128)S(1)} %fusion.58) | copy-start | bytes 772
  22.7 5.4 copy-start.9
  29.2 57.1 %reduce-scatter.5.cloned.1.call-start = ((), (), s32[]{:S(2)}) async-start(), calls=%async_computation.4 | async-start | bytes 589824 | tf_op jit(solution)/shard_map/reduce_scatter | solution.py:118
  29.4 16.0 %copy-start.7 = (s32[1024]{0:T(1024)}, s32[1024]{0:T(1024)S(1)}, u32[]{:S(2)}) copy-start(s32[1024]{0:T(1024)S(1)} %pad_clamp_fusion) | copy-start | bytes 12292
  45.5 3.2 copy-start.2
  47.7 192.9 %copy-start.6 = (f32[32,2]{1,0:T(8,128)S(1)}, f32[32,2]{1,0:T(8,128)}, u32[]{:S(2)}) copy-start(f32[32,2]{1,0:T(8,128)} %copy-done.5) | copy-start | bytes 772
  48.5 215.3 %reduce-scatter.11.cloned.1.call-start = ((), (), s32[]{:S(2)}) async-start(), calls=%async_computation.7 | async-start | bytes 163840 | tf_op jit(solution)/shard_map/reduce_scatter | solution.py:140
  216.8 24.9 %copy-start.10 = (s32[64]{0:T(128)S(1)}, s32[64]{0:T(128)}, u32[]{:S(2)}) copy-start(s32[64]{0:T(128)} %copy-done.9) | copy-start | bytes 772
  217.0 455.6 %copy-start.3 = (f32[16,512]{1,0:T(8,128)}, f32[16,512]{1,0:T(8,128)S(1)}, u32[]{:S(2)}) copy-start(f32[16,512]{1,0:T(8,128)S(1)} %convolution_subtract_fusion) | copy-start | bytes 98308
  240.6 4.8 copy-start.8
  245.3 53.4 %reduce-scatter.9.cloned.1.call-start = ((), (), s32[]{:S(2)}) async-start(), calls=%async_computation.6 | async-start | bytes 294912 | tf_op jit(solution)/shard_map/reduce_scatter | solution.py:138
  246.0 2.5 copy-start.4
  596.5 139.8 %copy-start.1 = (f32[48,48]{1,0:T(8,128)}, f32[48,48]{1,0:T(8,128)S(1)}, u32[]{:S(2)}) copy-start(f32[48,48]{1,0:T(8,128)S(1)} %get-tuple-element.811) | copy-start | bytes 27652
Sparse Core Ops, SparseCore 0:
  29.3 20.9 reduce-scatter.6
  53.4 32.8 reduce-scatter.4
  245.4 18.4 reduce-scatter.10
  266.7 31.8 reduce-scatter.8
where the time goes:
time: 748 us; the launch traced here: 743 us
  other arithmetic  385 us (51%)
  blocking collectives  129 us (17%)
  loops' own time  111 us (15%)
  waiting for transfers between devices  87 us (12%)
  between operations  14.1 us (2%)
  matrix products  9.73 us (1%)
    another operation x3, loops' own time, cholesky_lower(): return lax.fori_loop(0, order_small, column_step, jnp.zeros_like(matrix))  108 us
    div x128, other arithmetic, row_step(): value = (right_row - jnp.sum(row_now[:, None] * solved, axis=0)) / pivot  83.7 us
    reduce_sum x128, other arithmetic, row_step(): pivot = jnp.sum(row_now * pick)  78 us
    reduce_sum x80, other arithmetic, column_step(): pivot = jnp.sum(column_now * pick) - jnp.sum(row_now * row_now)  51.4 us
    div x64, other arithmetic, row_step(): value = (right_row - jnp.sum(column_now[:, None] * solved, axis=0)) / pivot  42.2 us
    psum x1, blocking collectives, per_device(): lax.psum((outer(basis, basis), gram_apply), ('row', 'col'))  39.9 us
    reduce_sum x64, other arithmetic, row_step(): pivot = jnp.sum(column_now * pick)  39.8 us
    psum x1, blocking collectives, per_device(): lax.psum((outer(block_vecs, block_vecs), outer(block_vecs, image_x)), ('r...  39.4 us
  transfers between devices with their start and end apart: 4, of which 4 were waited for; matrix products, arithmetic and copies ran while one was open for 1% of the time, Pallas kernels for 0%

commit v1 on v0

v1 whole, which is shorter than its diff:
```python
import functools
import math

import jax
import jax.numpy as jnp
from jax import lax
from jax.experimental import pallas as pl
from jax.experimental.pallas import tpu as pltpu
from jax.sharding import PartitionSpec as P

highest = lax.Precision.HIGHEST
f32 = jnp.float32
bf16 = jnp.bfloat16
VMEM = pltpu.MemorySpace.VMEM
SMEM = pltpu.MemorySpace.SMEM
LANES = 128


def dot_nt(a, b, precision=highest):
    return lax.dot_general(
        a, b, (((1,), (1,)), ((), ())), precision=precision, preferred_element_type=f32
    )


def dot_nn(a, b, precision=highest):
    return lax.dot_general(
        a, b, (((1,), (0,)), ((), ())), precision=precision, preferred_element_type=f32
    )


def dot_tn(a, b, precision=highest):
    return lax.dot_general(
        a, b, (((0,), (0,)), ((), ())), precision=precision, preferred_element_type=f32
    )


def split(x):
    hi = x.astype(bf16)
    lo = (x - hi.astype(f32)).astype(bf16)
    return hi, lo


def split_rows(x):
    hi, lo = split(x)
    return jnp.concatenate([hi, lo], axis=0)


def eye(n):
    return (
        lax.broadcasted_iota(jnp.int32, (n, n), 0) == lax.broadcasted_iota(jnp.int32, (n, n), 1)
    ).astype(f32)


def eliminate(stack, n):
    m = stack.shape[1]
    row_at = lax.broadcasted_iota(jnp.int32, (n, m), 0)
    lane_at = lax.broadcasted_iota(jnp.int32, (n, m), 1)
    for j in range(n - 1):
        row = stack[j : j + 1, :]
        pivot = stack[j : j + 1, j : j + 1]
        column = jnp.broadcast_to(stack[:, j : j + 1], (n, m))
        scaled = row / pivot
        stack = stack - jnp.where(row_at > j, column, 0.0) * scaled
    diagonal = jnp.sum(jnp.where(row_at == lane_at, stack, 0.0), axis=1, keepdims=True)
    return stack / jnp.sqrt(diagonal)


def place(block_cols_ref, b, k, me_col, per_span, row_count):
    g = block_cols_ref[b, k]
    span = lax.div(g, per_span)
    return (lax.div(span, row_count) ^ me_col) * per_span + lax.rem(g, per_span)


def first_kernel(
    row_count, col_count, slots, width, bs,
    block_cols_ref, live_ref, rows_ref, *rest,
):
    col_refs = rest[:col_count]
    blocks_ref = rest[col_count]
    fr_ref, fp_ref = rest[col_count + 1 : col_count + 3]
    bk_refs = rest[col_count + 3 : 2 * col_count + 3]
    picks, spread = rest[2 * col_count + 3 :]
    span_rows = rows_ref.shape[2]
    per_span = span_rows // bs
    me_col = lax.axis_index("col")
    for s in range(col_count):
        for o in range(per_span):
            picks[s * per_span + o] = split_rows(col_refs[s][:, o * bs : (o + 1) * bs])
    spread[...] = jnp.zeros_like(spread)

    def span_step(q, cross):
        panel = rows_ref[q]
        own = split_rows(panel[:width])
        parts = []
        for o in range(per_span):
            b = q * per_span + o
            tiles, chosen, weights, where = [], [], [], []
            for k in range(slots):
                w = (k < live_ref[b, 0]).astype(f32)
                at = place(block_cols_ref, b, k, me_col, per_span, row_count)
                tiles.append(blocks_ref[b, k])
                chosen.append(picks[at] * w.astype(bf16))
                weights.append(w)
                where.append(at)
            tile = jnp.concatenate(tiles, axis=1)
            forward = dot_nt(jnp.concatenate(chosen, axis=1), tile, None)
            parts.append(forward[: 2 * width] + forward[2 * width :])
            back = dot_nn(own[:, o * bs : (o + 1) * bs], tile, None)
            back = back[:width] + back[width:]
            for k in range(slots):
                spread[where[k]] += back[:, k * bs : (k + 1) * bs] * weights[k]
        forward = jnp.concatenate(parts, axis=1)
        fr_ref[q, :, :span_rows] = forward[:width]
        fp_ref[q] = forward[width:]
        return cross + dot_nt(panel, forward)

    cross = lax.fori_loop(0, row_count, span_step, jnp.zeros((2 * width, 2 * width), f32))
    gram = dot_nt(col_refs[0][...], col_refs[0][...])
    extra = jnp.concatenate([gram[:width], gram[width:], cross[:width], cross[width:]], axis=1)
    for q in range(row_count):
        fr_ref[q, :, span_rows:] = extra
    for s in range(col_count):
        for o in range(per_span):
            bk_refs[s][:, o * bs : (o + 1) * bs] = spread[s * per_span + o]


def middle_kernel(row_count, col_count, got_ref, *rest):
    back_refs = rest[:col_count]
    out_ref, y_ref = rest[col_count:]
    span_rows = y_ref.shape[1]
    total = got_ref[0]
    for q in range(1, row_count):
        total = total + got_ref[q]
    back = back_refs[0][...]
    for s in range(1, col_count):
        back = back + back_refs[s][...]
    y = 0.5 * (total[:, :span_rows] + back)
    y_ref[...] = y
    out_ref[:, :span_rows] = y
    out_ref[:, span_rows:] = total[:, span_rows:]


def tree_sum(terms):
    while len(terms) > 1:
        terms = [terms[i] + terms[i + 1] for i in range(0, len(terms), 2)]
    return terms[0]


def second_kernel(
    row_count, col_count, slots, width, bs,
    block_cols_ref, live_ref, rows_ref, fp_ref, yrows_ref, *rest,
):
    col_refs = rest[:col_count]
    y_refs = rest[col_count : 2 * col_count]
    blocks_ref = rest[2 * col_count]
    resid_ref, part_ref, aux_ref = rest[2 * col_count + 1 : 2 * col_count + 4]
    picks, forward_r, resid_rows = rest[2 * col_count + 4 :]
    span_rows = rows_ref.shape[2]
    per_span = span_rows // bs
    me_col = lax.axis_index("col")
    me_row = lax.axis_index("row")

    sums = tree_sum([y_refs[s][:, span_rows:] for s in range(col_count)])
    gram_x = sums[:, :width]
    cross_x = sums[:, 4 * width : 5 * width]
    cross_x = 0.5 * (cross_x + cross_x.T)
    done = eliminate(jnp.concatenate([gram_x, cross_x, eye(width)], axis=1), width)
    inverse_l = done[:, 2 * width : 3 * width]
    coefficient = dot_tn(inverse_l, done[:, width : 2 * width])
    minus_c_t = -coefficient.T
    aux_ref[:, : sums.shape[1]] = sums
    aux_ref[:, sums.shape[1] :] = jnp.concatenate(
        [coefficient, jnp.zeros((width, sums.shape[1] - width), f32)], axis=1
    )
    for s in range(col_count):
        rest_s = y_refs[s][:, :span_rows] + dot_nn(minus_c_t, col_refs[s][:width, :])
        for o in range(per_span):
            picks[s * per_span + o] = split_rows(rest_s[:, o * bs : (o + 1) * bs])

    def span_step(q, carry):
        own, cross = carry
        rest_q = yrows_ref[q] + dot_nn(minus_c_t, rows_ref[q, :width, :])
        resid_rows[q] = rest_q
        parts = []
        for o in range(per_span):
            b = q * per_span + o
            tiles, chosen = [], []
            for k in range(slots):
                w = (k < live_ref[b, 0]).astype(f32)
                at = place(block_cols_ref, b, k, me_col, per_span, row_count)
                tiles.append(blocks_ref[b, k])
                chosen.append(picks[at] * w.astype(bf16))
            forward = dot_nt(
                jnp.concatenate(chosen, axis=1), jnp.concatenate(tiles, axis=1), None
            )
            parts.append(forward[:width] + forward[width:])
        forward = jnp.concatenate(parts, axis=1)
        own = own + dot_nt(forward, rest_q)
        cross = cross + dot_nt(forward, rows_ref[q, width:, :]) + dot_nt(rest_q, fp_ref[q])
        return own, cross

    zero = jnp.zeros((width, width), f32)
    own, cross = lax.fori_loop(0, row_count, span_step, (zero, zero))
    mine = resid_rows[me_row]
    resid_ref[...] = mine
    local = jnp.concatenate([col_refs[0][:width, :], mine, col_refs[0][width:, :]], axis=0)
    part = jnp.concatenate(
        [dot_nt(mine, local), own, 0.5 * cross, jnp.zeros((width, LANES - 5 * width), f32)],
        axis=1,
    )
    for d in range(part_ref.shape[0]):
        part_ref[d] = part


def last_kernel(width, scale, parts_ref, aux_ref, xp_ref, resid_ref, x_next_ref, reduced_ref):
    w = width
    total = parts_ref[0]
    for d in range(1, parts_ref.shape[0]):
        total = total + parts_ref[d]
    sums = aux_ref[:, :LANES]
    coefficient = aux_ref[:, LANES : LANES + w]
    piece = lambda array, i: array[:, i * w : (i + 1) * w]
    xx, xp, pp = piece(sums, 0), piece(sums, 1), piece(sums, 3)
    xbx, xbp, pbx, pbp = (piece(sums, i) for i in range(4, 8))
    rx, rr, rp, rbr, rap = (piece(total, i) for i in range(5))
    xr = rx.T
    gram_basis = jnp.concatenate(
        [
            jnp.concatenate([xx, xr, xp], axis=1),
            jnp.concatenate([rx, rr, rp], axis=1),
            jnp.concatenate([xp.T, rp.T, pp], axis=1),
        ],
        axis=0,
    )
    xax = 0.5 * (xbx + xbx.T)
    xap = 0.5 * (xbp + pbx.T)
    xar = rr + dot_tn(coefficient, xr)
    gram_apply = jnp.concatenate(
        [
            jnp.concatenate([xax, xar, xap], axis=1),
            jnp.concatenate([xar.T, 0.5 * (rbr + rbr.T), rap], axis=1),
            jnp.concatenate([xap.T, rap.T, 0.5 * (pbp + pbp.T)], axis=1),
        ],
        axis=0,
    )
    n = 3 * w
    inverse_l = eliminate(jnp.concatenate([gram_basis, eye(n)], axis=1), n)[:, n:]
    reduced = dot_nt(dot_nn(inverse_l, gram_apply), inverse_l)
    reduced_ref[...] = reduced
    shifted = reduced + 3.0 * eye(n)
    target = dot_nn(shifted, shifted[:, :w])
    gram_fresh = dot_tn(target, target)
    mixing = dot_tn(target, inverse_l)
    weights = scale * eliminate(jnp.concatenate([gram_fresh, mixing], axis=1), w)[:, w:]
    basis = jnp.concatenate([xp_ref[:w, :], resid_ref[...], xp_ref[w:, :]], axis=0)
    x_next_ref[...] = dot_nn(weights, basis)


def vmem_specs(n):
    return [pl.BlockSpec(memory_space=VMEM)] * n


def per_device(block_vecs, direction, blocks, block_cols, live_counts):
    row_count = lax.axis_size("row")
    col_count = lax.axis_size("col")
    width, span_rows = block_vecs.shape
    slots, bs = blocks.shape[1], blocks.shape[2]
    per_span = span_rows // bs
    order_total = span_rows * row_count * col_count
    col_blocks = col_count * per_span
    sizes = (row_count, col_count, slots, width, bs)

    def over_col(arrays):
        return [arrays[0]] + [
            lax.ppermute(arrays[s], "col", [(i, i ^ s) for i in range(col_count)])
            for s in range(1, col_count)
        ]

    shape = lambda *dims: jax.ShapeDtypeStruct(dims, f32)
    smem = [pl.BlockSpec(memory_space=SMEM)] * 2
    params = pltpu.CompilerParams(vmem_limit_bytes=48 * 1024 * 1024)

    pair = jnp.concatenate([block_vecs, direction], axis=0)
    pair_cols = over_col([pair] * col_count)
    pair_rows = lax.all_gather(pair, "row")
    first = pl.pallas_call(
        functools.partial(first_kernel, *sizes),
        in_specs=smem + vmem_specs(col_count + 2),
        out_specs=vmem_specs(col_count + 2),
        out_shape=[shape(row_count, width, span_rows + LANES), shape(row_count, width, span_rows)]
        + [shape(width, span_rows)] * col_count,
        scratch_shapes=[
            pltpu.VMEM((col_blocks, 4 * width, bs), bf16),
            pltpu.VMEM((col_blocks, width, bs), f32),
        ],
        compiler_params=params,
        name="first",
    )(block_cols, live_counts, pair_rows, *pair_cols, blocks)
    forward, forward_p, backs = first[0], first[1], first[2:]
    got_backs = over_col(backs)
    got = lax.all_to_all(forward, "row", 0, 0)
    message, image = pl.pallas_call(
        functools.partial(middle_kernel, row_count, col_count),
        in_specs=vmem_specs(col_count + 1),
        out_specs=vmem_specs(2),
        out_shape=[shape(width, span_rows + LANES), shape(width, span_rows)],
        compiler_params=params,
        name="middle",
    )(got, *got_backs)
    image_cols = over_col([message] * col_count)
    image_rows = lax.all_gather(image, "row")
    device_count = row_count * col_count
    resid, part, aux = pl.pallas_call(
        functools.partial(second_kernel, *sizes),
        in_specs=smem + vmem_specs(2 * col_count + 4),
        out_specs=vmem_specs(3),
        out_shape=[
            shape(width, span_rows),
            shape(device_count, width, LANES),
            shape(width, 2 * LANES),
        ],
        scratch_shapes=[
            pltpu.VMEM((col_blocks, 2 * width, bs), bf16),
            pltpu.VMEM((8, LANES), f32),
            pltpu.VMEM((row_count, width, span_rows), f32),
        ],
        compiler_params=params,
        name="second",
    )(block_cols, live_counts, pair_rows, forward_p, image_rows, *pair_cols, *image_cols, blocks)
    parts = lax.all_to_all(part, ("col", "row"), 0, 0)
    x_next, reduced = pl.pallas_call(
        functools.partial(last_kernel, width, math.sqrt(order_total)),
        in_specs=vmem_specs(4),
        out_specs=vmem_specs(2),
        out_shape=[shape(width, span_rows), shape(3 * width, 3 * width)],
        compiler_params=params,
        name="last",
    )(parts, aux, pair, resid)
    return (x_next, reduced, resid)


def solution(mesh):
    return jax.shard_map(
        per_device,
        mesh=mesh,
        in_specs=(
            P(None, ("col", "row")),
            P(None, ("col", "row")),
            P("col", "row", None, None),
            P("col", "row"),
            P("col", "row"),
        ),
        out_specs=(P(None, ("col", "row")), P(), P(None, ("col", "row"))),
        check_vma=False,
    )
```

time: 748 us -> 88.6 us (0.12)
  other arithmetic: 385 us -> 0 us
  loops' own time: 111 us -> 0 us
  blocking collectives: 129 us -> 32 us
  waiting for transfers between devices: 87 us -> 4.49 us
  Pallas kernels: 0 us -> 21.4 us
  starting transfers between devices: 0.16 us -> 18 us
  between operations: 14.1 us -> 0.69 us
  matrix products: 9.73 us -> 0 us
    reduce_sum x816 -> x0, other arithmetic: 226 us -> none  [the longest x128 78 us: row_step(): pivot = jnp.sum(row_now * pick)]
    div x192 -> x0, other arithmetic: 126 us -> none  [the longest x128 83.7 us: row_step(): value = (right_row - jnp.sum(row_now[:, None] * solved, axis=0)) / pivot]
    another operation x9 -> x0, loops' own time: 111 us -> none  [the longest x3 108 us: cholesky_lower(): return lax.fori_loop(0, order_small, column_step, jnp.zeros_like(matrix))]
    reduce_scatter x4 -> x0, waiting for transfers between devices: 86.9 us -> none  [the longest x1 35.9 us: per_device(): lax.psum_scatter(forward, 'row', scatter_dimension=1, tiled=True)]
    psum x2 -> x0, blocking collectives: 79.3 us -> none  [the longest x1 39.9 us: per_device(): lax.psum((outer(basis, basis), gram_apply), ('row', 'col'))]
    all_gather x4 -> x2, blocking collectives: 50.1 us -> 19.7 us  [the longest x1 10.1 us: per_device(): pair_rows = lax.all_gather(pair, 'row')]
    add x274 -> x0, other arithmetic: 21.6 us -> none  [the longest x192 14.6 us: row_step(): return solved + pick[:, None] * value[None, :]]
    pallas_call x0 -> x4, Pallas kernels: none -> 21.4 us  [the longest x1 8.73 us: per_device(): pl.pallas_call(functools.partial(second_kernel, *sizes), in_specs=smem +...]
  transfers between devices with their start and end apart: 4 -> 10, of which waited for: 4 -> 2; matrix products, arithmetic and copies ran while one was open for 1% -> 2% of each run, Pallas kernels for 0% -> 0%
where the time goes in v1:
time: 88.6 us; the launch traced here: 87.9 us
  blocking collectives  32 us (36%)
  Pallas kernels  21.4 us (24%)
  starting transfers between devices  18 us (20%)
  local copies, waits for them, and re-layouts  11.3 us (13%)
  waiting for transfers between devices  4.49 us (5%)
    ppermute x9, starting transfers between devices, over_col(): lax.ppermute(arrays[s], 'col', [(i, i ^ s) for i in range(col_count)])  14.5 us
    all_to_all x1, blocking collectives, per_device(): parts = lax.all_to_all(part, ('col', 'row'), 0, 0)  12.3 us
    unnamed x27, local copies, waits for them, and re-layouts  10.5 us
    all_gather x1, blocking collectives, per_device(): pair_rows = lax.all_gather(pair, 'row')  10.1 us
    all_gather x1, blocking collectives, per_device(): image_rows = lax.all_gather(image, 'row')  9.65 us
    pallas_call x1, Pallas kernels, per_device(): pl.pallas_call(functools.partial(second_kernel, *sizes), in_specs=smem +...  8.73 us
    pallas_call x1, Pallas kernels, per_device(): pl.pallas_call(functools.partial(last_kernel, width, math.sqrt(order_tota...  7.34 us
    pallas_call x1, Pallas kernels, per_device(): pl.pallas_call(functools.partial(first_kernel, *sizes), in_specs=smem + v...  5.34 us
  transfers between devices with their start and end apart: 10, of which 2 were waited for; matrix products, arithmetic and copies ran while one was open for 2% of the time, Pallas kernels for 0%

profile of v1, /device:TPU:0, one launch (start us, length us, event | category | flops | bytes accessed | tf_op | source)
XLA Modules:
  0.0 87.9 jit_solution(14191877816768773762)
XLA Ops:
  0.6 0.8 constant_dynamic-update-slice_fusion.1
  1.4 0.8 constant_dynamic-update-slice_fusion.rest_0_.xp_ref
  2.2 5.1 %collective-permute-start.2 = (f32[32,512]{1,0:T(8,128)S(1)}, f32[32,512]{1,0:T(8,128)S(1)}, u32[]{:S(2)}, u32[]{:S(2)}) collective-permute-start(f32[32,512]{1,0:T(8,128)S(1)} %constant_dynamic-update-slice_fusion.rest_0_.xp_ref), channel_id=1, source_target_pairs={{0,3},{1,2},{2,1},{3,0},{4,7},{5,6},{6,5},{7,4},{8,11},{9,10},{10,... | collective-permute-start | bytes 196616 | tf_op jit(solution)/shard_map/ppermute | solution.py:275
  7.2 0.6 collective-permute-start
  7.8 0.8 copy.10.block_cols_ref
  8.6 0.7 copy.11.live_ref
  9.3 10.1 %all-gather = f32[256,512]{1,0:T(8,128)S(1)} all-gather(f32[32,512]{1,0:T(8,128)S(1)} %constant_dynamic-update-slice_fusion.rest_0_.xp_ref), channel_id=2, replica_groups=mesh['row'=8,'col'=4] {'row'}, dimensions={0}, use_global_device_ids=true | all-gather | bytes 589824 | tf_op jit(solution)/shard_map/all_gather | solution.py:285
  19.4 0.0 copy-start
  19.4 1.6 %copy-done = bf16[32,2,128,128]{3,2,1,0:T(8,128)(2,1)S(1)} copy-done((bf16[32,2,128,128]{3,2,1,0:T(8,128)(2,1)S(1)}, bf16[32,2,128,128]{3,2,1,0:T(8,128)(2,1)}, u32[]{:S(2)}) %copy-start) | copy-done | bytes 2097176
  21.0 5.3 %first.1 = (f32[8,16,640]{2,1,0:T(8,128)}, f32[8,16,512]{2,1,0:T(8,128)S(1)}, f32[16,512]{1,0:T(8,128)S(1)}, f32[16,512]{1,0:T(8,128)S(1)}, f32[16,512]{1,0:T(8,128)S(1)}, /*index=5*/f32[16,512]{1,0:T(8,128)S(1)}) custom-call(s32[32,2]{1,0:T(8,128)S(1)} %copy.10.block_cols_ref, s32[32,1]{1,0:T(8,128)S(1)} %copy.11.live_ref, f32[8,32,512]{2,1,0:T(8,128)S(1)} %bitcast.2, ...), custom_call_target="tpu_custom_call" | custom-call | tf_op jit(solution)/shard_map/first/pallas_call | solution.py:286
  26.3 0.6 copy-done.9
  26.9 0.6 copy-done.10
  27.5 0.6 copy-done.11
  28.1 3.4 %all-to-all-start = ((f32[8,16,640]{2,1,0:T(8,128)}), f32[8,16,640]{2,1,0:T(8,128)S(1)}, u32[]{:S(2)}, u32[]{:S(2)}) async-start(f32[8,16,640]{2,1,0:T(8,128)} %get-tuple-element.17), calls=%async_computation | async-start | bytes 655360 | tf_op jit(solution)/shard_map/all_to_all | solution.py:301
  31.6 1.3 %collective-permute-start.3 = (f32[16,512]{1,0:T(8,128)}, f32[16,512]{1,0:T(8,128)S(1)}, u32[]{:S(2)}, u32[]{:S(2)}) collective-permute-start(f32[16,512]{1,0:T(8,128)} %copy-done.11), channel_id=1, source_target_pairs={{0,1},{1,0},{2,3},{3,2},{4,5},{5,4},{6,7},{7,6},{8,9},{9,8},{10,11... | collective-permute-start | bytes 98312 | tf_op jit(solution)/shard_map/ppermute | solution.py:275
  32.9 2.9 %collective-permute-start.4 = (f32[16,512]{1,0:T(8,128)}, f32[16,512]{1,0:T(8,128)S(1)}, u32[]{:S(2)}, u32[]{:S(2)}) collective-permute-start(f32[16,512]{1,0:T(8,128)} %copy-done.10), channel_id=1, source_target_pairs={{0,2},{1,3},{2,0},{3,1},{4,6},{5,7},{6,4},{7,5},{8,10},{9,11},{10,... | collective-permute-start | bytes 98312 | tf_op jit(solution)/shard_map/ppermute | solution.py:275
  35.8 0.2 collective-permute-start.5
  36.0 0.6 copy-done.2
  36.7 1.8 %collective-permute-done.4.rest_2_ = f32[16,512]{1,0:T(8,128)S(1)} collective-permute-done((f32[16,512]{1,0:T(8,128)}, f32[16,512]{1,0:T(8,128)S(1)}, u32[]{:S(2)}, u32[]{:S(2)}) %collective-permute-start.4) | collective-permute-done | bytes 32800 | tf_op jit(solution)/shard_map/ppermute | solution.py:275
  38.4 0.6 copy-done.4
  39.1 2.7 %collective-permute-done.5.rest_3_ = f32[16,512]{1,0:T(8,128)S(1)} collective-permute-done((f32[16,512]{1,0:T(8,128)}, f32[16,512]{1,0:T(8,128)S(1)}, u32[]{:S(2)}, u32[]{:S(2)}) %collective-permute-start.5) | collective-permute-done | bytes 32800 | tf_op jit(solution)/shard_map/ppermute | solution.py:275
  41.7 0.6 copy-done.6
  42.4 0.8 copy-done.3
  43.1 0.8 copy-done.5
  43.9 0.8 copy-done.7
  44.7 0.4 collective-permute-start.8
  45.1 4.0 %collective-permute-start.6 = (f32[16,640]{1,0:T(8,128)S(1)}, f32[16,640]{1,0:T(8,128)S(1)}, u32[]{:S(2)}, u32[]{:S(2)}) collective-permute-start(f32[16,640]{1,0:T(8,128)S(1)} %get-tuple-element.23.rest_4_), channel_id=1, source_target_pairs={{0,1},{1,0},{2,3},{3,2},{4,5},{5,4},{6,7},{7,6},{8,9},{9,8},{10,11... | collective-permute-start | bytes 122888 | tf_op jit(solution)/shard_map/ppermute | solution.py:275
  49.1 9.6 %all-gather.1 = f32[128,512]{1,0:T(8,128)S(1)} all-gather(f32[16,512]{1,0:T(8,128)S(1)} %get-tuple-element.22), channel_id=3, replica_groups=mesh['row'=8,'col'=4] {'row'}, dimensions={0}, use_global_device_ids=true | all-gather | bytes 294912 | tf_op jit(solution)/shard_map/all_gather | solution.py:311
  58.8 8.7 %second.1 = (f32[16,512]{1,0:T(8,128)}, f32[32,16,128]{2,1,0:T(8,128)S(1)}, f32[16,256]{1,0:T(8,128)S(1)}) custom-call(s32[32,2]{1,0:T(8,128)S(1)} %copy.10.block_cols_ref, s32[32,1]{1,0:T(8,128)S(1)} %copy.11.live_ref, f32[8,32,512]{2,1,0:T(8,128)S(1)} %bitcast.3, f32[8,16,512]{2,1,0:T(8,128)S(1)} %get-tuple-element.16.fp_ref, f32[8,16,512]{2,1,0:T(8,128)S(1)} %bitcast.4, ...), custom_call_target="tpu_custom_call" | custom-call | tf_op jit(solution)/shard_map/second/pallas_call | solution.py:313
  67.5 12.3 %all_to_all.10.parts_ref = f32[32,16,128]{2,1,0:T(8,128)S(1)} all-to-all(f32[32,16,128]{2,1,0:T(8,128)S(1)} %get-tuple-element.24), channel_id=1, replica_groups=mesh['row'=8,'col'=4] {'col','row'}, dimensions={0} | all-to-all | bytes 524288 | tf_op jit(solution)/shard_map/all_to_all | solution.py:330
  79.8 0.8 copy-done.8
  80.5 7.3 %last.1 = (f32[16,512]{1,0:T(8,128)}, f32[48,48]{1,0:T(8,128)}) custom-call(f32[32,16,128]{2,1,0:T(8,128)S(1)} %all_to_all.10.parts_ref, f32[16,256]{1,0:T(8,128)S(1)} %get-tuple-element.25.aux_ref, f32[32,512]{1,0:T(8,128)S(1)} %constant_dynamic-update-slice_fusion.rest_0_.xp_ref, f32[16,512]{1,0:T(8,128)S(1)} %copy-done.8), custom_call_target="tpu_custom_call" | custom-call | tf_op jit(solution)/shard_map/last/pallas_call | solution.py:331
  (23 shorter events, 0.1 us)
Async XLA Ops:
  2.2 17.2 %collective-permute-start.2 = (f32[32,512]{1,0:T(8,128)S(1)}, f32[32,512]{1,0:T(8,128)S(1)}, u32[]{:S(2)}, u32[]{:S(2)}) collective-permute-start(f32[32,512]{1,0:T(8,128)S(1)} %constant_dynamic-update-slice_fusion.rest_0_.xp_ref), channel_id=1, source_target_pairs={{0,3},{1,2},{2,1},{3,0},{4,7},{5,6},{6,5},{7,4},{8,11},{9,10},{10,... | collective-permute-start | bytes 196616 | tf_op jit(solution)/shard_map/ppermute | solution.py:275
  7.2 12.1 %collective-permute-start.1 = (f32[32,512]{1,0:T(8,128)S(1)}, f32[32,512]{1,0:T(8,128)S(1)}, u32[]{:S(2)}, u32[]{:S(2)}) collective-permute-start(f32[32,512]{1,0:T(8,128)S(1)} %constant_dynamic-update-slice_fusion.rest_0_.xp_ref), channel_id=1, source_target_pairs={{0,2},{1,3},{2,0},{3,1},{4,6},{5,7},{6,4},{7,5},{8,10},{9,11},{10,... | collective-permute-start | bytes 196616 | tf_op jit(solution)/shard_map/ppermute | solution.py:275
  7.2 12.1 %collective-permute-start = (f32[32,512]{1,0:T(8,128)S(1)}, f32[32,512]{1,0:T(8,128)S(1)}, u32[]{:S(2)}, u32[]{:S(2)}) collective-permute-start(f32[32,512]{1,0:T(8,128)S(1)} %constant_dynamic-update-slice_fusion.rest_0_.xp_ref), channel_id=1, source_target_pairs={{0,1},{1,0},{2,3},{3,2},{4,5},{5,4},{6,7},{7,6},{8,9},{9,8},{10,11... | collective-permute-start | bytes 196616 | tf_op jit(solution)/shard_map/ppermute | solution.py:275
  19.4 1.6 %copy-start = (bf16[32,2,128,128]{3,2,1,0:T(8,128)(2,1)S(1)}, bf16[32,2,128,128]{3,2,1,0:T(8,128)(2,1)}, u32[]{:S(2)}) copy-start(bf16[32,2,128,128]{3,2,1,0:T(8,128)(2,1)} %rest_8_.1) | copy-start | bytes 6291460
  21.0 37.8 %copy-start.1 = (bf16[32,2,128,128]{3,2,1,0:T(8,128)(2,1)S(1)}, bf16[32,2,128,128]{3,2,1,0:T(8,128)(2,1)}, u32[]{:S(2)}) copy-start(bf16[32,2,128,128]{3,2,1,0:T(8,128)(2,1)} %rest_8_.1) | copy-start | bytes 6291460
  26.3 0.6 copy-start.9
  26.9 0.6 copy-start.10
  27.5 0.6 copy-start.11
  28.1 14.2 %all-to-all-start = ((f32[8,16,640]{2,1,0:T(8,128)}), f32[8,16,640]{2,1,0:T(8,128)S(1)}, u32[]{:S(2)}, u32[]{:S(2)}) async-start(f32[8,16,640]{2,1,0:T(8,128)} %get-tuple-element.17), calls=%async_computation | async-start | bytes 655360 | tf_op jit(solution)/shard_map/all_to_all | solution.py:301
  31.6 4.5 %collective-permute-start.3 = (f32[16,512]{1,0:T(8,128)}, f32[16,512]{1,0:T(8,128)S(1)}, u32[]{:S(2)}, u32[]{:S(2)}) collective-permute-start(f32[16,512]{1,0:T(8,128)} %copy-done.11), channel_id=1, source_target_pairs={{0,1},{1,0},{2,3},{3,2},{4,5},{5,4},{6,7},{7,6},{8,9},{9,8},{10,11... | collective-permute-start | bytes 98312 | tf_op jit(solution)/shard_map/ppermute | solution.py:275
  32.9 5.6 %collective-permute-start.4 = (f32[16,512]{1,0:T(8,128)}, f32[16,512]{1,0:T(8,128)S(1)}, u32[]{:S(2)}, u32[]{:S(2)}) collective-permute-start(f32[16,512]{1,0:T(8,128)} %copy-done.10), channel_id=1, source_target_pairs={{0,2},{1,3},{2,0},{3,1},{4,6},{5,7},{6,4},{7,5},{8,10},{9,11},{10,... | collective-permute-start | bytes 98312 | tf_op jit(solution)/shard_map/ppermute | solution.py:275
  35.8 5.9 %collective-permute-start.5 = (f32[16,512]{1,0:T(8,128)}, f32[16,512]{1,0:T(8,128)S(1)}, u32[]{:S(2)}, u32[]{:S(2)}) collective-permute-start(f32[16,512]{1,0:T(8,128)} %copy-done.9), channel_id=1, source_target_pairs={{0,3},{1,2},{2,1},{3,0},{4,7},{5,6},{6,5},{7,4},{8,11},{9,10},{10,... | collective-permute-start | bytes 98312 | tf_op jit(solution)/shard_map/ppermute | solution.py:275
  36.0 0.6 copy-start.2
  38.4 0.6 copy-start.4
  41.7 0.6 copy-start.6
  42.4 0.8 copy-start.3
  43.1 0.8 copy-start.5
  43.9 0.8 copy-start.7
  44.7 14.1 %collective-permute-start.8 = (f32[16,640]{1,0:T(8,128)S(1)}, f32[16,640]{1,0:T(8,128)S(1)}, u32[]{:S(2)}, u32[]{:S(2)}) collective-permute-start(f32[16,640]{1,0:T(8,128)S(1)} %get-tuple-element.23.rest_4_), channel_id=1, source_target_pairs={{0,3},{1,2},{2,1},{3,0},{4,7},{5,6},{6,5},{7,4},{8,11},{9,10},{10,... | collective-permute-start | bytes 122888 | tf_op jit(solution)/shard_map/ppermute | solution.py:275
  45.1 13.7 %collective-permute-start.7 = (f32[16,640]{1,0:T(8,128)S(1)}, f32[16,640]{1,0:T(8,128)S(1)}, u32[]{:S(2)}, u32[]{:S(2)}) collective-permute-start(f32[16,640]{1,0:T(8,128)S(1)} %get-tuple-element.23.rest_4_), channel_id=1, source_target_pairs={{0,2},{1,3},{2,0},{3,1},{4,6},{5,7},{6,4},{7,5},{8,10},{9,11},{10,... | collective-permute-start | bytes 122888 | tf_op jit(solution)/shard_map/ppermute | solution.py:275
  45.1 13.7 %collective-permute-start.6 = (f32[16,640]{1,0:T(8,128)S(1)}, f32[16,640]{1,0:T(8,128)S(1)}, u32[]{:S(2)}, u32[]{:S(2)}) collective-permute-start(f32[16,640]{1,0:T(8,128)S(1)} %get-tuple-element.23.rest_4_), channel_id=1, source_target_pairs={{0,1},{1,0},{2,3},{3,2},{4,5},{5,4},{6,7},{7,6},{8,9},{9,8},{10,11... | collective-permute-start | bytes 122888 | tf_op jit(solution)/shard_map/ppermute | solution.py:275
  79.8 0.8 copy-start.8

commit v2 on v1

v2 whole, which is shorter than its diff:
```python
import functools
import math

import jax
import jax.numpy as jnp
from jax import lax
from jax.experimental import pallas as pl
from jax.experimental.pallas import tpu as pltpu
from jax.sharding import PartitionSpec as P


highest = lax.Precision.HIGHEST
f32 = jnp.float32
bf16 = jnp.bfloat16
VMEM = pltpu.MemorySpace.VMEM
HBM = pltpu.MemorySpace.HBM
LANES = 128
VMEM_LIMIT = 16 * 1024 * 1024


def dot_nt(a, b, precision=highest):
    return lax.dot_general(
        a, b, (((1,), (1,)), ((), ())), precision=precision, preferred_element_type=f32
    )


def dot_nn(a, b, precision=highest):
    return lax.dot_general(
        a, b, (((1,), (0,)), ((), ())), precision=precision, preferred_element_type=f32
    )


def dot_tn(a, b, precision=highest):
    return lax.dot_general(
        a, b, (((0,), (0,)), ((), ())), precision=precision, preferred_element_type=f32
    )


def split(x):
    hi = x.astype(bf16)
    lo = (x - hi.astype(f32)).astype(bf16)
    return hi, lo


def split_rows(x):
    hi, lo = split(x)
    return jnp.concatenate([hi, lo], axis=0)


def eye(n):
    return (
        lax.broadcasted_iota(jnp.int32, (n, n), 0) == lax.broadcasted_iota(jnp.int32, (n, n), 1)
    ).astype(f32)


def eliminate(stack, n):
    m = stack.shape[1]
    row_at = lax.broadcasted_iota(jnp.int32, (n, m), 0)
    lane_at = lax.broadcasted_iota(jnp.int32, (n, m), 1)
    for j in range(n - 1):
        row = stack[j : j + 1, :]
        pivot = stack[j : j + 1, j : j + 1]
        column = jnp.broadcast_to(stack[:, j : j + 1], (n, m))
        scaled = row / pivot
        stack = stack - jnp.where(row_at > j, column, 0.0) * scaled
    diagonal = jnp.sum(jnp.where(row_at == lane_at, stack, 0.0), axis=1, keepdims=True)
    return stack / jnp.sqrt(diagonal)


def tree_sum(terms):
    while len(terms) > 1:
        terms = [terms[i] + terms[i + 1] for i in range(0, len(terms), 2)]
    return terms[0]


def place(block_cols_ref, b, k, me_col, per_span, row_count):
    g = block_cols_ref[k, b]
    span = lax.div(g, per_span)
    return (lax.div(span, row_count) ^ me_col) * per_span + lax.rem(g, per_span)


def pair_kernel(x_hbm, p_hbm, out_ref, sems):
    w = x_hbm.shape[0]
    copies = [
        pltpu.make_async_copy(x_hbm, out_ref.at[:w], sems.at[0]),
        pltpu.make_async_copy(p_hbm, out_ref.at[w:], sems.at[1]),
    ]
    for copy in copies:
        copy.start()
    for copy in copies:
        copy.wait()


def first_kernel(
    row_count, col_count, slots, width, bs,
    cols_hbm, live_hbm, even_ref, odd_ref, *rest,
):
    col_refs = rest[:col_count]
    blocks_hbm = rest[col_count]
    keep_ref, send_ref, fp_ref = rest[col_count + 1 : col_count + 4]
    bk_refs = rest[col_count + 4 : 2 * col_count + 4]
    picks, spread, blocks_ref, block_cols_ref, live_ref, sems, small_sems = rest[2 * col_count + 4 :]
    span_rows = even_ref.shape[2]
    per_span = span_rows // bs
    half = row_count // 2
    me_col = lax.axis_index("col")
    me_row = lax.axis_index("row")

    def fetch(s):
        at = pl.ds(pl.multiple_of((me_row ^ s) * per_span, per_span), per_span)
        return pltpu.make_async_copy(blocks_hbm.at[at], blocks_ref.at[at], sems.at[s])

    index_copies = [
        pltpu.make_async_copy(cols_hbm, block_cols_ref, small_sems.at[0]),
        pltpu.make_async_copy(live_hbm, live_ref, small_sems.at[1]),
    ]
    for copy in index_copies:
        copy.start()
    for s in range(row_count):
        fetch(s).start()
    for s in range(col_count):
        for o in range(per_span):
            picks[s * per_span + o] = split_rows(col_refs[s][:, o * bs : (o + 1) * bs])
    spread[...] = jnp.zeros_like(spread)
    for copy in index_copies:
        copy.wait()

    def span_step(s, panel):
        fetch(s).wait()
        q = me_row ^ s
        own = split_rows(panel[:width])
        parts = []
        for o in range(per_span):
            b = q * per_span + o
            tiles, chosen, weights, where = [], [], [], []
            for k in range(slots):
                w = (k < live_ref[0, b]).astype(f32)
                at = place(block_cols_ref, b, k, me_col, per_span, row_count)
                tiles.append(blocks_ref[b, k])
                chosen.append(picks[at] * w.astype(bf16))
                weights.append(w)
                where.append(at)
            tile = jnp.concatenate(tiles, axis=1)
            forward = dot_nt(jnp.concatenate(chosen, axis=1), tile, None)
            parts.append(forward[: 2 * width] + forward[2 * width :])
            back = dot_nn(own[:, o * bs : (o + 1) * bs], tile, None)
            back = back[:width] + back[width:]
            for k in range(slots):
                spread[where[k]] += back[:, k * bs : (k + 1) * bs] * weights[k]
        forward = jnp.concatenate(parts, axis=1)
        fp_ref[s] = forward[width:]
        return forward[:width], dot_nt(panel, forward)

    def two_spans(h, cross):
        keep, c0 = span_step(2 * h, even_ref[h])
        send, c1 = span_step(2 * h + 1, odd_ref[h])
        keep_ref[h, :, :span_rows] = keep
        send_ref[h, :, :span_rows] = send
        return cross + c0 + c1

    cross = lax.fori_loop(0, half, two_spans, jnp.zeros((2 * width, 2 * width), f32))
    gram = dot_nt(col_refs[0][...], col_refs[0][...])
    extra = jnp.concatenate([gram[:width], gram[width:], cross[:width], cross[width:]], axis=1)
    for h in range(half):
        keep_ref[h, :, span_rows:] = extra
        send_ref[h, :, span_rows:] = extra
    for s in range(col_count):
        for o in range(per_span):
            bk_refs[s][:, o * bs : (o + 1) * bs] = spread[s * per_span + o]


def fold_kernel(keep_ref, got_ref, *out_refs):
    for h, out_ref in enumerate(out_refs):
        out_ref[...] = keep_ref[h] + got_ref[h]


def middle_kernel(half, col_count, *refs):
    row_refs = refs[:half]
    back_refs = refs[half : half + col_count]
    out_ref, y_ref = refs[half + col_count :]
    span_rows = y_ref.shape[1]
    total = tree_sum([ref[...] for ref in row_refs])
    back = tree_sum([ref[...] for ref in back_refs])
    y = 0.5 * (total[:, :span_rows] + back)
    y_ref[...] = y
    out_ref[:, :span_rows] = y
    out_ref[:, span_rows:] = total[:, span_rows:]


def pack(matrices):
    h = matrices[0].shape[0] // 2
    return jnp.concatenate([part for m in matrices for part in (m[:h], m[h:])], axis=1)


def unpack(packed, i):
    w = 2 * packed.shape[0]
    at = 2 * i * w
    return jnp.concatenate([packed[:, at : at + w], packed[:, at + w : at + 2 * w]], axis=0)


def second_kernel(
    row_count, col_count, slots, width, bs,
    cols_hbm, live_hbm, even_ref, odd_ref, fp_ref, yeven_ref, yodd_ref, *rest,
):
    col_refs = rest[:col_count]
    y_refs = rest[col_count : 2 * col_count]
    blocks_ref = rest[2 * col_count]
    resid_ref, part_ref, aux_ref = rest[2 * col_count + 1 : 2 * col_count + 4]
    picks, block_cols_ref, live_ref, small_sems = rest[2 * col_count + 4 :]
    span_rows = even_ref.shape[2]
    per_span = span_rows // bs
    half = row_count // 2
    me_col = lax.axis_index("col")
    me_row = lax.axis_index("row")
    index_copies = [
        pltpu.make_async_copy(cols_hbm, block_cols_ref, small_sems.at[0]),
        pltpu.make_async_copy(live_hbm, live_ref, small_sems.at[1]),
    ]
    for copy in index_copies:
        copy.start()

    sums = tree_sum([y_refs[s][:, span_rows:] for s in range(col_count)])
    gram_x = sums[:, :width]
    cross_x = sums[:, 4 * width : 5 * width]
    cross_x = 0.5 * (cross_x + cross_x.T)
    done = eliminate(jnp.concatenate([gram_x, cross_x, eye(width)], axis=1), width)
    inverse_l = done[:, 2 * width : 3 * width]
    coefficient = dot_tn(inverse_l, done[:, width : 2 * width])
    minus_c_t = -coefficient.T
    x_resid = cross_x - dot_nn(gram_x, coefficient)
    aux_ref[:, : sums.shape[1]] = sums
    aux_ref[:, sums.shape[1] :] = jnp.concatenate(
        [coefficient, x_resid, jnp.zeros((width, sums.shape[1] - 2 * width), f32)], axis=1
    )
    for s in range(col_count):
        rest_s = y_refs[s][:, :span_rows] + dot_nn(minus_c_t, col_refs[s][:width, :])
        for o in range(per_span):
            picks[s * per_span + o] = split_rows(rest_s[:, o * bs : (o + 1) * bs])
    mine = y_refs[0][:, :span_rows] + dot_nn(minus_c_t, col_refs[0][:width, :])
    resid_ref[...] = mine
    for copy in index_copies:
        copy.wait()

    def span_step(s, panel, image):
        q = me_row ^ s
        rest_q = image + dot_nn(minus_c_t, panel[:width])
        parts = []
        for o in range(per_span):
            b = q * per_span + o
            tiles, chosen = [], []
            for k in range(slots):
                w = (k < live_ref[0, b]).astype(f32)
                at = place(block_cols_ref, b, k, me_col, per_span, row_count)
                tiles.append(blocks_ref[b, k])
                chosen.append(picks[at] * w.astype(bf16))
            forward = dot_nt(
                jnp.concatenate(chosen, axis=1), jnp.concatenate(tiles, axis=1), None
            )
            parts.append(forward[:width] + forward[width:])
        forward = jnp.concatenate(parts, axis=1)
        own = dot_nt(forward, rest_q)
        cross = dot_nt(forward, panel[width:]) + dot_nt(rest_q, fp_ref[s])
        return own, cross

    def two_spans(h, carry):
        own, cross = carry
        own0, cross0 = span_step(2 * h, even_ref[h], yeven_ref[h])
        own1, cross1 = span_step(2 * h + 1, odd_ref[h], yodd_ref[h])
        return own + own0 + own1, cross + cross0 + cross1

    zero = jnp.zeros((width, width), f32)
    own, cross = lax.fori_loop(0, half, two_spans, (zero, zero))
    local = jnp.concatenate([mine, col_refs[0][width:, :]], axis=0)
    gram = dot_nt(mine, local)
    part = pack([gram[:, :width], gram[:, width:], own, 0.5 * cross])
    for d in range(part_ref.shape[0]):
        part_ref[d] = part


def last_kernel(
    width, scale, parts_ref, aux_ref, xp_ref, resid_hbm, x_next_ref, reduced_ref, resid_ref, sem
):
    w = width
    fetch = pltpu.make_async_copy(resid_hbm, resid_ref, sem)
    fetch.start()
    total = parts_ref[0]
    for d in range(1, parts_ref.shape[0]):
        total = total + parts_ref[d]
    piece = lambda i: aux_ref[:, i * w : (i + 1) * w]
    per = LANES // w
    xx, xp, pp = piece(0), piece(1), piece(3)
    xbx, xbp, pbx, pbp = (piece(i) for i in range(4, 8))
    coefficient, xr = piece(per), piece(per + 1)
    rr, rp, rbr, rap = (unpack(total, i) for i in range(4))
    gram_basis = jnp.concatenate(
        [
            jnp.concatenate([xx, xr, xp], axis=1),
            jnp.concatenate([xr.T, rr, rp], axis=1),
            jnp.concatenate([xp.T, rp.T, pp], axis=1),
        ],
        axis=0,
    )
    xax = 0.5 * (xbx + xbx.T)
    xap = 0.5 * (xbp + pbx.T)
    xar = rr + dot_tn(coefficient, xr)
    gram_apply = jnp.concatenate(
        [
            jnp.concatenate([xax, xar, xap], axis=1),
            jnp.concatenate([xar.T, 0.5 * (rbr + rbr.T), rap], axis=1),
            jnp.concatenate([xap.T, rap.T, 0.5 * (pbp + pbp.T)], axis=1),
        ],
        axis=0,
    )
    n = 3 * w
    inverse_l = eliminate(jnp.concatenate([gram_basis, eye(n)], axis=1), n)[:, n:]
    reduced = dot_nt(dot_nn(inverse_l, gram_apply), inverse_l)
    reduced_ref[...] = reduced
    shifted = reduced + 3.0 * eye(n)
    target = dot_nn(shifted, shifted[:, :w])
    gram_fresh = dot_tn(target, target)
    mixing = dot_tn(target, inverse_l)
    weights = scale * eliminate(jnp.concatenate([gram_fresh, mixing], axis=1), w)[:, w:]
    fetch.wait()
    basis = jnp.concatenate([xp_ref[:w, :], resid_ref[...], xp_ref[w:, :]], axis=0)
    x_next_ref[...] = dot_nn(weights, basis)


def vmem_specs(n):
    return [pl.BlockSpec(memory_space=VMEM)] * n


def hbm_specs(n):
    return [pl.BlockSpec(memory_space=HBM)] * n


def per_device(block_vecs, direction, blocks, block_cols, live_counts):
    row_count = lax.axis_size("row")
    col_count = lax.axis_size("col")
    width, span_rows = block_vecs.shape
    _, slots, bs = blocks.shape[:3]
    per_span = span_rows // bs
    half = row_count // 2
    order_total = span_rows * row_count * col_count
    col_blocks = col_count * per_span
    sizes = (row_count, col_count, slots, width, bs)
    shape = lambda *dims: jax.ShapeDtypeStruct(dims, f32)
    params = pltpu.CompilerParams(vmem_limit_bytes=VMEM_LIMIT)

    in_hbm = lambda array: pltpu.with_memory_space_constraint(array, HBM)
    blocks_hbm, block_cols, live_counts = map(in_hbm, (blocks, block_cols.T, live_counts.T))

    def swap(array, axis, s):
        return lax.ppermute(array, axis, [(i, i ^ s) for i in range(lax.axis_size(axis))])

    far = list(reversed(range(1, col_count)))
    across = list(reversed(range(2, row_count, 2)))

    def gather(array, array_col):
        rows = {s: swap(array, "row", s) for s in across}
        cols = {s: swap(array_col, "col", s) for s in far}
        even = jnp.stack([array] + [rows[s] for s in range(2, row_count, 2)])
        odd = swap(even, "row", 1)
        return even, odd, [array_col] + [cols[s] for s in range(1, col_count)]

    index_scratch = [
        pltpu.SMEM(block_cols.shape, jnp.int32),
        pltpu.SMEM(live_counts.shape, jnp.int32),
    ]
    pair = pl.pallas_call(
        pair_kernel,
        in_specs=hbm_specs(2),
        scratch_shapes=[pltpu.SemaphoreType.DMA((2,))],
        out_specs=vmem_specs(1)[0],
        out_shape=shape(2 * width, span_rows),
        compiler_params=params,
        name="pair",
    )(in_hbm(block_vecs), in_hbm(direction))
    pair_even, pair_odd, pair_cols = gather(pair, pair)
    first = pl.pallas_call(
        functools.partial(first_kernel, *sizes),
        in_specs=hbm_specs(2) + vmem_specs(col_count + 2) + hbm_specs(1),
        out_specs=vmem_specs(col_count + 3),
        out_shape=[shape(half, width, span_rows + LANES)] * 2
        + [shape(row_count, width, span_rows)]
        + [shape(width, span_rows)] * col_count,
        scratch_shapes=[
            pltpu.VMEM((col_blocks, 4 * width, bs), bf16),
            pltpu.VMEM((col_blocks, width, bs), f32),
            pltpu.VMEM(blocks.shape, bf16),
        ]
        + index_scratch
        + [pltpu.SemaphoreType.DMA((row_count,)), pltpu.SemaphoreType.DMA((2,))],
        compiler_params=params,
        name="first",
    )(block_cols, live_counts, pair_even, pair_odd, *pair_cols, blocks_hbm)
    keep, send, forward_p, backs = first[0], first[1], first[2], first[3:]
    got_pair = swap(send, "row", 1)
    got_backs = {s: swap(backs[s], "col", s) for s in far}
    folded = pl.pallas_call(
        fold_kernel,
        in_specs=vmem_specs(2),
        out_specs=vmem_specs(half),
        out_shape=[shape(width, span_rows + LANES)] * half,
        compiler_params=params,
        name="fold",
    )(keep, got_pair)
    got_rows = {s: swap(folded[s // 2], "row", s) for s in across}
    message, image = pl.pallas_call(
        functools.partial(middle_kernel, half, col_count),
        in_specs=vmem_specs(half + col_count),
        out_specs=vmem_specs(2),
        out_shape=[shape(width, span_rows + LANES), shape(width, span_rows)],
        compiler_params=params,
        name="middle",
    )(
        folded[0],
        *[got_rows[s] for s in range(2, row_count, 2)],
        backs[0],
        *[got_backs[s] for s in range(1, col_count)],
    )
    image_even, image_odd, image_cols = gather(image, message)
    device_count = row_count * col_count
    resid, part, aux = pl.pallas_call(
        functools.partial(second_kernel, *sizes),
        in_specs=hbm_specs(2) + vmem_specs(2 * col_count + 6),
        out_specs=vmem_specs(3),
        out_shape=[
            shape(width, span_rows),
            shape(device_count, width // 2, LANES),
            shape(width, 2 * LANES),
        ],
        scratch_shapes=[pltpu.VMEM((col_blocks, 2 * width, bs), bf16)]
        + index_scratch
        + [pltpu.SemaphoreType.DMA((2,))],
        compiler_params=params,
        name="second",
    )(
        block_cols, live_counts, pair_even, pair_odd, forward_p, image_even, image_odd,
        *pair_cols, *image_cols, blocks,
    )
    parts = lax.all_to_all(part, ("col", "row"), 0, 0)
    x_next, reduced = pl.pallas_call(
        functools.partial(last_kernel, width, math.sqrt(order_total)),
        in_specs=vmem_specs(3) + hbm_specs(1),
        out_specs=vmem_specs(2),
        out_shape=[shape(width, span_rows), shape(3 * width, 3 * width)],
        scratch_shapes=[pltpu.VMEM((width, span_rows), f32), pltpu.SemaphoreType.DMA(())],
        compiler_params=params,
        name="last",
    )(parts, aux, pair, in_hbm(resid))
    return (x_next, reduced, resid)


def solution(mesh):
    return jax.shard_map(
        per_device,
        mesh=mesh,
        in_specs=(
            P(None, ("col", "row")),
            P(None, ("col", "row")),
            P("col", "row", None, None),
            P("col", "row"),
            P("col", "row"),
        ),
        out_specs=(P(None, ("col", "row")), P(), P(None, ("col", "row"))),
        check_vma=False,
    )
```

time: 88.6 us -> 76.7 us (0.87)
  blocking collectives: 32 us -> 12.1 us
  waiting for transfers between devices: 4.49 us -> 18.8 us
  local copies, waits for them, and re-layouts: 11.3 us -> 0.01 us
  starting transfers between devices: 18 us -> 25.7 us
  Pallas kernels: 21.4 us -> 19 us
    all_gather x2 -> x0, blocking collectives: 19.7 us -> none  [the longest x1 10.1 us: per_device(): pair_rows = lax.all_gather(pair, 'row')]
    ppermute x9 -> x21, waiting for transfers between devices: 4.49 us -> 18.8 us  [swap(): lax.ppermute(array, axis, [(i, i ^ s) for i in range(lax.axis_size(axis))])]
    ppermute x9 -> x21, starting transfers between devices: 14.5 us -> 25.7 us  [swap(): lax.ppermute(array, axis, [(i, i ^ s) for i in range(lax.axis_size(axis))])]
    unnamed x27 -> x2, local copies, waits for them, and re-layouts: 10.5 us -> 0.01 us
    all_to_all x1 -> x0, starting transfers between devices: 3.43 us -> none  [per_device(): got = lax.all_to_all(forward, 'row', 0, 0)]
    pallas_call x3 -> x5, Pallas kernels: 14.1 us -> 11.7 us  [the longest x1 6.32 us: per_device(): pl.pallas_call(functools.partial(second_kernel, *sizes), in_specs=hbm_spe...]
  transfers between devices with their start and end apart: 10 -> 21, of which waited for: 2 -> 13; matrix products, arithmetic and copies ran while one was open for 2% -> 0% of each run, Pallas kernels for 0% -> 0%
where the time goes in v2:
time: 76.7 us; the launch traced here: 76.5 us
  starting transfers between devices  25.7 us (34%)
  Pallas kernels  19 us (25%)
  waiting for transfers between devices  18.8 us (25%)
  blocking collectives  12.1 us (16%)
    ppermute x21, starting transfers between devices, swap(): lax.ppermute(array, axis, [(i, i ^ s) for i in range(lax.axis_size(axis))])  25.7 us
    ppermute x21, waiting for transfers between devices, swap(): lax.ppermute(array, axis, [(i, i ^ s) for i in range(lax.axis_size(axis))])  18.8 us
    all_to_all x1, blocking collectives, per_device(): parts = lax.all_to_all(part, ('col', 'row'), 0, 0)  12.1 us
    pallas_call x1, Pallas kernels, per_device(): pl.pallas_call(functools.partial(last_kernel, width, math.sqrt(order_tota...  7.3 us
    pallas_call x1, Pallas kernels, per_device(): pl.pallas_call(functools.partial(second_kernel, *sizes), in_specs=hbm_spe...  6.32 us
    pallas_call x1, Pallas kernels, per_device(): pl.pallas_call(functools.partial(first_kernel, *sizes), in_specs=hbm_spec...  4.56 us
  transfers between devices with their start and end apart: 21, of which 13 were waited for; matrix products, arithmetic and copies ran while one was open for 0% of the time, Pallas kernels for 0%

profile of v2, /device:TPU:0, one launch (start us, length us, event | category | flops | bytes accessed | tf_op | source)
XLA Modules:
  0.0 76.5 jit_solution(15841114599239418762)
XLA Ops:
  0.6 0.8 %pair.1.rest_0_.xp_ref = f32[32,512]{1,0:T(8,128)S(1)} custom-call(f32[16,512]{1,0:T(8,128)} %x_hbm.1, f32[16,512]{1,0:T(8,128)} %p_hbm.1), custom_call_target="tpu_custom_call" | custom-call | tf_op jit(solution)/shard_map/pair/pallas_call | solution.py:369
  1.4 4.0 %collective-permute-start.2 = (f32[32,512]{1,0:T(8,128)S(1)}, f32[32,512]{1,0:T(8,128)S(1)}, u32[]{:S(2)}, u32[]{:S(2)}) collective-permute-start(f32[32,512]{1,0:T(8,128)S(1)} %pair.1.rest_0_.xp_ref), channel_id=1, source_target_pairs={{0,24},{4,28},{8,16},{12,20},{16,8},{20,12},{24,0},{28,4},{1,25},{... | collective-permute-start | bytes 196616 | tf_op jit(solution)/shard_map/ppermute | solution.py:353
  5.4 0.5 collective-permute-start.1
  6.1 1.6 %collective-permute-done.2 = f32[32,512]{1,0:T(8,128)S(1)} collective-permute-done((f32[32,512]{1,0:T(8,128)S(1)}, f32[32,512]{1,0:T(8,128)S(1)}, u32[]{:S(2)}, u32[]{:S(2)}) %collective-permute-start.2) | collective-permute-done | bytes 65568 | tf_op jit(solution)/shard_map/ppermute | solution.py:353
  7.7 2.0 %collective-permute-done.1 = f32[32,512]{1,0:T(8,128)S(1)} collective-permute-done((f32[32,512]{1,0:T(8,128)S(1)}, f32[32,512]{1,0:T(8,128)S(1)}, u32[]{:S(2)}, u32[]{:S(2)}) %collective-permute-start.1) | collective-permute-done | bytes 65568 | tf_op jit(solution)/shard_map/ppermute | solution.py:353
  9.7 0.5 collective-permute-done
  10.3 3.7 %collective-permute-start.6 = (f32[32,512]{1,0:T(8,128)S(1)}, f32[32,512]{1,0:T(8,128)S(1)}, u32[]{:S(2)}, u32[]{:S(2)}) collective-permute-start(f32[32,512]{1,0:T(8,128)S(1)} %pair.1.rest_0_.xp_ref), channel_id=1, source_target_pairs={{0,3},{1,2},{2,1},{3,0},{4,7},{5,6},{6,5},{7,4},{8,11},{9,10},{10,... | collective-permute-start | bytes 196616 | tf_op jit(solution)/shard_map/ppermute | solution.py:353
  14.0 0.8 %collective-permute-start.4 = (f32[32,512]{1,0:T(8,128)S(1)}, f32[32,512]{1,0:T(8,128)S(1)}, u32[]{:S(2)}, u32[]{:S(2)}) collective-permute-start(f32[32,512]{1,0:T(8,128)S(1)} %pair.1.rest_0_.xp_ref), channel_id=1, source_target_pairs={{0,1},{1,0},{2,3},{3,2},{4,5},{5,4},{6,7},{7,6},{8,9},{9,8},{10,11... | collective-permute-start | bytes 196616 | tf_op jit(solution)/shard_map/ppermute | solution.py:353
  14.7 2.1 %collective-permute-done.6.rest_3_ = f32[32,512]{1,0:T(8,128)S(1)} collective-permute-done((f32[32,512]{1,0:T(8,128)S(1)}, f32[32,512]{1,0:T(8,128)S(1)}, u32[]{:S(2)}, u32[]{:S(2)}) %collective-permute-start.6) | collective-permute-done | bytes 65568 | tf_op jit(solution)/shard_map/ppermute | solution.py:353
  16.9 3.2 %collective-permute-done.5.rest_2_ = f32[32,512]{1,0:T(8,128)S(1)} collective-permute-done((f32[32,512]{1,0:T(8,128)S(1)}, f32[32,512]{1,0:T(8,128)S(1)}, u32[]{:S(2)}, u32[]{:S(2)}) %collective-permute-start.5) | collective-permute-done | bytes 65568 | tf_op jit(solution)/shard_map/ppermute | solution.py:353
  20.0 4.6 %first.1 = (f32[4,16,640]{2,1,0:T(8,128)S(1)}, f32[4,16,640]{2,1,0:T(8,128)S(1)}, f32[8,16,512]{2,1,0:T(8,128)S(1)}, f32[16,512]{1,0:T(8,128)S(1)}, f32[16,512]{...) custom-call(s32[2,32]{1,0:T(2,128)} %bitcast.18, s32[1,32]{1,0:T(1,128)} %bitcast.20, ...), custom_call_target="tpu_custom_call" | custom-call | tf_op jit(solution)/shard_map/first/pallas_call | solution.py:379
  24.7 1.3 %collective-permute-start.11 = (f32[16,512]{1,0:T(8,128)S(1)}, f32[16,512]{1,0:T(8,128)S(1)}, u32[]{:S(2)}, u32[]{:S(2)}) collective-permute-start(f32[16,512]{1,0:T(8,128)S(1)} %get-tuple-element.29), channel_id=1, source_target_pairs={{0,1},{1,0},{2,3},{3,2},{4,5},{5,4},{6,7},{7,6},{8,9},{9,8},{10,11... | collective-permute-start | bytes 98312 | tf_op jit(solution)/shard_map/ppermute | solution.py:353
  26.1 0.6 collective-permute-start.8
  26.7 1.5 %collective-permute-start.9 = (f32[16,640]{1,0:T(8,128)S(1)}, f32[16,640]{1,0:T(8,128)S(1)}, u32[]{:S(2)}, u32[]{:S(2)}) collective-permute-start(f32[16,640]{1,0:T(8,128)S(1)} %get-tuple-element.26), channel_id=1, source_target_pairs={{0,16},{4,20},{8,24},{12,28},{16,0},{20,4},{24,8},{28,12},{1,17},{... | collective-permute-start | bytes 122888 | tf_op jit(solution)/shard_map/ppermute | solution.py:353
  28.2 1.4 %collective-permute-start.10 = (f32[16,640]{1,0:T(8,128)S(1)}, f32[16,640]{1,0:T(8,128)S(1)}, u32[]{:S(2)}, u32[]{:S(2)}) collective-permute-start(f32[16,640]{1,0:T(8,128)S(1)} %get-tuple-element.27), channel_id=1, source_target_pairs={{0,24},{4,28},{8,16},{12,20},{16,8},{20,12},{24,0},{28,4},{1,25},{... | collective-permute-start | bytes 122888 | tf_op jit(solution)/shard_map/ppermute | solution.py:353
  29.6 1.7 %collective-permute-start.12 = (f32[16,512]{1,0:T(8,128)S(1)}, f32[16,512]{1,0:T(8,128)S(1)}, u32[]{:S(2)}, u32[]{:S(2)}) collective-permute-start(f32[16,512]{1,0:T(8,128)S(1)} %get-tuple-element.30), channel_id=1, source_target_pairs={{0,2},{1,3},{2,0},{3,1},{4,6},{5,7},{6,4},{7,5},{8,10},{9,11},{10,... | collective-permute-start | bytes 98312 | tf_op jit(solution)/shard_map/ppermute | solution.py:353
  31.4 1.9 %collective-permute-start.13 = (f32[16,512]{1,0:T(8,128)S(1)}, f32[16,512]{1,0:T(8,128)S(1)}, u32[]{:S(2)}, u32[]{:S(2)}) collective-permute-start(f32[16,512]{1,0:T(8,128)S(1)} %get-tuple-element.31), channel_id=1, source_target_pairs={{0,3},{1,2},{2,1},{3,0},{4,7},{5,6},{6,5},{7,4},{8,11},{9,10},{10,... | collective-permute-start | bytes 98312 | tf_op jit(solution)/shard_map/ppermute | solution.py:353
  33.2 1.2 %collective-permute-done.12.refs_6_ = f32[16,512]{1,0:T(8,128)S(1)} collective-permute-done((f32[16,512]{1,0:T(8,128)S(1)}, f32[16,512]{1,0:T(8,128)S(1)}, u32[]{:S(2)}, u32[]{:S(2)}) %collective-permute-start.12) | collective-permute-done | bytes 32800 | tf_op jit(solution)/shard_map/ppermute | solution.py:353
  34.4 2.6 %collective-permute-done.13.refs_7_ = f32[16,512]{1,0:T(8,128)S(1)} collective-permute-done((f32[16,512]{1,0:T(8,128)S(1)}, f32[16,512]{1,0:T(8,128)S(1)}, u32[]{:S(2)}, u32[]{:S(2)}) %collective-permute-start.13) | collective-permute-done | bytes 32800 | tf_op jit(solution)/shard_map/ppermute | solution.py:353
  37.1 1.6 %collective-permute-start.16 = (f32[16,512]{1,0:T(8,128)S(1)}, f32[16,512]{1,0:T(8,128)S(1)}, u32[]{:S(2)}, u32[]{:S(2)}) collective-permute-start(f32[16,512]{1,0:T(8,128)S(1)} %get-tuple-element.32), channel_id=1, source_target_pairs={{0,24},{4,28},{8,16},{12,20},{16,8},{20,12},{24,0},{28,4},{1,25},{... | collective-permute-start | bytes 98312 | tf_op jit(solution)/shard_map/ppermute | solution.py:353
  38.7 0.5 collective-permute-start.15
  39.2 1.5 %collective-permute-start.14 = (f32[16,512]{1,0:T(8,128)S(1)}, f32[16,512]{1,0:T(8,128)S(1)}, u32[]{:S(2)}, u32[]{:S(2)}) collective-permute-start(f32[16,512]{1,0:T(8,128)S(1)} %get-tuple-element.32), channel_id=1, source_target_pairs={{0,8},{4,12},{8,0},{12,4},{16,24},{20,28},{24,16},{28,20},{1,9},{5... | collective-permute-start | bytes 98312 | tf_op jit(solution)/shard_map/ppermute | solution.py:353
  40.7 1.3 %collective-permute-done.16 = f32[16,512]{1,0:T(8,128)S(1)} collective-permute-done((f32[16,512]{1,0:T(8,128)S(1)}, f32[16,512]{1,0:T(8,128)S(1)}, u32[]{:S(2)}, u32[]{:S(2)}) %collective-permute-start.16) | collective-permute-done | bytes 32800 | tf_op jit(solution)/shard_map/ppermute | solution.py:353
  42.0 0.6 collective-permute-done.15
  42.6 0.5 collective-permute-done.14
  43.2 1.9 %collective-permute-start.20 = (f32[16,640]{1,0:T(8,128)S(1)}, f32[16,640]{1,0:T(8,128)S(1)}, u32[]{:S(2)}, u32[]{:S(2)}) collective-permute-start(f32[16,640]{1,0:T(8,128)S(1)} %get-tuple-element.33.rest_4_), channel_id=1, source_target_pairs={{0,3},{1,2},{2,1},{3,0},{4,7},{5,6},{6,5},{7,4},{8,11},{9,10},{10,... | collective-permute-start | bytes 122888 | tf_op jit(solution)/shard_map/ppermute | solution.py:353
  45.1 2.5 %collective-permute-start.18 = (f32[16,640]{1,0:T(8,128)S(1)}, f32[16,640]{1,0:T(8,128)S(1)}, u32[]{:S(2)}, u32[]{:S(2)}) collective-permute-start(f32[16,640]{1,0:T(8,128)S(1)} %get-tuple-element.33.rest_4_), channel_id=1, source_target_pairs={{0,1},{1,0},{2,3},{3,2},{4,5},{5,4},{6,7},{7,6},{8,9},{9,8},{10,11... | collective-permute-start | bytes 122888 | tf_op jit(solution)/shard_map/ppermute | solution.py:353
  47.6 1.8 %collective-permute-done.20.rest_7_ = f32[16,640]{1,0:T(8,128)S(1)} collective-permute-done((f32[16,640]{1,0:T(8,128)S(1)}, f32[16,640]{1,0:T(8,128)S(1)}, u32[]{:S(2)}, u32[]{:S(2)}) %collective-permute-start.20) | collective-permute-done | bytes 40992 | tf_op jit(solution)/shard_map/ppermute | solution.py:353
  49.5 1.3 %collective-permute-done.19.rest_6_ = f32[16,640]{1,0:T(8,128)S(1)} collective-permute-done((f32[16,640]{1,0:T(8,128)S(1)}, f32[16,640]{1,0:T(8,128)S(1)}, u32[]{:S(2)}, u32[]{:S(2)}) %collective-permute-start.19) | collective-permute-done | bytes 40992 | tf_op jit(solution)/shard_map/ppermute | solution.py:353
  50.7 6.3 %second.1 = (f32[16,512]{1,0:T(8,128)}, f32[32,8,128]{2,1,0:T(8,128)S(1)}, f32[16,256]{1,0:T(8,128)S(1)}) custom-call(s32[2,32]{1,0:T(2,128)} %bitcast.19, s32[1,32]{1,0:T(1,128)} %bitcast.21, f32[4,32,512]{2,1,0:T(8,128)S(1)} %pad_maximum_fusion.even_ref, f32[4,32,512]{2,1,0:T(8,128)S(1)} %collective-permute-done.3.odd_ref, ...), custom_call_target="tpu_custom_call" | custom-call | tf_op jit(solution)/shard_map/second/pallas_call | solution.py:423
  57.0 12.1 %all_to_all.5.parts_ref = f32[32,8,128]{2,1,0:T(8,128)S(1)} all-to-all(f32[32,8,128]{2,1,0:T(8,128)S(1)} %get-tuple-element.34), channel_id=1, replica_groups=mesh['row'=8,'col'=4] {'col','row'}, dimensions={0} | all-to-all | bytes 262144 | tf_op jit(solution)/shard_map/all_to_all | solution.py:441
  69.2 7.3 %last.1 = (f32[16,512]{1,0:T(8,128)}, f32[48,48]{1,0:T(8,128)}) custom-call(f32[32,8,128]{2,1,0:T(8,128)S(1)} %all_to_all.5.parts_ref, f32[16,256]{1,0:T(8,128)S(1)} %get-tuple-element.35.aux_ref, f32[32,512]{1,0:T(8,128)S(1)} %pair.1.rest_0_.xp_ref, f32[16,512]{1,0:T(8,128)} %get-tuple-element.20.resid_hbm), custom_call_target="tpu_custom_call" | custom-call | tf_op jit(solution)/shard_map/last/pallas_call | solution.py:442
  (21 shorter events, 0.5 us)
Async XLA Ops:
  1.4 6.2 %collective-permute-start.2 = (f32[32,512]{1,0:T(8,128)S(1)}, f32[32,512]{1,0:T(8,128)S(1)}, u32[]{:S(2)}, u32[]{:S(2)}) collective-permute-start(f32[32,512]{1,0:T(8,128)S(1)} %pair.1.rest_0_.xp_ref), channel_id=1, source_target_pairs={{0,24},{4,28},{8,16},{12,20},{16,8},{20,12},{24,0},{28,4},{1,25},{... | collective-permute-start | bytes 196616 | tf_op jit(solution)/shard_map/ppermute | solution.py:353
  5.4 4.3 %collective-permute-start.1 = (f32[32,512]{1,0:T(8,128)S(1)}, f32[32,512]{1,0:T(8,128)S(1)}, u32[]{:S(2)}, u32[]{:S(2)}) collective-permute-start(f32[32,512]{1,0:T(8,128)S(1)} %pair.1.rest_0_.xp_ref), channel_id=1, source_target_pairs={{0,16},{4,20},{8,24},{12,28},{16,0},{20,4},{24,8},{28,12},{1,17},{... | collective-permute-start | bytes 196616 | tf_op jit(solution)/shard_map/ppermute | solution.py:353
  5.9 4.3 %collective-permute-start = (f32[32,512]{1,0:T(8,128)S(1)}, f32[32,512]{1,0:T(8,128)S(1)}, u32[]{:S(2)}, u32[]{:S(2)}) collective-permute-start(f32[32,512]{1,0:T(8,128)S(1)} %pair.1.rest_0_.xp_ref), channel_id=1, source_target_pairs={{0,8},{4,12},{8,0},{12,4},{16,24},{20,28},{24,16},{28,20},{1,9},{5... | collective-permute-start | bytes 196616 | tf_op jit(solution)/shard_map/ppermute | solution.py:353
  10.2 40.5 %copy-start = (bf16[32,2,128,128]{3,2,1,0:T(8,128)(2,1)S(1)}, bf16[32,2,128,128]{3,2,1,0:T(8,128)(2,1)}, u32[]{:S(2)}) copy-start(bf16[32,2,128,128]{3,2,1,0:T(8,128)(2,1)} %rest_8_.1) | copy-start | bytes 6291460
  10.2 9.8 %collective-permute-start.3 = (f32[4,32,512]{2,1,0:T(8,128)S(1)}, f32[4,32,512]{2,1,0:T(8,128)S(1)}, u32[]{:S(2)}, u32[]{:S(2)}) collective-permute-start(f32[4,32,512]{2,1,0:T(8,128)S(1)} %pad_maximum_fusion.even_ref), channel_id=1, source_target_pairs={{0,4},{4,0},{8,12},{12,8},{16,20},{20,16},{24,28},{28,24},{1,5},{5... | collective-permute-start | bytes 786440 | tf_op jit(solution)/shard_map/ppermute | solution.py:353
  10.3 6.6 %collective-permute-start.6 = (f32[32,512]{1,0:T(8,128)S(1)}, f32[32,512]{1,0:T(8,128)S(1)}, u32[]{:S(2)}, u32[]{:S(2)}) collective-permute-start(f32[32,512]{1,0:T(8,128)S(1)} %pair.1.rest_0_.xp_ref), channel_id=1, source_target_pairs={{0,3},{1,2},{2,1},{3,0},{4,7},{5,6},{6,5},{7,4},{8,11},{9,10},{10,... | collective-permute-start | bytes 196616 | tf_op jit(solution)/shard_map/ppermute | solution.py:353
  14.0 6.1 %collective-permute-start.5 = (f32[32,512]{1,0:T(8,128)S(1)}, f32[32,512]{1,0:T(8,128)S(1)}, u32[]{:S(2)}, u32[]{:S(2)}) collective-permute-start(f32[32,512]{1,0:T(8,128)S(1)} %pair.1.rest_0_.xp_ref), channel_id=1, source_target_pairs={{0,2},{1,3},{2,0},{3,1},{4,6},{5,7},{6,4},{7,5},{8,10},{9,11},{10,... | collective-permute-start | bytes 196616 | tf_op jit(solution)/shard_map/ppermute | solution.py:353
  14.0 6.1 %collective-permute-start.4 = (f32[32,512]{1,0:T(8,128)S(1)}, f32[32,512]{1,0:T(8,128)S(1)}, u32[]{:S(2)}, u32[]{:S(2)}) collective-permute-start(f32[32,512]{1,0:T(8,128)S(1)} %pair.1.rest_0_.xp_ref), channel_id=1, source_target_pairs={{0,1},{1,0},{2,3},{3,2},{4,5},{5,4},{6,7},{7,6},{8,9},{9,8},{10,11... | collective-permute-start | bytes 196616 | tf_op jit(solution)/shard_map/ppermute | solution.py:353
  24.6 1.5 %collective-permute-start.7 = (f32[4,16,640]{2,1,0:T(8,128)S(1)}, f32[4,16,640]{2,1,0:T(8,128)S(1)}, u32[]{:S(2)}, u32[]{:S(2)}) collective-permute-start(f32[4,16,640]{2,1,0:T(8,128)S(1)} %get-tuple-element.23), channel_id=1, source_target_pairs={{0,4},{4,0},{8,12},{12,8},{16,20},{20,16},{24,28},{28,24},{1,5},{5... | collective-permute-start | bytes 491528 | tf_op jit(solution)/shard_map/ppermute | solution.py:353
  24.7 6.7 %collective-permute-start.11 = (f32[16,512]{1,0:T(8,128)S(1)}, f32[16,512]{1,0:T(8,128)S(1)}, u32[]{:S(2)}, u32[]{:S(2)}) collective-permute-start(f32[16,512]{1,0:T(8,128)S(1)} %get-tuple-element.29), channel_id=1, source_target_pairs={{0,1},{1,0},{2,3},{3,2},{4,5},{5,4},{6,7},{7,6},{8,9},{9,8},{10,11... | collective-permute-start | bytes 98312 | tf_op jit(solution)/shard_map/ppermute | solution.py:353
  26.1 11.0 %collective-permute-start.8 = (f32[16,640]{1,0:T(8,128)S(1)}, f32[16,640]{1,0:T(8,128)S(1)}, u32[]{:S(2)}, u32[]{:S(2)}) collective-permute-start(f32[16,640]{1,0:T(8,128)S(1)} %get-tuple-element.25), channel_id=1, source_target_pairs={{0,8},{4,12},{8,0},{12,4},{16,24},{20,28},{24,16},{28,20},{1,9},{5... | collective-permute-start | bytes 122888 | tf_op jit(solution)/shard_map/ppermute | solution.py:353
  26.7 10.4 %collective-permute-start.9 = (f32[16,640]{1,0:T(8,128)S(1)}, f32[16,640]{1,0:T(8,128)S(1)}, u32[]{:S(2)}, u32[]{:S(2)}) collective-permute-start(f32[16,640]{1,0:T(8,128)S(1)} %get-tuple-element.26), channel_id=1, source_target_pairs={{0,16},{4,20},{8,24},{12,28},{16,0},{20,4},{24,8},{28,12},{1,17},{... | collective-permute-start | bytes 122888 | tf_op jit(solution)/shard_map/ppermute | solution.py:353
  28.2 8.9 %collective-permute-start.10 = (f32[16,640]{1,0:T(8,128)S(1)}, f32[16,640]{1,0:T(8,128)S(1)}, u32[]{:S(2)}, u32[]{:S(2)}) collective-permute-start(f32[16,640]{1,0:T(8,128)S(1)} %get-tuple-element.27), channel_id=1, source_target_pairs={{0,24},{4,28},{8,16},{12,20},{16,8},{20,12},{24,0},{28,4},{1,25},{... | collective-permute-start | bytes 122888 | tf_op jit(solution)/shard_map/ppermute | solution.py:353
  29.6 4.8 %collective-permute-start.12 = (f32[16,512]{1,0:T(8,128)S(1)}, f32[16,512]{1,0:T(8,128)S(1)}, u32[]{:S(2)}, u32[]{:S(2)}) collective-permute-start(f32[16,512]{1,0:T(8,128)S(1)} %get-tuple-element.30), channel_id=1, source_target_pairs={{0,2},{1,3},{2,0},{3,1},{4,6},{5,7},{6,4},{7,5},{8,10},{9,11},{10,... | collective-permute-start | bytes 98312 | tf_op jit(solution)/shard_map/ppermute | solution.py:353
  31.4 5.7 %collective-permute-start.13 = (f32[16,512]{1,0:T(8,128)S(1)}, f32[16,512]{1,0:T(8,128)S(1)}, u32[]{:S(2)}, u32[]{:S(2)}) collective-permute-start(f32[16,512]{1,0:T(8,128)S(1)} %get-tuple-element.31), channel_id=1, source_target_pairs={{0,3},{1,2},{2,1},{3,0},{4,7},{5,6},{6,5},{7,4},{8,11},{9,10},{10,... | collective-permute-start | bytes 98312 | tf_op jit(solution)/shard_map/ppermute | solution.py:353
  37.1 4.9 %collective-permute-start.16 = (f32[16,512]{1,0:T(8,128)S(1)}, f32[16,512]{1,0:T(8,128)S(1)}, u32[]{:S(2)}, u32[]{:S(2)}) collective-permute-start(f32[16,512]{1,0:T(8,128)S(1)} %get-tuple-element.32), channel_id=1, source_target_pairs={{0,24},{4,28},{8,16},{12,20},{16,8},{20,12},{24,0},{28,4},{1,25},{... | collective-permute-start | bytes 98312 | tf_op jit(solution)/shard_map/ppermute | solution.py:353
  38.7 3.9 %collective-permute-start.15 = (f32[16,512]{1,0:T(8,128)S(1)}, f32[16,512]{1,0:T(8,128)S(1)}, u32[]{:S(2)}, u32[]{:S(2)}) collective-permute-start(f32[16,512]{1,0:T(8,128)S(1)} %get-tuple-element.32), channel_id=1, source_target_pairs={{0,16},{4,20},{8,24},{12,28},{16,0},{20,4},{24,8},{28,12},{1,17},{... | collective-permute-start | bytes 98312 | tf_op jit(solution)/shard_map/ppermute | solution.py:353
  39.2 3.9 %collective-permute-start.14 = (f32[16,512]{1,0:T(8,128)S(1)}, f32[16,512]{1,0:T(8,128)S(1)}, u32[]{:S(2)}, u32[]{:S(2)}) collective-permute-start(f32[16,512]{1,0:T(8,128)S(1)} %get-tuple-element.32), channel_id=1, source_target_pairs={{0,8},{4,12},{8,0},{12,4},{16,24},{20,28},{24,16},{28,20},{1,9},{5... | collective-permute-start | bytes 98312 | tf_op jit(solution)/shard_map/ppermute | solution.py:353
  43.1 7.6 %collective-permute-start.17 = (f32[4,16,512]{2,1,0:T(8,128)S(1)}, f32[4,16,512]{2,1,0:T(8,128)S(1)}, u32[]{:S(2)}, u32[]{:S(2)}) collective-permute-start(f32[4,16,512]{2,1,0:T(8,128)S(1)} %pad_maximum_fusion.1.yeven_ref), channel_id=1, source_target_pairs={{0,4},{4,0},{8,12},{12,8},{16,20},{20,16},{24,28},{28,24},{1,5},{5... | collective-permute-start | bytes 393224 | tf_op jit(solution)/shard_map/ppermute | solution.py:353
  43.2 6.3 %collective-permute-start.20 = (f32[16,640]{1,0:T(8,128)S(1)}, f32[16,640]{1,0:T(8,128)S(1)}, u32[]{:S(2)}, u32[]{:S(2)}) collective-permute-start(f32[16,640]{1,0:T(8,128)S(1)} %get-tuple-element.33.rest_4_), channel_id=1, source_target_pairs={{0,3},{1,2},{2,1},{3,0},{4,7},{5,6},{6,5},{7,4},{8,11},{9,10},{10,... | collective-permute-start | bytes 122888 | tf_op jit(solution)/shard_map/ppermute | solution.py:353
  45.1 5.6 %collective-permute-start.19 = (f32[16,640]{1,0:T(8,128)S(1)}, f32[16,640]{1,0:T(8,128)S(1)}, u32[]{:S(2)}, u32[]{:S(2)}) collective-permute-start(f32[16,640]{1,0:T(8,128)S(1)} %get-tuple-element.33.rest_4_), channel_id=1, source_target_pairs={{0,2},{1,3},{2,0},{3,1},{4,6},{5,7},{6,4},{7,5},{8,10},{9,11},{10,... | collective-permute-start | bytes 122888 | tf_op jit(solution)/shard_map/ppermute | solution.py:353
  45.1 5.6 %collective-permute-start.18 = (f32[16,640]{1,0:T(8,128)S(1)}, f32[16,640]{1,0:T(8,128)S(1)}, u32[]{:S(2)}, u32[]{:S(2)}) collective-permute-start(f32[16,640]{1,0:T(8,128)S(1)} %get-tuple-element.33.rest_4_), channel_id=1, source_target_pairs={{0,1},{1,0},{2,3},{3,2},{4,5},{5,4},{6,7},{7,6},{8,9},{9,8},{10,11... | collective-permute-start | bytes 122888 | tf_op jit(solution)/shard_map/ppermute | solution.py:353

commit v3 on v0

v3 whole, which is shorter than its diff:
```python
import functools
import math

import jax
import jax.numpy as jnp
from jax import lax
from jax.experimental import pallas as pl
from jax.experimental.pallas import tpu as pltpu
from jax.sharding import PartitionSpec as P


highest = lax.Precision.HIGHEST
f32 = jnp.float32
bf16 = jnp.bfloat16
VMEM = pltpu.MemorySpace.VMEM
HBM = pltpu.MemorySpace.HBM
SMEM = pltpu.MemorySpace.SMEM
LANES = 128
VMEM_LIMIT = 16 * 1024 * 1024
LOAD_FLOPS = 20_000_000_000


def dot_nt(a, b, precision=highest):
    return lax.dot_general(
        a, b, (((1,), (1,)), ((), ())), precision=precision, preferred_element_type=f32
    )


def dot_nn(a, b, precision=highest):
    return lax.dot_general(
        a, b, (((1,), (0,)), ((), ())), precision=precision, preferred_element_type=f32
    )


def dot_tn(a, b, precision=highest):
    return lax.dot_general(
        a, b, (((0,), (0,)), ((), ())), precision=precision, preferred_element_type=f32
    )


def split(x):
    hi = x.astype(bf16)
    lo = (x - hi.astype(f32)).astype(bf16)
    return hi, lo


def split_rows(x):
    hi, lo = split(x)
    return jnp.concatenate([hi, lo], axis=0)


def three_pass(dot, a, b):
    a_hi, a_lo = split(a)
    b_hi, b_lo = split(b)
    n = a.shape[0]
    top = dot(jnp.concatenate([a_hi, a_lo], axis=0), b_hi, None)
    return top[:n] + top[n:] + dot(a_hi, b_lo, None)


def eye(n):
    return (
        lax.broadcasted_iota(jnp.int32, (n, n), 0) == lax.broadcasted_iota(jnp.int32, (n, n), 1)
    ).astype(f32)


def eliminate(stack, n):
    m = stack.shape[1]
    row_at = lax.broadcasted_iota(jnp.int32, (n, m), 0)
    lane_at = lax.broadcasted_iota(jnp.int32, (n, m), 1)
    for j in range(0, n - 2, 2):
        one = jnp.broadcast_to(stack[:, j : j + 1], (n, m))
        two = jnp.broadcast_to(stack[:, j + 1 : j + 2], (n, m))
        a, b, d = one[j : j + 1], two[j : j + 1], two[j + 1 : j + 2]
        row_one, row_two = stack[j : j + 1], stack[j + 1 : j + 2]
        over = 1.0 / (a * d - b * b)
        scaled_one = (d * row_one - b * row_two) * over
        scaled_two = (a * row_two - b * row_one) * over
        below = row_at > j + 1
        stack = (
            stack
            - jnp.where(below, one, 0.0) * scaled_one
            - jnp.where(below, two, 0.0) * scaled_two
        )
    odd = row_at % 2 == 1
    above = jnp.concatenate([stack[n - 1 :], stack[: n - 1]], axis=0)
    pivot = jnp.sum(jnp.where(row_at == lane_at + 1, above, 0.0), axis=1, keepdims=True)
    beside = jnp.sum(jnp.where(row_at == lane_at + 1, stack, 0.0), axis=1, keepdims=True)
    ratio = beside / jnp.where(odd[:, :1], pivot, 1.0)
    stack = jnp.where(odd, stack - ratio * above, stack)
    diagonal = jnp.sum(jnp.where(row_at == lane_at, stack, 0.0), axis=1, keepdims=True)
    return stack / jnp.sqrt(diagonal)


def place(block_cols_ref, b, k, me_col, per_span, row_count):
    g = block_cols_ref[k, b]
    span = lax.div(g, per_span)
    return (lax.div(span, row_count) ^ me_col) * per_span + lax.rem(g, per_span)


def load_kernel(x_hbm, p_hbm, cols_hbm, live_hbm, pair_ref, cols_ref, live_ref, sems):
    w = x_hbm.shape[0]
    copies = [
        pltpu.make_async_copy(x_hbm, pair_ref.at[:w], sems.at[0]),
        pltpu.make_async_copy(p_hbm, pair_ref.at[w:], sems.at[1]),
        pltpu.make_async_copy(cols_hbm, cols_ref, sems.at[2]),
        pltpu.make_async_copy(live_hbm, live_ref, sems.at[3]),
    ]
    for copy in copies:
        copy.start()
    for copy in copies:
        copy.wait()


def forward_kernel(sizes, cols_ref, live_ref, even_ref, odd_ref, *rest):
    row_count, col_count, _, width, bs = sizes
    x_refs = rest[:col_count]
    blocks_ref, keep_ref, send_ref, extra_ref, picks = rest[col_count:]
    per_span = keep_ref.shape[2] // bs
    me_col = lax.axis_index("col")
    me_row = lax.axis_index("row")
    for s in range(col_count):
        for o in range(per_span):
            picks[s * per_span + o] = split_rows(x_refs[s][:width, o * bs : (o + 1) * bs])
    pair = x_refs[0][...]
    gram = dot_nt(pair, pair)

    def two_spans(h, cross):
        for i, (out_ref, rows_ref) in enumerate(((keep_ref, even_ref), (send_ref, odd_ref))):
            forward = forward_span(
                sizes, 2 * h + i, cols_ref, live_ref, picks, blocks_ref, per_span, me_row, me_col
            )
            out_ref[h] = forward
            cross = cross + three_pass(dot_nt, rows_ref[h, :width, :], forward)
        return cross

    cross = lax.fori_loop(0, row_count // 2, two_spans, jnp.zeros((width, width), f32))
    extra_ref[...] = pack([gram[:width, :width], gram[:width, width:], gram[width:, width:], cross])


def forward_span(
    sizes, s, cols_ref, live_ref, picks, blocks_ref, per_span, me_row, me_col
):
    row_count, _, slots, _, _ = sizes
    n = picks.shape[1] // 2
    parts = []
    for o in range(per_span):
        b = (me_row ^ s) * per_span + o
        tiles, chosen = [], []
        for k in range(slots):
            w = (k < live_ref[0, b]).astype(f32)
            at = place(cols_ref, b, k, me_col, per_span, row_count)
            tiles.append(blocks_ref[b, k])
            chosen.append(picks[at] * w.astype(bf16))
        both = dot_nt(jnp.concatenate(chosen, axis=1), jnp.concatenate(tiles, axis=1), None)
        parts.append(both[:n] + both[n:])
    return jnp.concatenate(parts, axis=1)


def backward_spans(sizes, parity, cols_ref, live_ref, rows_ref, blocks_ref, spread):
    row_count, _, slots, width, bs = sizes
    per_span = rows_ref.shape[2] // bs
    me_col = lax.axis_index("col")
    me_row = lax.axis_index("row")

    def one_span(h, carry):
        own = split_rows(rows_ref[h, :width, :])
        for o in range(per_span):
            b = (me_row ^ (2 * h + parity)) * per_span + o
            tile = jnp.concatenate([blocks_ref[b, k] for k in range(slots)], axis=1)
            back = dot_nn(own[:, o * bs : (o + 1) * bs], tile, None)
            back = back[:width] + back[width:]
            for k in range(slots):
                at = place(cols_ref, b, k, me_col, per_span, row_count)
                w = (k < live_ref[0, b]).astype(f32)
                spread[at] += back[:, k * bs : (k + 1) * bs] * w
        return carry

    lax.fori_loop(0, row_count // 2, one_span, 0)


def back_even_kernel(sizes, cols_ref, live_ref, even_ref, blocks_ref, spread_ref):
    spread_ref[...] = jnp.zeros_like(spread_ref)
    backward_spans(sizes, 0, cols_ref, live_ref, even_ref, blocks_ref, spread_ref)


def back_odd_kernel(sizes, cols_ref, live_ref, odd_ref, blocks_ref, begun_ref, *rest):
    bs = sizes[4]
    out_refs, spread = rest[:-1], rest[-1]
    spread[...] = begun_ref[...]
    backward_spans(sizes, 1, cols_ref, live_ref, odd_ref, blocks_ref, spread)
    per_span = odd_ref.shape[2] // bs
    for s, out_ref in enumerate(out_refs):
        for o in range(per_span):
            out_ref[:, o * bs : (o + 1) * bs] = spread[s * per_span + o]


def put(ref, vectors, extra):
    h, n = vectors.shape[0] // 2, vectors.shape[1]
    ref[:, :n] = vectors[:h]
    ref[:, n : 2 * n] = vectors[h:]
    ref[:, 2 * n :] = extra


def take(message):
    n = (message.shape[1] - LANES) // 2
    return jnp.concatenate([message[:, :n], message[:, n : 2 * n]], axis=0), message[:, 2 * n :]


def fold_kernel(keep_ref, got_ref, extra_ref, got_extra_ref, low_ref, high_ref):
    extra = extra_ref[...] + got_extra_ref[...]
    n = low_ref.shape[0]
    for i, out_ref in enumerate((low_ref, high_ref)):
        for h in range(n):
            put(out_ref.at[h], keep_ref[i * n + h] + got_ref[i * n + h], extra)


def fold_more_kernel(keep_ref, got_ref, low_ref, high_ref):
    n = low_ref.shape[0]
    low_ref[...] = keep_ref[:n] + got_ref[:n]
    high_ref[...] = keep_ref[n:] + got_ref[n:]


def tree_sum(terms):
    while len(terms) > 1:
        terms = [terms[i] + terms[i + 1] for i in range(0, len(terms), 2)]
    return terms[0]


def middle_kernel(col_count, keep_ref, got_ref, *refs):
    back_refs = refs[:col_count]
    out_ref, y_ref = refs[col_count:]
    forward, sums = take(keep_ref[0] + got_ref[0])
    y = 0.5 * (forward + tree_sum([ref[...] for ref in back_refs]))
    y_ref[...] = y
    put(out_ref, y, sums)


def solve_kernel(col_count, width, *rest):
    y_refs = rest[:col_count]
    aux_ref, wide_ref = rest[col_count:]
    w = width
    sums = tree_sum([take(y_ref[...])[1] for y_ref in y_refs])
    gram_x, xp, pp, xbx = (unpack(sums, i) for i in range(4))
    cross_x = 0.5 * (xbx + xbx.T)
    done = eliminate(jnp.concatenate([gram_x, eye(w), cross_x, xp], axis=1), w)
    inverse_l, below_p = done[:, w : 2 * w], done[:, 3 * w : 4 * w]
    coefficient = dot_tn(inverse_l, done[:, 2 * w : 3 * w])
    xr = cross_x - dot_nn(gram_x, coefficient)
    aux_ref[...] = jnp.concatenate(
        [-coefficient.T, coefficient, xr, xp, pp, cross_x, inverse_l, jnp.zeros_like(xp)], axis=1
    )
    upper = jnp.concatenate([dot_nn(inverse_l, xr), below_p], axis=1)
    wide_ref[...] = jnp.concatenate(
        [dot_tn(upper, upper), -dot_tn(upper, inverse_l), jnp.zeros((2 * w, w), f32)], axis=1
    )


def forward_rest_kernel(sizes, cols_ref, live_ref, aux_ref, *rest):
    row_count, col_count, _, width, bs = sizes
    y_refs, x_refs = (rest[i * col_count : (i + 1) * col_count] for i in range(2))
    blocks_ref, out_ref, resid_ref, resid_out_ref, picks = rest[2 * col_count :]
    span_rows = out_ref.shape[2]
    per_span = span_rows // bs
    me_col = lax.axis_index("col")
    me_row = lax.axis_index("row")
    minus_c_t = aux_ref[:, :width]
    for s in range(col_count):
        rest_s = take(y_refs[s][...])[0] + dot_nn(minus_c_t, x_refs[s][:width])
        if s == 0:
            resid_ref[...] = rest_s
            resid_out_ref[...] = rest_s
        both = jnp.concatenate([rest_s, x_refs[s][width:]], axis=0)
        for o in range(per_span):
            picks[s * per_span + o] = split_rows(both[:, o * bs : (o + 1) * bs])

    def two_spans(h, carry):
        for s in (2 * h, 2 * h + 1):
            out_ref[s] = forward_span(
                sizes, s, cols_ref, live_ref, picks, blocks_ref, per_span, me_row, me_col
            )
        return carry

    lax.fori_loop(0, row_count // 2, two_spans, 0)


def iota(shape, axis):
    return lax.broadcasted_iota(jnp.int32, shape, axis)


def pack(matrices):
    h = matrices[0].shape[0] // 2
    return jnp.concatenate([part for m in matrices for part in (m[:h], m[h:])], axis=1)


def unpack(packed, i):
    w = 2 * packed.shape[0]
    at = 2 * i * w
    return jnp.concatenate([packed[:, at : at + w], packed[:, at + w : at + 2 * w]], axis=0)


def gram_kernel(
    width, half, aux_ref, even_ref, odd_ref, yeven_ref, yodd_ref, forward_ref, pair_ref,
    resid_ref, part_ref,
):
    w = width
    minus_c_t = aux_ref[:, :w]

    def two_spans(h, cross):
        for i, (rows_ref, y_ref) in enumerate(((even_ref, yeven_ref), (odd_ref, yodd_ref))):
            rest_q = y_ref[h] + three_pass(dot_nn, minus_c_t, rows_ref[h, :w, :])
            both = jnp.concatenate([rest_q, rows_ref[h, w:, :]], axis=0)
            cross = cross + three_pass(dot_nt, both, forward_ref[2 * h + i])
        return cross

    mine = resid_ref[...]
    gram = dot_nt(mine, jnp.concatenate([mine, pair_ref[w:]], axis=0))
    cross = lax.fori_loop(0, half, two_spans, jnp.zeros((2 * w, 2 * w), f32))
    rar, pap = cross[:w, :w], cross[w:, w:]
    rar = 0.5 * (rar + rar.T)
    pap = 0.5 * (pap + pap.T)
    rap = 0.5 * (cross[:w, w:] + cross[w:, :w].T)
    row, lane = iota((w, w), 0), iota((w, w), 1)
    diagonal = jnp.sum(jnp.where(row == lane, rar, 0.0), axis=1, keepdims=True)
    first = jnp.where(row <= lane, gram[:, :w], rar)
    corner = jnp.where((row == w - 1) & (lane == 1), diagonal[0:1, 0:1], 0.0)
    second = jnp.where(row <= lane, pap, jnp.where(lane == 0, diagonal, corner))
    part = pack([first, second, gram[:, w:], rap])
    for d in range(part_ref.shape[0]):
        part_ref[d] = part


def last_kernel(
    width, scale, parts_ref, aux_ref, wide_ref, xp_ref, resid_ref, x_next_ref, reduced_ref
):
    w = width
    total = parts_ref[0]
    for d in range(1, parts_ref.shape[0]):
        total = total + parts_ref[d]
    first, second, rp, rap = (unpack(total, i) for i in range(4))
    row, lane = iota((w, w), 0), iota((w, w), 1)
    below = first.T
    diagonal = jnp.where(iota((w, 1), 0) == 0, second[w - 1 : w, 1:2], second[:, 0:1])
    rr = jnp.where(row <= lane, first, below)
    rar = jnp.where(row > lane, first, jnp.where(row < lane, below, diagonal))
    pap = jnp.where(row <= lane, second, second.T)
    coefficient, xr, xp, pp, xax, inverse_x = (aux_ref[:, i * w : (i + 1) * w] for i in range(1, 7))
    schur = (
        jnp.concatenate(
            [jnp.concatenate([rr, rp], axis=1), jnp.concatenate([rp.T, pp], axis=1)], axis=0
        )
        - wide_ref[:, : 2 * w]
    )
    xar = rr + dot_tn(coefficient, xr)
    xap = rp + dot_tn(coefficient, xp)
    gram_apply = jnp.concatenate(
        [
            jnp.concatenate([xax, xar, xap], axis=1),
            jnp.concatenate([xar.T, rar, rap], axis=1),
            jnp.concatenate([xap.T, rap.T, pap], axis=1),
        ],
        axis=0,
    )
    n = 3 * w
    rest = eliminate(
        jnp.concatenate([schur, eye(2 * w), wide_ref[:, 2 * w : 3 * w]], axis=1), 2 * w
    )
    inverse_l = jnp.concatenate(
        [
            jnp.concatenate([inverse_x, jnp.zeros((w, 2 * w), f32)], axis=1),
            jnp.concatenate([rest[:, 4 * w : 5 * w], rest[:, 2 * w : 4 * w]], axis=1),
        ],
        axis=0,
    )
    reduced = dot_nt(dot_nn(inverse_l, gram_apply), inverse_l)
    reduced_ref[...] = reduced
    shifted = reduced + 3.0 * eye(n)
    target = dot_nn(shifted, shifted[:, :w])
    gram_fresh = dot_tn(target, target)
    mixing = dot_tn(target, inverse_l)
    weights = scale * eliminate(jnp.concatenate([gram_fresh, mixing], axis=1), w)[:, w:]
    basis = jnp.concatenate([xp_ref[:w, :], resid_ref[...], xp_ref[w:, :]], axis=0)
    x_next_ref[...] = dot_nn(weights, basis)


def per_device(block_vecs, direction, blocks, block_cols, live_counts):
    row_count = lax.axis_size("row")
    col_count = lax.axis_size("col")
    width, span_rows = block_vecs.shape
    block_rows, slots, bs = blocks.shape[:3]
    per_span = span_rows // bs
    half = row_count // 2
    order_total = span_rows * row_count * col_count
    col_blocks = col_count * per_span
    sizes = (row_count, col_count, slots, width, bs)
    shape = lambda *dims: jax.ShapeDtypeStruct(dims, f32)
    in_hbm = lambda array: pltpu.with_memory_space_constraint(array, HBM)
    spec = {
        "v": pl.BlockSpec(memory_space=VMEM),
        "s": pl.BlockSpec(memory_space=SMEM),
        "h": pl.BlockSpec(memory_space=HBM),
    }

    def call(kernel, ins, args, outs, scratch=(), cost=None):
        return pl.pallas_call(
            kernel,
            in_specs=[spec[letter] for letter in ins],
            out_specs=[spec["v"]] * len(outs),
            out_shape=outs,
            scratch_shapes=scratch,
            compiler_params=pltpu.CompilerParams(vmem_limit_bytes=VMEM_LIMIT),
            cost_estimate=cost,
        )(*args)

    def swap(array, axis, s):
        return lax.ppermute(array, axis, [(i, i ^ s) for i in range(lax.axis_size(axis))])

    far = list(reversed(range(1, col_count)))
    bits = row_bits(row_count)

    def gather_rows(array):
        even = array[None]
        for bit in bits:
            got = swap(even, "row", bit)
            even = jnp.concatenate([even, got], axis=0)
        return even, swap(even, "row", 1)

    def over_col(arrays):
        got = {s: swap(arrays[s], "col", s) for s in far}
        return [arrays[0]] + [got[s] for s in range(1, col_count)]

    pair, cols, live = call(
        load_kernel,
        "hhhh",
        [in_hbm(a) for a in (block_vecs, direction, block_cols.T, live_counts.T)],
        [
            shape(2 * width, span_rows),
            jax.ShapeDtypeStruct((slots, block_rows), jnp.int32),
            jax.ShapeDtypeStruct((1, block_rows), jnp.int32),
        ],
        [pltpu.SemaphoreType.DMA((4,))],
        pl.CostEstimate(flops=LOAD_FLOPS, bytes_accessed=0, transcendentals=0),
    )
    pair_cols = over_col([pair] * col_count)
    pair_even, pair_odd = gather_rows(pair)
    (begun,) = call(
        functools.partial(back_even_kernel, sizes),
        "ssvv",
        [cols, live, pair_even, blocks],
        [shape(col_blocks, width, bs)],
    )
    backs = call(
        functools.partial(back_odd_kernel, sizes),
        "ssvvv",
        [cols, live, pair_odd, blocks, begun],
        [shape(width, span_rows)] * col_count,
        [pltpu.VMEM((col_blocks, width, bs), f32)],
    )
    keep, send, extra = call(
        functools.partial(forward_kernel, sizes),
        "ssvv" + "v" * (col_count + 1),
        [cols, live, pair_even, pair_odd, *pair_cols, blocks],
        [shape(half, width, span_rows)] * 2 + [shape(width // 2, LANES)],
        [pltpu.VMEM((col_blocks, 2 * width, bs), bf16)],
    )
    got_pair = swap(send, "row", 1)
    got_extra = swap(extra, "row", 1)
    got_backs = over_col(backs)
    low, high = call(
        fold_kernel,
        "vvvv",
        [keep, got_pair, extra, got_extra],
        [shape(half // 2, width // 2, 2 * span_rows + LANES)] * 2,
    )
    for bit in reversed(bits):
        got = swap(high, "row", bit)
        if bit != bits[0]:
            low, high = call(
                fold_more_kernel,
                "vv",
                [low, got],
                [shape(low.shape[0] // 2, width // 2, 2 * span_rows + LANES)] * 2,
            )
    message, image = call(
        functools.partial(middle_kernel, col_count),
        "v" * (2 + col_count),
        [low, got, *got_backs],
        [shape(width // 2, 2 * span_rows + LANES), shape(width, span_rows)],
    )
    image_cols = over_col([message] * col_count)
    image_even, image_odd = gather_rows(image)
    aux, wide = call(
        functools.partial(solve_kernel, col_count, width),
        "v" * col_count,
        image_cols,
        [shape(width, LANES), shape(2 * width, 4 * width)],
    )
    forward_rp, resid, resid_out = call(
        functools.partial(forward_rest_kernel, sizes),
        "ssv" + "v" * (2 * col_count + 1),
        [cols, live, aux, *image_cols, *pair_cols, blocks],
        [shape(row_count, 2 * width, span_rows)] + [shape(width, span_rows)] * 2,
        [pltpu.VMEM((col_blocks, 4 * width, bs), bf16)],
    )
    (part,) = call(
        functools.partial(gram_kernel, width, half),
        "v" * 8,
        [aux, pair_even, pair_odd, image_even, image_odd, forward_rp, pair, resid],
        [shape(row_count * col_count, width // 2, LANES)],
    )
    parts = lax.all_to_all(part, ("col", "row"), 0, 0)
    x_next, reduced = call(
        functools.partial(last_kernel, width, math.sqrt(order_total)),
        "v" * 5,
        [parts, aux, wide, pair, resid],
        [shape(width, span_rows), shape(3 * width, 3 * width)],
    )
    return (x_next, reduced, resid_out)


def row_bits(row_count):
    return [1 << i for i in range(1, row_count.bit_length() - 1)]


def solution(mesh):
    return jax.shard_map(
        per_device,
        mesh=mesh,
        in_specs=(
            P(None, ("col", "row")),
            P(None, ("col", "row")),
            P("col", "row", None, None),
            P("col", "row"),
            P("col", "row"),
        ),
        out_specs=(P(None, ("col", "row")), P(), P(None, ("col", "row"))),
        check_vma=False,
    )
```

time: 748 us -> 84.5 us (0.11)
  other arithmetic: 385 us -> 0.04 us
  blocking collectives: 129 us -> 11.7 us
  loops' own time: 111 us -> 0 us
  waiting for transfers between devices: 87 us -> 28.8 us
  starting transfers between devices: 0.16 us -> 24.7 us
  Pallas kernels: 0 us -> 18.3 us
  between operations: 14.1 us -> 0.74 us
  matrix products: 9.73 us -> 0 us
    reduce_sum x816 -> x0, other arithmetic: 226 us -> none  [the longest x128 78 us: row_step(): pivot = jnp.sum(row_now * pick)]
    div x192 -> x0, other arithmetic: 126 us -> none  [the longest x128 83.7 us: row_step(): value = (right_row - jnp.sum(row_now[:, None] * solved, axis=0)) / pivot]
    another operation x9 -> x0, loops' own time: 111 us -> none  [the longest x3 108 us: cholesky_lower(): return lax.fori_loop(0, order_small, column_step, jnp.zeros_like(matrix))]
    reduce_scatter x4 -> x0, waiting for transfers between devices: 86.9 us -> none  [the longest x1 35.9 us: per_device(): lax.psum_scatter(forward, 'row', scatter_dimension=1, tiled=True)]
    psum x2 -> x0, blocking collectives: 79.3 us -> none  [the longest x1 39.9 us: per_device(): lax.psum((outer(basis, basis), gram_apply), ('row', 'col'))]
    all_gather x4 -> x0, blocking collectives: 50.1 us -> none  [the longest x1 15.4 us: per_device(): pair_cols = lax.all_gather(paired, 'col', axis=1, tiled=True)]
    ppermute x0 -> x19, waiting for transfers between devices: none -> 28.8 us  [swap(): lax.ppermute(array, axis, [(i, i ^ s) for i in range(lax.axis_size(axis))])]
    ppermute x0 -> x19, starting transfers between devices: none -> 24.7 us  [swap(): lax.ppermute(array, axis, [(i, i ^ s) for i in range(lax.axis_size(axis))])]
  transfers between devices with their start and end apart: 4 -> 19, of which waited for: 4 -> 13; matrix products, arithmetic and copies ran while one was open for 1% -> 0% of each run, Pallas kernels for 0% -> 9%
where the time goes in v3:
time: 84.5 us; the launch traced here: 84.4 us
  waiting for transfers between devices  28.8 us (34%)
  starting transfers between devices  24.7 us (29%)
  Pallas kernels  18.3 us (22%)
  blocking collectives  11.7 us (14%)
    ppermute x19, waiting for transfers between devices, swap(): lax.ppermute(array, axis, [(i, i ^ s) for i in range(lax.axis_size(axis))])  28.8 us
    ppermute x19, starting transfers between devices, swap(): lax.ppermute(array, axis, [(i, i ^ s) for i in range(lax.axis_size(axis))])  24.7 us
    pallas_call x11, Pallas kernels, call(): pl.pallas_call(kernel, in_specs=[spec[letter] for letter in ins], out_spe...  18.3 us
    all_to_all x1, blocking collectives, per_device(): parts = lax.all_to_all(part, ('col', 'row'), 0, 0)  11.7 us
  transfers between devices with their start and end apart: 19, of which 13 were waited for; matrix products, arithmetic and copies ran while one was open for 0% of the time, Pallas kernels for 9%

profile of v3, /device:TPU:0, one launch (start us, length us, event | category | flops | bytes accessed | tf_op | source)
XLA Modules:
  0.0 84.4 jit_solution(2661776189111327037)
XLA Ops:
  0.6 1.0 %shard_map.76 = (f32[32,512]{1,0:T(8,128)S(1)}, s32[2,32]{1,0:T(2,128)S(1)}, s32[1,32]{1,0:T(1,128)S(1)}) custom-call(f32[16,512]{1,0:T(8,128)} %x_hbm.1, f32[16,512]{1,0:T(8,128)} %p_hbm.1, s32[2,32]{1,0:T(2,128)} %bitcast.10, s32[1,32]{1,0:T(1,128)} %bitcast.11), custom_call_target="tpu_custom_call" | custom-call | flops 20000000000 | tf_op jit(solution)/shard_map/pallas_call | solution.py:404
  1.6 3.0 %collective-permute-start = (f32[1,32,512]{2,1,0:T(8,128)S(1)}, f32[1,32,512]{2,1,0:T(8,128)S(1)}, u32[]{:S(2)}, u32[]{:S(2)}) collective-permute-start(f32[1,32,512]{2,1,0:T(8,128)S(1)} %bitcast.4), channel_id=1, source_target_pairs={{0,8},{4,12},{8,0},{12,4},{16,24},{20,28},{24,16},{28,20},{1,9},{5... | collective-permute-start | bytes 196616 | tf_op jit(solution)/shard_map/ppermute | solution.py:415
  4.6 2.2 %collective-permute-done = f32[1,32,512]{2,1,0:T(8,128)S(1)} collective-permute-done((f32[1,32,512]{2,1,0:T(8,128)S(1)}, f32[1,32,512]{2,1,0:T(8,128)S(1)}, u32[]{:S(2)}, u32[]{:S(2)}) %collective-permute-start) | collective-permute-done | bytes 65568 | tf_op jit(solution)/shard_map/ppermute | solution.py:415
  6.9 2.1 %collective-permute-start.1 = (f32[2,32,512]{2,1,0:T(8,128)S(1)}, f32[2,32,512]{2,1,0:T(8,128)S(1)}, u32[]{:S(2)}, u32[]{:S(2)}) collective-permute-start(f32[2,32,512]{2,1,0:T(8,128)S(1)} %pad_maximum_fusion.1), channel_id=1, source_target_pairs={{0,16},{4,20},{8,24},{12,28},{16,0},{20,4},{24,8},{28,12},{1,17},{... | collective-permute-start | bytes 393224 | tf_op jit(solution)/shard_map/ppermute | solution.py:415
  9.0 2.9 %collective-permute-done.1 = f32[2,32,512]{2,1,0:T(8,128)S(1)} collective-permute-done((f32[2,32,512]{2,1,0:T(8,128)S(1)}, f32[2,32,512]{2,1,0:T(8,128)S(1)}, u32[]{:S(2)}, u32[]{:S(2)}) %collective-permute-start.1) | collective-permute-done | bytes 131104 | tf_op jit(solution)/shard_map/ppermute | solution.py:415
  12.1 2.1 %collective-permute-start.3 = (f32[32,512]{1,0:T(8,128)S(1)}, f32[32,512]{1,0:T(8,128)S(1)}, u32[]{:S(2)}, u32[]{:S(2)}) collective-permute-start(f32[32,512]{1,0:T(8,128)S(1)} %get-tuple-element.28.rest_0_.rest_4_.pair_ref.xp_ref), channel_id=1, source_target_pairs={{0,1},{1,0},{2,3},{3,2},{4,5},{5,4},{6,7},{7,6},{8,9},{9,8},{10,11... | collective-permute-start | bytes 196616 | tf_op jit(solution)/shard_map/ppermute | solution.py:415
  14.2 2.6 %collective-permute-start.4 = (f32[32,512]{1,0:T(8,128)S(1)}, f32[32,512]{1,0:T(8,128)S(1)}, u32[]{:S(2)}, u32[]{:S(2)}) collective-permute-start(f32[32,512]{1,0:T(8,128)S(1)} %get-tuple-element.28.rest_0_.rest_4_.pair_ref.xp_ref), channel_id=1, source_target_pairs={{0,2},{1,3},{2,0},{3,1},{4,6},{5,7},{6,4},{7,5},{8,10},{9,11},{10,... | collective-permute-start | bytes 196616 | tf_op jit(solution)/shard_map/ppermute | solution.py:415
  16.9 5.0 %collective-permute-done.4.rest_2_.rest_6_ = f32[32,512]{1,0:T(8,128)S(1)} collective-permute-done((f32[32,512]{1,0:T(8,128)S(1)}, f32[32,512]{1,0:T(8,128)S(1)}, u32[]{:S(2)}, u32[]{:S(2)}) %collective-permute-start.4) | collective-permute-done | bytes 65568 | tf_op jit(solution)/shard_map/ppermute | solution.py:415
  21.9 1.0 %collective-permute-done.5.rest_3_.rest_7_ = f32[32,512]{1,0:T(8,128)S(1)} collective-permute-done((f32[32,512]{1,0:T(8,128)S(1)}, f32[32,512]{1,0:T(8,128)S(1)}, u32[]{:S(2)}, u32[]{:S(2)}) %collective-permute-start.5) | collective-permute-done | bytes 65568 | tf_op jit(solution)/shard_map/ppermute | solution.py:415
  22.9 3.1 %shard_map.77 = (f32[4,16,512]{2,1,0:T(8,128)S(1)}, f32[4,16,512]{2,1,0:T(8,128)S(1)}, f32[8,128]{1,0:T(8,128)S(1)}) custom-call(s32[2,32]{1,0:T(2,128)S(1)} %get-tuple-element.26.cols_ref, s32[1,32]{1,0:T(1,128)S(1)} %get-tuple-element.27.live_ref, f32[4,32,512]{2,1,0:T(8,128)S(1)} %pad_maximum_fusion.even_ref, ...), custom_call_target="tpu_custom_call" | custom-call | tf_op jit(solution)/shard_map/pallas_call | solution.py:404
  26.6 0.8 collective-permute-done.7.got_extra_ref
  27.4 1.6 %collective-permute-start.8 = (f32[2,8,1152]{2,1,0:T(8,128)S(1)}, f32[2,8,1152]{2,1,0:T(8,128)S(1)}, u32[]{:S(2)}, u32[]{:S(2)}) collective-permute-start(f32[2,8,1152]{2,1,0:T(8,128)S(1)} %get-tuple-element.33), channel_id=1, source_target_pairs={{0,16},{4,20},{8,24},{12,28},{16,0},{20,4},{24,8},{28,12},{1,17},{... | collective-permute-start | bytes 221192 | tf_op jit(solution)/shard_map/ppermute | solution.py:415
  29.0 3.0 %collective-permute-done.8.got_ref = f32[2,8,1152]{2,1,0:T(8,128)S(1)} collective-permute-done((f32[2,8,1152]{2,1,0:T(8,128)S(1)}, f32[2,8,1152]{2,1,0:T(8,128)S(1)}, u32[]{:S(2)}, u32[]{:S(2)}) %collective-permute-start.8) | collective-permute-done | bytes 73760 | tf_op jit(solution)/shard_map/ppermute | solution.py:415
  32.0 1.6 %collective-permute-start.9 = (f32[1,8,1152]{2,1,0:T(8,128)S(1)}, f32[1,8,1152]{2,1,0:T(8,128)S(1)}, u32[]{:S(2)}, u32[]{:S(2)}) collective-permute-start(f32[1,8,1152]{2,1,0:T(8,128)S(1)} %get-tuple-element.35), channel_id=1, source_target_pairs={{0,8},{4,12},{8,0},{12,4},{16,24},{20,28},{24,16},{28,20},{1,9},{5... | collective-permute-start | bytes 110600 | tf_op jit(solution)/shard_map/ppermute | solution.py:415
  33.6 1.3 %shard_map.80.begun_ref = f32[16,16,128]{2,1,0:T(8,128)S(1)} custom-call(s32[2,32]{1,0:T(2,128)S(1)} %get-tuple-element.26.cols_ref, s32[1,32]{1,0:T(1,128)S(1)} %get-tuple-element.27.live_ref, f32[4,32,512]{2,1,0:T(8,128)S(1)} %pad_maximum_fusion.even_ref, bf16[32,2,128,128]{3,2,1,0:T(8,128)(2,1)S(1)} %copy-done), custom_call_target="tpu_custom_call" | custom-call | tf_op jit(solution)/shard_map/pallas_call | solution.py:404
  34.8 1.3 %shard_map.81 = (f32[16,512]{1,0:T(8,128)S(1)}, f32[16,512]{1,0:T(8,128)S(1)}, f32[16,512]{1,0:T(8,128)S(1)}, f32[16,512]{1,0:T(8,128)S(1)}) custom-call(s32[2,32]{1,0:T(2,128)S(1)} %get-tuple-element.26.cols_ref, s32[1,32]{1,0:T(1,128)S(1)} %get-tuple-element.27.live_ref, f32[4,32,512]{2,1,0:T(8,128)S(1)} %collective-permute-done.2.odd_ref, ...), custom_call_target="tpu_custom_call" | custom-call | tf_op jit(solution)/shard_map/pallas_call | solution.py:404
  36.1 1.3 %collective-permute-start.10 = (f32[16,512]{1,0:T(8,128)S(1)}, f32[16,512]{1,0:T(8,128)S(1)}, u32[]{:S(2)}, u32[]{:S(2)}) collective-permute-start(f32[16,512]{1,0:T(8,128)S(1)} %get-tuple-element.37), channel_id=1, source_target_pairs={{0,1},{1,0},{2,3},{3,2},{4,5},{5,4},{6,7},{7,6},{8,9},{9,8},{10,11... | collective-permute-start | bytes 98312 | tf_op jit(solution)/shard_map/ppermute | solution.py:415
  37.4 1.7 %collective-permute-start.11 = (f32[16,512]{1,0:T(8,128)S(1)}, f32[16,512]{1,0:T(8,128)S(1)}, u32[]{:S(2)}, u32[]{:S(2)}) collective-permute-start(f32[16,512]{1,0:T(8,128)S(1)} %get-tuple-element.38), channel_id=1, source_target_pairs={{0,2},{1,3},{2,0},{3,1},{4,6},{5,7},{6,4},{7,5},{8,10},{9,11},{10,... | collective-permute-start | bytes 98312 | tf_op jit(solution)/shard_map/ppermute | solution.py:415
  39.2 1.4 %collective-permute-start.12 = (f32[16,512]{1,0:T(8,128)S(1)}, f32[16,512]{1,0:T(8,128)S(1)}, u32[]{:S(2)}, u32[]{:S(2)}) collective-permute-start(f32[16,512]{1,0:T(8,128)S(1)} %get-tuple-element.39), channel_id=1, source_target_pairs={{0,3},{1,2},{2,1},{3,0},{4,7},{5,6},{6,5},{7,4},{8,11},{9,10},{10,... | collective-permute-start | bytes 98312 | tf_op jit(solution)/shard_map/ppermute | solution.py:415
  40.6 2.3 %collective-permute-done.11.refs_2_ = f32[16,512]{1,0:T(8,128)S(1)} collective-permute-done((f32[16,512]{1,0:T(8,128)S(1)}, f32[16,512]{1,0:T(8,128)S(1)}, u32[]{:S(2)}, u32[]{:S(2)}) %collective-permute-start.11) | collective-permute-done | bytes 32800 | tf_op jit(solution)/shard_map/ppermute | solution.py:415
  42.9 1.9 %collective-permute-done.12.refs_3_ = f32[16,512]{1,0:T(8,128)S(1)} collective-permute-done((f32[16,512]{1,0:T(8,128)S(1)}, f32[16,512]{1,0:T(8,128)S(1)}, u32[]{:S(2)}, u32[]{:S(2)}) %collective-permute-start.12) | collective-permute-done | bytes 32800 | tf_op jit(solution)/shard_map/ppermute | solution.py:415
  45.5 3.4 %collective-permute-done.16 = f32[1,16,512]{2,1,0:T(8,128)S(1)} collective-permute-done((f32[1,16,512]{2,1,0:T(8,128)S(1)}, f32[1,16,512]{2,1,0:T(8,128)S(1)}, u32[]{:S(2)}, u32[]{:S(2)}) %collective-permute-start.16) | collective-permute-done | bytes 32800 | tf_op jit(solution)/shard_map/ppermute | solution.py:415
  48.9 1.5 %collective-permute-start.17 = (f32[2,16,512]{2,1,0:T(8,128)S(1)}, f32[2,16,512]{2,1,0:T(8,128)S(1)}, u32[]{:S(2)}, u32[]{:S(2)}) collective-permute-start(f32[2,16,512]{2,1,0:T(8,128)S(1)} %pad_maximum_fusion.3), channel_id=1, source_target_pairs={{0,16},{4,20},{8,24},{12,28},{16,0},{20,4},{24,8},{28,12},{1,17},{... | collective-permute-start | bytes 196616 | tf_op jit(solution)/shard_map/ppermute | solution.py:415
  50.4 2.7 %collective-permute-done.17 = f32[2,16,512]{2,1,0:T(8,128)S(1)} collective-permute-done((f32[2,16,512]{2,1,0:T(8,128)S(1)}, f32[2,16,512]{2,1,0:T(8,128)S(1)}, u32[]{:S(2)}, u32[]{:S(2)}) %collective-permute-start.17) | collective-permute-done | bytes 65568 | tf_op jit(solution)/shard_map/ppermute | solution.py:415
  53.3 2.0 %collective-permute-start.14 = (f32[8,1152]{1,0:T(8,128)S(1)}, f32[8,1152]{1,0:T(8,128)S(1)}, u32[]{:S(2)}, u32[]{:S(2)}) collective-permute-start(f32[8,1152]{1,0:T(8,128)S(1)} %get-tuple-element.40.rest_0_), channel_id=1, source_target_pairs={{0,2},{1,3},{2,0},{3,1},{4,6},{5,7},{6,4},{7,5},{8,10},{9,11},{10,... | collective-permute-start | bytes 110600 | tf_op jit(solution)/shard_map/ppermute | solution.py:415
  55.3 2.4 %collective-permute-start.15 = (f32[8,1152]{1,0:T(8,128)S(1)}, f32[8,1152]{1,0:T(8,128)S(1)}, u32[]{:S(2)}, u32[]{:S(2)}) collective-permute-start(f32[8,1152]{1,0:T(8,128)S(1)} %get-tuple-element.40.rest_0_), channel_id=1, source_target_pairs={{0,3},{1,2},{2,1},{3,0},{4,7},{5,6},{6,5},{7,4},{8,11},{9,10},{10,... | collective-permute-start | bytes 110600 | tf_op jit(solution)/shard_map/ppermute | solution.py:415
  58.4 2.6 %collective-permute-done.15.rest_3_ = f32[8,1152]{1,0:T(8,128)S(1)} collective-permute-done((f32[8,1152]{1,0:T(8,128)S(1)}, f32[8,1152]{1,0:T(8,128)S(1)}, u32[]{:S(2)}, u32[]{:S(2)}) %collective-permute-start.15) | collective-permute-done | bytes 36896 | tf_op jit(solution)/shard_map/ppermute | solution.py:415
  61.1 2.1 %shard_map.83 = (f32[16,128]{1,0:T(8,128)S(1)}, f32[32,64]{1,0:T(8,128)S(1)}) custom-call(f32[8,1152]{1,0:T(8,128)S(1)} %get-tuple-element.40.rest_0_, f32[8,1152]{1,0:T(8,128)S(1)} %collective-permute-done.13.rest_1_, f32[8,1152]{1,0:T(8,128)S(1)} %collective-permute-done.14.rest_2_, f32[8,1152]{1,0:T(8,128)S(1)} %collective-permute-done.15.rest_3_), custom_call_target="tpu_custom_call" | custom-call | tf_op jit(solution)/shard_map/pallas_call | solution.py:404
  63.2 2.7 %shard_map.84 = (f32[8,32,512]{2,1,0:T(8,128)S(1)}, f32[16,512]{1,0:T(8,128)S(1)}, f32[16,512]{1,0:T(8,128)}) custom-call(s32[2,32]{1,0:T(2,128)S(1)} %get-tuple-element.26.cols_ref, s32[1,32]{1,0:T(1,128)S(1)} %get-tuple-element.27.live_ref, f32[16,128]{1,0:T(8,128)S(1)} %get-tuple-element.41.aux_ref, f32[8,1152]{1,0:T(8,128)S(1)} %get-tuple-element.40.rest_0_, ...), custom_call_target="tpu_custom_call" | custom-call | tf_op jit(solution)/shard_map/pallas_call | solution.py:404
  65.8 2.5 %shard_map.85 = f32[32,8,128]{2,1,0:T(8,128)S(1)} custom-call(f32[16,128]{1,0:T(8,128)S(1)} %get-tuple-element.41.aux_ref, f32[4,32,512]{2,1,0:T(8,128)S(1)} %pad_maximum_fusion.even_ref, f32[4,32,512]{2,1,0:T(8,128)S(1)} %collective-permute-done.2.odd_ref, f32[4,16,512]{2,1,0:T(8,128)S(1)} %pad_maximum_fusion.2.yeven_ref, ...), custom_call_target="tpu_custom_call" | custom-call | tf_op jit(solution)/shard_map/pallas_call | solution.py:404
  68.4 11.7 %all_to_all.5.parts_ref = f32[32,8,128]{2,1,0:T(8,128)S(1)} all-to-all(f32[32,8,128]{2,1,0:T(8,128)S(1)} %shard_map.85), channel_id=1, replica_groups=mesh['row'=8,'col'=4] {'col','row'}, dimensions={0} | all-to-all | bytes 262144 | tf_op jit(solution)/shard_map/all_to_all | solution.py:510
  80.1 4.3 %shard_map.86 = (f32[16,512]{1,0:T(8,128)}, f32[48,48]{1,0:T(8,128)}) custom-call(f32[32,8,128]{2,1,0:T(8,128)S(1)} %all_to_all.5.parts_ref, f32[16,128]{1,0:T(8,128)S(1)} %get-tuple-element.41.aux_ref, f32[32,64]{1,0:T(8,128)S(1)} %get-tuple-element.45.wide_ref, f32[32,512]{1,0:T(8,128)S(1)} %get-tuple-element.28.rest_0_.rest_4_.pair_ref.xp_ref, ...), custom_call_target="tpu_custom_call" | custom-call | tf_op jit(solution)/shard_map/pallas_call | solution.py:404
  (24 shorter events, 2.3 us)
Async XLA Ops:
  0.6 22.2 %copy-start = (bf16[32,2,128,128]{3,2,1,0:T(8,128)(2,1)S(1)}, bf16[32,2,128,128]{3,2,1,0:T(8,128)(2,1)}, u32[]{:S(2)}) copy-start(bf16[32,2,128,128]{3,2,1,0:T(8,128)(2,1)} %rest_8_.1) | copy-start | bytes 6291460
  1.6 5.3 %collective-permute-start = (f32[1,32,512]{2,1,0:T(8,128)S(1)}, f32[1,32,512]{2,1,0:T(8,128)S(1)}, u32[]{:S(2)}, u32[]{:S(2)}) collective-permute-start(f32[1,32,512]{2,1,0:T(8,128)S(1)} %bitcast.4), channel_id=1, source_target_pairs={{0,8},{4,12},{8,0},{12,4},{16,24},{20,28},{24,16},{28,20},{1,9},{5... | collective-permute-start | bytes 196616 | tf_op jit(solution)/shard_map/ppermute | solution.py:415
  6.9 5.1 %collective-permute-start.1 = (f32[2,32,512]{2,1,0:T(8,128)S(1)}, f32[2,32,512]{2,1,0:T(8,128)S(1)}, u32[]{:S(2)}, u32[]{:S(2)}) collective-permute-start(f32[2,32,512]{2,1,0:T(8,128)S(1)} %pad_maximum_fusion.1), channel_id=1, source_target_pairs={{0,16},{4,20},{8,24},{12,28},{16,0},{20,4},{24,8},{28,12},{1,17},{... | collective-permute-start | bytes 393224 | tf_op jit(solution)/shard_map/ppermute | solution.py:415
  12.0 10.9 %collective-permute-start.2 = (f32[4,32,512]{2,1,0:T(8,128)S(1)}, f32[4,32,512]{2,1,0:T(8,128)S(1)}, u32[]{:S(2)}, u32[]{:S(2)}) collective-permute-start(f32[4,32,512]{2,1,0:T(8,128)S(1)} %pad_maximum_fusion.even_ref), channel_id=1, source_target_pairs={{0,4},{4,0},{8,12},{12,8},{16,20},{20,16},{24,28},{28,24},{1,5},{5... | collective-permute-start | bytes 786440 | tf_op jit(solution)/shard_map/ppermute | solution.py:415
  12.1 4.8 %collective-permute-start.3 = (f32[32,512]{1,0:T(8,128)S(1)}, f32[32,512]{1,0:T(8,128)S(1)}, u32[]{:S(2)}, u32[]{:S(2)}) collective-permute-start(f32[32,512]{1,0:T(8,128)S(1)} %get-tuple-element.28.rest_0_.rest_4_.pair_ref.xp_ref), channel_id=1, source_target_pairs={{0,1},{1,0},{2,3},{3,2},{4,5},{5,4},{6,7},{7,6},{8,9},{9,8},{10,11... | collective-permute-start | bytes 196616 | tf_op jit(solution)/shard_map/ppermute | solution.py:415
  14.2 7.7 %collective-permute-start.4 = (f32[32,512]{1,0:T(8,128)S(1)}, f32[32,512]{1,0:T(8,128)S(1)}, u32[]{:S(2)}, u32[]{:S(2)}) collective-permute-start(f32[32,512]{1,0:T(8,128)S(1)} %get-tuple-element.28.rest_0_.rest_4_.pair_ref.xp_ref), channel_id=1, source_target_pairs={{0,2},{1,3},{2,0},{3,1},{4,6},{5,7},{6,4},{7,5},{8,10},{9,11},{10,... | collective-permute-start | bytes 196616 | tf_op jit(solution)/shard_map/ppermute | solution.py:415
  16.8 6.1 %collective-permute-start.5 = (f32[32,512]{1,0:T(8,128)S(1)}, f32[32,512]{1,0:T(8,128)S(1)}, u32[]{:S(2)}, u32[]{:S(2)}) collective-permute-start(f32[32,512]{1,0:T(8,128)S(1)} %get-tuple-element.28.rest_0_.rest_4_.pair_ref.xp_ref), channel_id=1, source_target_pairs={{0,3},{1,2},{2,1},{3,0},{4,7},{5,6},{6,5},{7,4},{8,11},{9,10},{10,... | collective-permute-start | bytes 196616 | tf_op jit(solution)/shard_map/ppermute | solution.py:415
  26.0 1.4 %collective-permute-start.6 = (f32[4,16,512]{2,1,0:T(8,128)S(1)}, f32[4,16,512]{2,1,0:T(8,128)S(1)}, u32[]{:S(2)}, u32[]{:S(2)}) collective-permute-start(f32[4,16,512]{2,1,0:T(8,128)S(1)} %get-tuple-element.30), channel_id=1, source_target_pairs={{0,4},{4,0},{8,12},{12,8},{16,20},{20,16},{24,28},{28,24},{1,5},{5... | collective-permute-start | bytes 393224 | tf_op jit(solution)/shard_map/ppermute | solution.py:415
  26.1 1.3 %collective-permute-start.7 = (f32[8,128]{1,0:T(8,128)S(1)}, f32[8,128]{1,0:T(8,128)S(1)}, u32[]{:S(2)}, u32[]{:S(2)}) collective-permute-start(f32[8,128]{1,0:T(8,128)S(1)} %get-tuple-element.31.extra_ref), channel_id=1, source_target_pairs={{0,4},{4,0},{8,12},{12,8},{16,20},{20,16},{24,28},{28,24},{1,5},{5... | collective-permute-start | bytes 12296 | tf_op jit(solution)/shard_map/ppermute | solution.py:415
  27.4 4.6 %collective-permute-start.8 = (f32[2,8,1152]{2,1,0:T(8,128)S(1)}, f32[2,8,1152]{2,1,0:T(8,128)S(1)}, u32[]{:S(2)}, u32[]{:S(2)}) collective-permute-start(f32[2,8,1152]{2,1,0:T(8,128)S(1)} %get-tuple-element.33), channel_id=1, source_target_pairs={{0,16},{4,20},{8,24},{12,28},{16,0},{20,4},{24,8},{28,12},{1,17},{... | collective-permute-start | bytes 221192 | tf_op jit(solution)/shard_map/ppermute | solution.py:415
  32.0 12.9 %collective-permute-start.9 = (f32[1,8,1152]{2,1,0:T(8,128)S(1)}, f32[1,8,1152]{2,1,0:T(8,128)S(1)}, u32[]{:S(2)}, u32[]{:S(2)}) collective-permute-start(f32[1,8,1152]{2,1,0:T(8,128)S(1)} %get-tuple-element.35), channel_id=1, source_target_pairs={{0,8},{4,12},{8,0},{12,4},{16,24},{20,28},{24,16},{28,20},{1,9},{5... | collective-permute-start | bytes 110600 | tf_op jit(solution)/shard_map/ppermute | solution.py:415
  36.1 4.5 %collective-permute-start.10 = (f32[16,512]{1,0:T(8,128)S(1)}, f32[16,512]{1,0:T(8,128)S(1)}, u32[]{:S(2)}, u32[]{:S(2)}) collective-permute-start(f32[16,512]{1,0:T(8,128)S(1)} %get-tuple-element.37), channel_id=1, source_target_pairs={{0,1},{1,0},{2,3},{3,2},{4,5},{5,4},{6,7},{7,6},{8,9},{9,8},{10,11... | collective-permute-start | bytes 98312 | tf_op jit(solution)/shard_map/ppermute | solution.py:415
  37.4 5.5 %collective-permute-start.11 = (f32[16,512]{1,0:T(8,128)S(1)}, f32[16,512]{1,0:T(8,128)S(1)}, u32[]{:S(2)}, u32[]{:S(2)}) collective-permute-start(f32[16,512]{1,0:T(8,128)S(1)} %get-tuple-element.38), channel_id=1, source_target_pairs={{0,2},{1,3},{2,0},{3,1},{4,6},{5,7},{6,4},{7,5},{8,10},{9,11},{10,... | collective-permute-start | bytes 98312 | tf_op jit(solution)/shard_map/ppermute | solution.py:415
  39.2 5.7 %collective-permute-start.12 = (f32[16,512]{1,0:T(8,128)S(1)}, f32[16,512]{1,0:T(8,128)S(1)}, u32[]{:S(2)}, u32[]{:S(2)}) collective-permute-start(f32[16,512]{1,0:T(8,128)S(1)} %get-tuple-element.39), channel_id=1, source_target_pairs={{0,3},{1,2},{2,1},{3,0},{4,7},{5,6},{6,5},{7,4},{8,11},{9,10},{10,... | collective-permute-start | bytes 98312 | tf_op jit(solution)/shard_map/ppermute | solution.py:415
  44.9 4.0 %collective-permute-start.16 = (f32[1,16,512]{2,1,0:T(8,128)S(1)}, f32[1,16,512]{2,1,0:T(8,128)S(1)}, u32[]{:S(2)}, u32[]{:S(2)}) collective-permute-start(f32[1,16,512]{2,1,0:T(8,128)S(1)} %bitcast.7), channel_id=1, source_target_pairs={{0,8},{4,12},{8,0},{12,4},{16,24},{20,28},{24,16},{28,20},{1,9},{5... | collective-permute-start | bytes 98312 | tf_op jit(solution)/shard_map/ppermute | solution.py:415
  48.9 4.3 %collective-permute-start.17 = (f32[2,16,512]{2,1,0:T(8,128)S(1)}, f32[2,16,512]{2,1,0:T(8,128)S(1)}, u32[]{:S(2)}, u32[]{:S(2)}) collective-permute-start(f32[2,16,512]{2,1,0:T(8,128)S(1)} %pad_maximum_fusion.3), channel_id=1, source_target_pairs={{0,16},{4,20},{8,24},{12,28},{16,0},{20,4},{24,8},{28,12},{1,17},{... | collective-permute-start | bytes 196616 | tf_op jit(solution)/shard_map/ppermute | solution.py:415
  53.2 12.7 %collective-permute-start.18 = (f32[4,16,512]{2,1,0:T(8,128)S(1)}, f32[4,16,512]{2,1,0:T(8,128)S(1)}, u32[]{:S(2)}, u32[]{:S(2)}) collective-permute-start(f32[4,16,512]{2,1,0:T(8,128)S(1)} %pad_maximum_fusion.2.yeven_ref), channel_id=1, source_target_pairs={{0,4},{4,0},{8,12},{12,8},{16,20},{20,16},{24,28},{28,24},{1,5},{5... | collective-permute-start | bytes 393224 | tf_op jit(solution)/shard_map/ppermute | solution.py:415
  53.2 4.5 %collective-permute-start.13 = (f32[8,1152]{1,0:T(8,128)S(1)}, f32[8,1152]{1,0:T(8,128)S(1)}, u32[]{:S(2)}, u32[]{:S(2)}) collective-permute-start(f32[8,1152]{1,0:T(8,128)S(1)} %get-tuple-element.40.rest_0_), channel_id=1, source_target_pairs={{0,1},{1,0},{2,3},{3,2},{4,5},{5,4},{6,7},{7,6},{8,9},{9,8},{10,11... | collective-permute-start | bytes 110600 | tf_op jit(solution)/shard_map/ppermute | solution.py:415
  53.3 5.1 %collective-permute-start.14 = (f32[8,1152]{1,0:T(8,128)S(1)}, f32[8,1152]{1,0:T(8,128)S(1)}, u32[]{:S(2)}, u32[]{:S(2)}) collective-permute-start(f32[8,1152]{1,0:T(8,128)S(1)} %get-tuple-element.40.rest_0_), channel_id=1, source_target_pairs={{0,2},{1,3},{2,0},{3,1},{4,6},{5,7},{6,4},{7,5},{8,10},{9,11},{10,... | collective-permute-start | bytes 110600 | tf_op jit(solution)/shard_map/ppermute | solution.py:415
  55.3 5.8 %collective-permute-start.15 = (f32[8,1152]{1,0:T(8,128)S(1)}, f32[8,1152]{1,0:T(8,128)S(1)}, u32[]{:S(2)}, u32[]{:S(2)}) collective-permute-start(f32[8,1152]{1,0:T(8,128)S(1)} %get-tuple-element.40.rest_0_), channel_id=1, source_target_pairs={{0,3},{1,2},{2,1},{3,0},{4,7},{5,6},{6,5},{7,4},{8,11},{9,10},{10,... | collective-permute-start | bytes 110600 | tf_op jit(solution)/shard_map/ppermute | solution.py:415

commit v4 on v3

--- a/solution.py
+++ b/solution.py
@@ -13,7 +13,6 @@
 f32 = jnp.float32
 bf16 = jnp.bfloat16
 VMEM = pltpu.MemorySpace.VMEM
-HBM = pltpu.MemorySpace.HBM
 SMEM = pltpu.MemorySpace.SMEM
 LANES = 128
 VMEM_LIMIT = 16 * 1024 * 1024
@@ -55,6 +54,14 @@
     n = a.shape[0]
     top = dot(jnp.concatenate([a_hi, a_lo], axis=0), b_hi, None)
     return top[:n] + top[n:] + dot(a_hi, b_lo, None)
+
+
+def four_pass(dot, a, b):
+    b_hi, b_lo = split(b)
+    n = a.shape[0]
+    both = split_rows(a)
+    top, low = dot(both, b_hi, None), dot(both, b_lo, None)
+    return top[:n] + (top[n:] + low[:n] + low[n:])
 
 
 def eye(n):
@@ -97,32 +104,31 @@
     return (lax.div(span, row_count) ^ me_col) * per_span + lax.rem(g, per_span)
 
 
-def load_kernel(x_hbm, p_hbm, cols_hbm, live_hbm, pair_ref, cols_ref, live_ref, sems):
-    w = x_hbm.shape[0]
-    copies = [
-        pltpu.make_async_copy(x_hbm, pair_ref.at[:w], sems.at[0]),
-        pltpu.make_async_copy(p_hbm, pair_ref.at[w:], sems.at[1]),
-        pltpu.make_async_copy(cols_hbm, cols_ref, sems.at[2]),
-        pltpu.make_async_copy(live_hbm, live_ref, sems.at[3]),
-    ]
-    for copy in copies:
-        copy.start()
-    for copy in copies:
-        copy.wait()
+def mark_kernel(mark_ref):
+    mark_ref[...] = jnp.zeros_like(mark_ref)
+
+
+def stack_kernel(*refs):
+    out_ref, at = refs[-1], 0
+    for ref in refs[:-2]:
+        array = ref[...]
+        n = array.shape[0] if array.ndim == 3 else 1
+        out_ref[at : at + n] = array.reshape((n,) + array.shape[-2:])
+        at += n
 
 
 def forward_kernel(sizes, cols_ref, live_ref, even_ref, odd_ref, *rest):
     row_count, col_count, _, width, bs = sizes
     x_refs = rest[:col_count]
-    blocks_ref, keep_ref, send_ref, extra_ref, picks = rest[col_count:]
+    p_ref, blocks_ref, keep_ref, send_ref, extra_ref, picks = rest[col_count:]
     per_span = keep_ref.shape[2] // bs
     me_col = lax.axis_index("col")
     me_row = lax.axis_index("row")
     for s in range(col_count):
         for o in range(per_span):
-            picks[s * per_span + o] = split_rows(x_refs[s][:width, o * bs : (o + 1) * bs])
-    pair = x_refs[0][...]
-    gram = dot_nt(pair, pair)
+            picks[s * per_span + o] = split_rows(x_refs[s][:, o * bs : (o + 1) * bs])
+    pair = jnp.concatenate([x_refs[0][...], p_ref[...]], axis=0)
+    gram = four_pass(dot_nt, pair, pair)
 
     def two_spans(h, cross):
         for i, (out_ref, rows_ref) in enumerate(((keep_ref, even_ref), (send_ref, odd_ref))):
@@ -130,7 +136,7 @@
                 sizes, 2 * h + i, cols_ref, live_ref, picks, blocks_ref, per_span, me_row, me_col
             )
             out_ref[h] = forward
-            cross = cross + three_pass(dot_nt, rows_ref[h, :width, :], forward)
+            cross = cross + three_pass(dot_nt, rows_ref[h], forward)
         return cross
 
     cross = lax.fori_loop(0, row_count // 2, two_spans, jnp.zeros((width, width), f32))
@@ -163,7 +169,7 @@
     me_row = lax.axis_index("row")
 
     def one_span(h, carry):
-        own = split_rows(rows_ref[h, :width, :])
+        own = split_rows(rows_ref[h])
         for o in range(per_span):
             b = (me_row ^ (2 * h + parity)) * per_span + o
             tile = jnp.concatenate([blocks_ref[b, k] for k in range(slots)], axis=1)
@@ -183,15 +189,16 @@
     backward_spans(sizes, 0, cols_ref, live_ref, even_ref, blocks_ref, spread_ref)
 
 
-def back_odd_kernel(sizes, cols_ref, live_ref, odd_ref, blocks_ref, begun_ref, *rest):
-    bs = sizes[4]
+def back_odd_kernel(sizes, cols_ref, live_ref, odd_ref, blocks_ref, begun_ref, p_ref, *rest):
+    width, bs = sizes[3:]
     out_refs, spread = rest[:-1], rest[-1]
     spread[...] = begun_ref[...]
     backward_spans(sizes, 1, cols_ref, live_ref, odd_ref, blocks_ref, spread)
     per_span = odd_ref.shape[2] // bs
     for s, out_ref in enumerate(out_refs):
         for o in range(per_span):
-            out_ref[:, o * bs : (o + 1) * bs] = spread[s * per_span + o]
+            out_ref[:width, o * bs : (o + 1) * bs] = spread[s * per_span + o]
+        out_ref[width:] = p_ref[...]
 
 
 def put(ref, vectors, extra):
@@ -229,9 +236,11 @@
 def middle_kernel(col_count, keep_ref, got_ref, *refs):
     back_refs = refs[:col_count]
     out_ref, y_ref = refs[col_count:]
+    width = y_ref.shape[0] // 2
     forward, sums = take(keep_ref[0] + got_ref[0])
-    y = 0.5 * (forward + tree_sum([ref[...] for ref in back_refs]))
-    y_ref[...] = y
+    y = 0.5 * (forward + tree_sum([ref[:width] for ref in back_refs]))
+    y_ref[:width] = y
+    y_ref[width:] = back_refs[0][width:]
     put(out_ref, y, sums)
 
 
@@ -257,19 +266,19 @@
 
 def forward_rest_kernel(sizes, cols_ref, live_ref, aux_ref, *rest):
     row_count, col_count, _, width, bs = sizes
-    y_refs, x_refs = (rest[i * col_count : (i + 1) * col_count] for i in range(2))
-    blocks_ref, out_ref, resid_ref, resid_out_ref, picks = rest[2 * col_count :]
+    y_refs, x_refs, p_refs = (rest[i * col_count : (i + 1) * col_count] for i in range(3))
+    blocks_ref, out_ref, resid_ref, resid_out_ref, picks = rest[3 * col_count :]
     span_rows = out_ref.shape[2]
     per_span = span_rows // bs
     me_col = lax.axis_index("col")
     me_row = lax.axis_index("row")
     minus_c_t = aux_ref[:, :width]
     for s in range(col_count):
-        rest_s = take(y_refs[s][...])[0] + dot_nn(minus_c_t, x_refs[s][:width])
+        rest_s = take(y_refs[s][...])[0] + dot_nn(minus_c_t, x_refs[s][...])
         if s == 0:
             resid_ref[...] = rest_s
             resid_out_ref[...] = rest_s
-        both = jnp.concatenate([rest_s, x_refs[s][width:]], axis=0)
+        both = jnp.concatenate([rest_s, p_refs[s][width:]], axis=0)
         for o in range(per_span):
             picks[s * per_span + o] = split_rows(both[:, o * bs : (o + 1) * bs])
 
@@ -298,23 +307,32 @@
     return jnp.concatenate([packed[:, at : at + w], packed[:, at + w : at + 2 * w]], axis=0)
 
 
-def gram_kernel(
-    width, half, aux_ref, even_ref, odd_ref, yeven_ref, yodd_ref, forward_ref, pair_ref,
-    resid_ref, part_ref,
-):
+def gram_spans(width, parity, aux_ref, x_ref, y_ref, forward_ref):
     w = width
     minus_c_t = aux_ref[:, :w]
 
-    def two_spans(h, cross):
-        for i, (rows_ref, y_ref) in enumerate(((even_ref, yeven_ref), (odd_ref, yodd_ref))):
-            rest_q = y_ref[h] + three_pass(dot_nn, minus_c_t, rows_ref[h, :w, :])
-            both = jnp.concatenate([rest_q, rows_ref[h, w:, :]], axis=0)
-            cross = cross + three_pass(dot_nt, both, forward_ref[2 * h + i])
+    def two_spans(i, cross):
+        for h in (2 * i, 2 * i + 1):
+            rest_q = y_ref[h, :w, :] + three_pass(dot_nn, minus_c_t, x_ref[h])
+            both = jnp.concatenate([rest_q, y_ref[h, w:, :]], axis=0)
+            cross = cross + three_pass(dot_nt, both, forward_ref[2 * h + parity])
         return cross
 
+    return lax.fori_loop(0, x_ref.shape[0] // 2, two_spans, jnp.zeros((2 * w, 2 * w), f32))
+
+
+def gram_even_kernel(
+    width, aux_ref, x_ref, y_ref, forward_ref, p_ref, resid_ref, cross_ref, gram_ref
+):
     mine = resid_ref[...]
-    gram = dot_nt(mine, jnp.concatenate([mine, pair_ref[w:]], axis=0))
-    cross = lax.fori_loop(0, half, two_spans, jnp.zeros((2 * w, 2 * w), f32))
+    gram_ref[...] = four_pass(dot_nt, mine, jnp.concatenate([mine, p_ref[...]], axis=0))
+    cross_ref[...] = gram_spans(width, 0, aux_ref, x_ref, y_ref, forward_ref)
+
+
+def gram_odd_kernel(width, aux_ref, x_ref, y_ref, forward_ref, cross_ref, gram_ref, part_ref):
+    w = width
+    gram = gram_ref[...]
+    cross = cross_ref[...] + gram_spans(w, 1, aux_ref, x_ref, y_ref, forward_ref)
     rar, pap = cross[:w, :w], cross[w:, w:]
     rar = 0.5 * (rar + rar.T)
     pap = 0.5 * (pap + pap.T)
@@ -330,7 +348,7 @@
 
 
 def last_kernel(
-    width, scale, parts_ref, aux_ref, wide_ref, xp_ref, resid_ref, x_next_ref, reduced_ref
+    width, scale, parts_ref, aux_ref, wide_ref, x_ref, yp_ref, resid_ref, x_next_ref, reduced_ref
 ):
     w = width
     total = parts_ref[0]
@@ -378,7 +396,7 @@
     gram_fresh = dot_tn(target, target)
     mixing = dot_tn(target, inverse_l)
     weights = scale * eliminate(jnp.concatenate([gram_fresh, mixing], axis=1), w)[:, w:]
-    basis = jnp.concatenate([xp_ref[:w, :], resid_ref[...], xp_ref[w:, :]], axis=0)
+    basis = jnp.concatenate([x_ref[0], resid_ref[...], yp_ref[w:, :]], axis=0)
     x_next_ref[...] = dot_nn(weights, basis)
 
 
@@ -386,18 +404,16 @@
     row_count = lax.axis_size("row")
     col_count = lax.axis_size("col")
     width, span_rows = block_vecs.shape
-    block_rows, slots, bs = blocks.shape[:3]
+    slots, bs = blocks.shape[1:3]
     per_span = span_rows // bs
     half = row_count // 2
     order_total = span_rows * row_count * col_count
     col_blocks = col_count * per_span
     sizes = (row_count, col_count, slots, width, bs)
     shape = lambda *dims: jax.ShapeDtypeStruct(dims, f32)
-    in_hbm = lambda array: pltpu.with_memory_space_constraint(array, HBM)
     spec = {
         "v": pl.BlockSpec(memory_space=VMEM),
         "s": pl.BlockSpec(memory_space=SMEM),
-        "h": pl.BlockSpec(memory_space=HBM),
     }
 
     def call(kernel, ins, args, outs, scratch=(), cost=None):
@@ -416,49 +432,40 @@
 
     far = list(reversed(range(1, col_count)))
     bits = row_bits(row_count)
+    window = pl.CostEstimate(flops=LOAD_FLOPS, bytes_accessed=0, transcendentals=0)
 
     def gather_rows(array):
-        even = array[None]
+        even = array
         for bit in bits:
             got = swap(even, "row", bit)
-            even = jnp.concatenate([even, got], axis=0)
+            (even,) = call(stack_kernel, "vvv", [even, got, mark], [shape(bit, *array.shape)])
         return even, swap(even, "row", 1)
 
     def over_col(arrays):
         got = {s: swap(arrays[s], "col", s) for s in far}
         return [arrays[0]] + [got[s] for s in range(1, col_count)]
 
-    pair, cols, live = call(
-        load_kernel,
-        "hhhh",
-        [in_hbm(a) for a in (block_vecs, direction, block_cols.T, live_counts.T)],
-        [
-            shape(2 * width, span_rows),
-            jax.ShapeDtypeStruct((slots, block_rows), jnp.int32),
-            jax.ShapeDtypeStruct((1, block_rows), jnp.int32),
-        ],
-        [pltpu.SemaphoreType.DMA((4,))],
-        pl.CostEstimate(flops=LOAD_FLOPS, bytes_accessed=0, transcendentals=0),
-    )
-    pair_cols = over_col([pair] * col_count)
-    pair_even, pair_odd = gather_rows(pair)
+    (mark,) = call(mark_kernel, "", [], [shape(8, LANES)], cost=window)
+    cols, live = block_cols.T, live_counts.T
+    x_cols = over_col([block_vecs] * col_count)
+    x_even, x_odd = gather_rows(block_vecs)
     (begun,) = call(
         functools.partial(back_even_kernel, sizes),
         "ssvv",
-        [cols, live, pair_even, blocks],
+        [cols, live, x_even, blocks],
         [shape(col_blocks, width, bs)],
     )
     backs = call(
         functools.partial(back_odd_kernel, sizes),
-        "ssvvv",
-        [cols, live, pair_odd, blocks, begun],
-        [shape(width, span_rows)] * col_count,
+        "ssvvvv",
+        [cols, live, x_odd, blocks, begun, direction],
+        [shape(2 * width, span_rows)] * col_count,
         [pltpu.VMEM((col_blocks, width, bs), f32)],
     )
     keep, send, extra = call(
         functools.partial(forward_kernel, sizes),
-        "ssvv" + "v" * (col_count + 1),
-        [cols, live, pair_even, pair_odd, *pair_cols, blocks],
+        "ssvv" + "v" * (col_count + 2),
+        [cols, live, x_even, x_odd, *x_cols, direction, blocks],
         [shape(half, width, span_rows)] * 2 + [shape(width // 2, LANES)],
         [pltpu.VMEM((col_blocks, 2 * width, bs), bf16)],
     )
@@ -484,7 +491,7 @@
         functools.partial(middle_kernel, col_count),
         "v" * (2 + col_count),
         [low, got, *got_backs],
-        [shape(width // 2, 2 * span_rows + LANES), shape(width, span_rows)],
+        [shape(width // 2, 2 * span_rows + LANES), shape(2 * width, span_rows)],
     )
     image_cols = over_col([message] * col_count)
     image_even, image_odd = gather_rows(image)
@@ -496,22 +503,28 @@
     )
     forward_rp, resid, resid_out = call(
         functools.partial(forward_rest_kernel, sizes),
-        "ssv" + "v" * (2 * col_count + 1),
-        [cols, live, aux, *image_cols, *pair_cols, blocks],
+        "ssv" + "v" * (3 * col_count + 1),
+        [cols, live, aux, *image_cols, *x_cols, *got_backs, blocks],
         [shape(row_count, 2 * width, span_rows)] + [shape(width, span_rows)] * 2,
         [pltpu.VMEM((col_blocks, 4 * width, bs), bf16)],
     )
+    cross, gram = call(
+        functools.partial(gram_even_kernel, width),
+        "v" * 6,
+        [aux, x_even, image_even, forward_rp, direction, resid],
+        [shape(2 * width, 2 * width), shape(width, 2 * width)],
+    )
     (part,) = call(
-        functools.partial(gram_kernel, width, half),
-        "v" * 8,
-        [aux, pair_even, pair_odd, image_even, image_odd, forward_rp, pair, resid],
+        functools.partial(gram_odd_kernel, width),
+        "v" * 6,
+        [aux, x_odd, image_odd, forward_rp, cross, gram],
         [shape(row_count * col_count, width // 2, LANES)],
     )
     parts = lax.all_to_all(part, ("col", "row"), 0, 0)
     x_next, reduced = call(
         functools.partial(last_kernel, width, math.sqrt(order_total)),
-        "v" * 5,
-        [parts, aux, wide, pair, resid],
+        "v" * 6,
+        [parts, aux, wide, x_even, image, resid],
         [shape(width, span_rows), shape(3 * width, 3 * width)],
     )
     return (x_next, reduced, resid_out)

time: 84.5 us -> 78.8 us (0.933)
  waiting for transfers between devices: 28.8 us -> 24.7 us
  Pallas kernels: 18.3 us -> 17.3 us
    ppermute x19, waiting for transfers between devices: 28.8 us -> 24.7 us  [swap(): lax.ppermute(array, axis, [(i, i ^ s) for i in range(lax.axis_size(axis))])]
    pallas_call x11 -> x16, Pallas kernels: 18.3 us -> 17.3 us  [call(): pl.pallas_call(kernel, in_specs=[spec[letter] for letter in ins], out_spe...]
  transfers between devices with their start and end apart: 19 -> 19, of which waited for: 13 -> 10; matrix products, arithmetic and copies ran while one was open for 0% -> 0% of each run, Pallas kernels for 9% -> 11%
where the time goes in v4:
time: 78.8 us; the launch traced here: 78.6 us
  starting transfers between devices  24.7 us (31%)
  waiting for transfers between devices  24.7 us (31%)
  Pallas kernels  17.3 us (22%)
  blocking collectives  11.1 us (14%)
  between operations  0.79 us (1%)
    ppermute x19, starting transfers between devices, swap(): lax.ppermute(array, axis, [(i, i ^ s) for i in range(lax.axis_size(axis))])  24.7 us
    ppermute x19, waiting for transfers between devices, swap(): lax.ppermute(array, axis, [(i, i ^ s) for i in range(lax.axis_size(axis))])  24.7 us
    pallas_call x16, Pallas kernels, call(): pl.pallas_call(kernel, in_specs=[spec[letter] for letter in ins], out_spe...  17.3 us
    all_to_all x1, blocking collectives, per_device(): parts = lax.all_to_all(part, ('col', 'row'), 0, 0)  11.1 us
  transfers between devices with their start and end apart: 19, of which 10 were waited for; matrix products, arithmetic and copies ran while one was open for 0% of the time, Pallas kernels for 11%

profile of v4, /device:TPU:0, one launch (start us, length us, event | category | flops | bytes accessed | tf_op | source)
XLA Modules:
  0.0 78.6 jit_solution(8106991967196113414)
XLA Ops:
  0.7 3.0 %collective-permute-start = (f32[16,512]{1,0:T(8,128)}, f32[16,512]{1,0:T(8,128)S(1)}, u32[]{:S(2)}, u32[]{:S(2)}) collective-permute-start(f32[16,512]{1,0:T(8,128)} %rest_4_.3), channel_id=1, source_target_pairs={{0,8},{4,12},{8,0},{12,4},{16,24},{20,28},{24,16},{28,20},{1,9},{5... | collective-permute-start | bytes 98312 | tf_op jit(solution)/shard_map/ppermute | solution.py:431
  3.7 2.1 %collective-permute-done.refs_1_ = f32[16,512]{1,0:T(8,128)S(1)} collective-permute-done((f32[16,512]{1,0:T(8,128)}, f32[16,512]{1,0:T(8,128)S(1)}, u32[]{:S(2)}, u32[]{:S(2)}) %collective-permute-start) | collective-permute-done | bytes 32800 | tf_op jit(solution)/shard_map/ppermute | solution.py:431
  5.8 2.1 %collective-permute-start.1 = (f32[2,16,512]{2,1,0:T(8,128)S(1)}, f32[2,16,512]{2,1,0:T(8,128)S(1)}, u32[]{:S(2)}, u32[]{:S(2)}) collective-permute-start(f32[2,16,512]{2,1,0:T(8,128)S(1)} %shard_map.77.refs_0_), channel_id=1, source_target_pairs={{0,16},{4,20},{8,24},{12,28},{16,0},{20,4},{24,8},{28,12},{1,17},{... | collective-permute-start | bytes 196616 | tf_op jit(solution)/shard_map/ppermute | solution.py:431
  7.9 2.2 %collective-permute-done.1.refs_1_ = f32[2,16,512]{2,1,0:T(8,128)S(1)} collective-permute-done((f32[2,16,512]{2,1,0:T(8,128)S(1)}, f32[2,16,512]{2,1,0:T(8,128)S(1)}, u32[]{:S(2)}, u32[]{:S(2)}) %collective-permute-start.1) | collective-permute-done | bytes 65568 | tf_op jit(solution)/shard_map/ppermute | solution.py:431
  10.3 2.1 %collective-permute-start.3 = (f32[16,512]{1,0:T(8,128)S(1)}, f32[16,512]{1,0:T(8,128)S(1)}, u32[]{:S(2)}, u32[]{:S(2)}) collective-permute-start(f32[16,512]{1,0:T(8,128)S(1)} %copy-done.2), channel_id=1, source_target_pairs={{0,1},{1,0},{2,3},{3,2},{4,5},{5,4},{6,7},{7,6},{8,9},{9,8},{10,11... | collective-permute-start | bytes 98312 | tf_op jit(solution)/shard_map/ppermute | solution.py:431
  12.4 2.6 %collective-permute-start.4 = (f32[16,512]{1,0:T(8,128)S(1)}, f32[16,512]{1,0:T(8,128)S(1)}, u32[]{:S(2)}, u32[]{:S(2)}) collective-permute-start(f32[16,512]{1,0:T(8,128)S(1)} %copy-done.2), channel_id=1, source_target_pairs={{0,2},{1,3},{2,0},{3,1},{4,6},{5,7},{6,4},{7,5},{8,10},{9,11},{10,... | collective-permute-start | bytes 98312 | tf_op jit(solution)/shard_map/ppermute | solution.py:431
  15.0 2.8 %collective-permute-done.4.rest_2_.rest_6_ = f32[16,512]{1,0:T(8,128)S(1)} collective-permute-done((f32[16,512]{1,0:T(8,128)S(1)}, f32[16,512]{1,0:T(8,128)S(1)}, u32[]{:S(2)}, u32[]{:S(2)}) %collective-permute-start.4) | collective-permute-done | bytes 32800 | tf_op jit(solution)/shard_map/ppermute | solution.py:431
  17.8 2.9 %collective-permute-done.5.rest_3_.rest_7_ = f32[16,512]{1,0:T(8,128)S(1)} collective-permute-done((f32[16,512]{1,0:T(8,128)S(1)}, f32[16,512]{1,0:T(8,128)S(1)}, u32[]{:S(2)}, u32[]{:S(2)}) %collective-permute-start.5) | collective-permute-done | bytes 32800 | tf_op jit(solution)/shard_map/ppermute | solution.py:431
  20.8 3.1 %shard_map.79 = (f32[4,16,512]{2,1,0:T(8,128)S(1)}, f32[4,16,512]{2,1,0:T(8,128)S(1)}, f32[8,128]{1,0:T(8,128)S(1)}) custom-call(s32[2,32]{1,0:T(2,128)S(1)} %bitcast.2, s32[1,32]{1,0:T(1,128)S(1)} %bitcast.6, f32[4,16,512]{2,1,0:T(8,128)S(1)} %shard_map.78.even_ref.x_ref, f32[4,16,512]{2,1,0:T(8,128)S(1)} %collective-permute-done.2.odd_ref.x_ref, ...), custom_call_target="tpu_custom_call" | custom-call | tf_op jit(solution)/shard_map/pallas_call | solution.py:420
  24.4 0.8 %collective-permute-done.7.got_extra_ref = f32[8,128]{1,0:T(8,128)S(1)} collective-permute-done((f32[8,128]{1,0:T(8,128)S(1)}, f32[8,128]{1,0:T(8,128)S(1)}, u32[]{:S(2)}, u32[]{:S(2)}) %collective-permute-start.7) | collective-permute-done | bytes 4128 | tf_op jit(solution)/shard_map/ppermute | solution.py:431
  25.3 1.6 %collective-permute-start.8 = (f32[2,8,1152]{2,1,0:T(8,128)S(1)}, f32[2,8,1152]{2,1,0:T(8,128)S(1)}, u32[]{:S(2)}, u32[]{:S(2)}) collective-permute-start(f32[2,8,1152]{2,1,0:T(8,128)S(1)} %get-tuple-element.29), channel_id=1, source_target_pairs={{0,16},{4,20},{8,24},{12,28},{16,0},{20,4},{24,8},{28,12},{1,17},{... | collective-permute-start | bytes 221192 | tf_op jit(solution)/shard_map/ppermute | solution.py:431
  26.9 1.3 %shard_map.82.begun_ref = f32[16,16,128]{2,1,0:T(8,128)S(1)} custom-call(s32[2,32]{1,0:T(2,128)S(1)} %bitcast.3, s32[1,32]{1,0:T(1,128)S(1)} %bitcast.7, f32[4,16,512]{2,1,0:T(8,128)S(1)} %shard_map.78.even_ref.x_ref, bf16[32,2,128,128]{3,2,1,0:T(8,128)(2,1)S(1)} %copy-done), custom_call_target="tpu_custom_call" | custom-call | tf_op jit(solution)/shard_map/pallas_call | solution.py:420
  28.2 1.3 %shard_map.83 = (f32[32,512]{1,0:T(8,128)S(1)}, f32[32,512]{1,0:T(8,128)S(1)}, f32[32,512]{1,0:T(8,128)S(1)}, f32[32,512]{1,0:T(8,128)S(1)}) custom-call(s32[2,32]{1,0:T(2,128)S(1)} %bitcast.4, s32[1,32]{1,0:T(1,128)S(1)} %bitcast.8, f32[4,16,512]{2,1,0:T(8,128)S(1)} %collective-permute-done.2.odd_ref.x_ref, bf16[32,2,128,128]{3,2,1,0:T(8,128)(2,1)S(1)} %copy-done, ...), custom_call_target="tpu_custom_call" | custom-call | tf_op jit(solution)/shard_map/pallas_call | solution.py:420
  29.5 1.0 %collective-permute-start.11 = (f32[32,512]{1,0:T(8,128)S(1)}, f32[32,512]{1,0:T(8,128)S(1)}, u32[]{:S(2)}, u32[]{:S(2)}) collective-permute-start(f32[32,512]{1,0:T(8,128)S(1)} %get-tuple-element.34), channel_id=1, source_target_pairs={{0,2},{1,3},{2,0},{3,1},{4,6},{5,7},{6,4},{7,5},{8,10},{9,11},{10,... | collective-permute-start | bytes 196616 | tf_op jit(solution)/shard_map/ppermute | solution.py:431
  30.5 3.4 %collective-permute-start.12 = (f32[32,512]{1,0:T(8,128)S(1)}, f32[32,512]{1,0:T(8,128)S(1)}, u32[]{:S(2)}, u32[]{:S(2)}) collective-permute-start(f32[32,512]{1,0:T(8,128)S(1)} %get-tuple-element.35), channel_id=1, source_target_pairs={{0,3},{1,2},{2,1},{3,0},{4,7},{5,6},{6,5},{7,4},{8,11},{9,10},{10,... | collective-permute-start | bytes 196616 | tf_op jit(solution)/shard_map/ppermute | solution.py:431
  33.9 1.6 %collective-permute-start.9 = (f32[1,8,1152]{2,1,0:T(8,128)S(1)}, f32[1,8,1152]{2,1,0:T(8,128)S(1)}, u32[]{:S(2)}, u32[]{:S(2)}) collective-permute-start(f32[1,8,1152]{2,1,0:T(8,128)S(1)} %get-tuple-element.31), channel_id=1, source_target_pairs={{0,8},{4,12},{8,0},{12,4},{16,24},{20,28},{24,16},{28,20},{1,9},{5... | collective-permute-start | bytes 110600 | tf_op jit(solution)/shard_map/ppermute | solution.py:431
  35.5 2.6 %collective-permute-done.11.refs_2_.rest_10_ = f32[32,512]{1,0:T(8,128)S(1)} collective-permute-done((f32[32,512]{1,0:T(8,128)S(1)}, f32[32,512]{1,0:T(8,128)S(1)}, u32[]{:S(2)}, u32[]{:S(2)}) %collective-permute-start.11) | collective-permute-done | bytes 65568 | tf_op jit(solution)/shard_map/ppermute | solution.py:431
  38.1 1.6 %collective-permute-start.16 = (f32[32,512]{1,0:T(8,128)S(1)}, f32[32,512]{1,0:T(8,128)S(1)}, u32[]{:S(2)}, u32[]{:S(2)}) collective-permute-start(f32[32,512]{1,0:T(8,128)S(1)} %get-tuple-element.38.refs_0_.yp_ref), channel_id=1, source_target_pairs={{0,8},{4,12},{8,0},{12,4},{16,24},{20,28},{24,16},{28,20},{1,9},{5... | collective-permute-start | bytes 196616 | tf_op jit(solution)/shard_map/ppermute | solution.py:431
  39.6 2.8 %collective-permute-done.16.refs_1_ = f32[32,512]{1,0:T(8,128)S(1)} collective-permute-done((f32[32,512]{1,0:T(8,128)S(1)}, f32[32,512]{1,0:T(8,128)S(1)}, u32[]{:S(2)}, u32[]{:S(2)}) %collective-permute-start.16) | collective-permute-done | bytes 65568 | tf_op jit(solution)/shard_map/ppermute | solution.py:431
  42.4 0.6 collective-permute-start.17
  43.0 4.5 %collective-permute-done.17.refs_1_ = f32[2,32,512]{2,1,0:T(8,128)S(1)} collective-permute-done((f32[2,32,512]{2,1,0:T(8,128)S(1)}, f32[2,32,512]{2,1,0:T(8,128)S(1)}, u32[]{:S(2)}, u32[]{:S(2)}) %collective-permute-start.17) | collective-permute-done | bytes 131104 | tf_op jit(solution)/shard_map/ppermute | solution.py:431
  47.6 1.3 %collective-permute-start.13 = (f32[8,1152]{1,0:T(8,128)S(1)}, f32[8,1152]{1,0:T(8,128)S(1)}, u32[]{:S(2)}, u32[]{:S(2)}) collective-permute-start(f32[8,1152]{1,0:T(8,128)S(1)} %get-tuple-element.36.rest_0_), channel_id=1, source_target_pairs={{0,1},{1,0},{2,3},{3,2},{4,5},{5,4},{6,7},{7,6},{8,9},{9,8},{10,11... | collective-permute-start | bytes 110600 | tf_op jit(solution)/shard_map/ppermute | solution.py:431
  48.9 1.3 %collective-permute-start.14 = (f32[8,1152]{1,0:T(8,128)S(1)}, f32[8,1152]{1,0:T(8,128)S(1)}, u32[]{:S(2)}, u32[]{:S(2)}) collective-permute-start(f32[8,1152]{1,0:T(8,128)S(1)} %get-tuple-element.36.rest_0_), channel_id=1, source_target_pairs={{0,2},{1,3},{2,0},{3,1},{4,6},{5,7},{6,4},{7,5},{8,10},{9,11},{10,... | collective-permute-start | bytes 110600 | tf_op jit(solution)/shard_map/ppermute | solution.py:431
  50.2 1.8 %collective-permute-start.15 = (f32[8,1152]{1,0:T(8,128)S(1)}, f32[8,1152]{1,0:T(8,128)S(1)}, u32[]{:S(2)}, u32[]{:S(2)}) collective-permute-start(f32[8,1152]{1,0:T(8,128)S(1)} %get-tuple-element.36.rest_0_), channel_id=1, source_target_pairs={{0,3},{1,2},{2,1},{3,0},{4,7},{5,6},{6,5},{7,4},{8,11},{9,10},{10,... | collective-permute-start | bytes 110600 | tf_op jit(solution)/shard_map/ppermute | solution.py:431
  52.0 2.5 %collective-permute-done.14.rest_2_ = f32[8,1152]{1,0:T(8,128)S(1)} collective-permute-done((f32[8,1152]{1,0:T(8,128)S(1)}, f32[8,1152]{1,0:T(8,128)S(1)}, u32[]{:S(2)}, u32[]{:S(2)}) %collective-permute-start.14) | collective-permute-done | bytes 36896 | tf_op jit(solution)/shard_map/ppermute | solution.py:431
  54.5 1.4 %collective-permute-done.15.rest_3_ = f32[8,1152]{1,0:T(8,128)S(1)} collective-permute-done((f32[8,1152]{1,0:T(8,128)S(1)}, f32[8,1152]{1,0:T(8,128)S(1)}, u32[]{:S(2)}, u32[]{:S(2)}) %collective-permute-start.15) | collective-permute-done | bytes 36896 | tf_op jit(solution)/shard_map/ppermute | solution.py:431
  56.0 2.1 %shard_map.85 = (f32[16,128]{1,0:T(8,128)S(1)}, f32[32,64]{1,0:T(8,128)S(1)}) custom-call(f32[8,1152]{1,0:T(8,128)S(1)} %get-tuple-element.36.rest_0_, f32[8,1152]{1,0:T(8,128)S(1)} %collective-permute-done.13.rest_1_, f32[8,1152]{1,0:T(8,128)S(1)} %collective-permute-done.14.rest_2_, f32[8,1152]{1,0:T(8,128)S(1)} %collective-permute-done.15.rest_3_), custom_call_target="tpu_custom_call" | custom-call | tf_op jit(solution)/shard_map/pallas_call | solution.py:420
  58.1 2.7 %shard_map.88 = (f32[8,32,512]{2,1,0:T(8,128)S(1)}, f32[16,512]{1,0:T(8,128)S(1)}, f32[16,512]{1,0:T(8,128)}) custom-call(s32[2,32]{1,0:T(2,128)S(1)} %bitcast.5, s32[1,32]{1,0:T(1,128)S(1)} %bitcast.9, f32[16,128]{1,0:T(8,128)S(1)} %get-tuple-element.37.aux_ref, f32[8,1152]{1,0:T(8,128)S(1)} %get-tuple-element.36.rest_0_, ...), custom_call_target="tpu_custom_call" | custom-call | tf_op jit(solution)/shard_map/pallas_call | solution.py:420
  60.7 1.1 %shard_map.89 = (f32[32,32]{1,0:T(8,128)S(1)}, f32[16,32]{1,0:T(8,128)S(1)}) custom-call(f32[16,128]{1,0:T(8,128)S(1)} %get-tuple-element.37.aux_ref, f32[4,16,512]{2,1,0:T(8,128)S(1)} %shard_map.78.even_ref.x_ref, f32[4,32,512]{2,1,0:T(8,128)S(1)} %shard_map.87.y_ref, f32[8,32,512]{2,1,0:T(8,128)S(1)} %get-tuple-element.39.forward_ref, ...), custom_call_target="tpu_custom_call" | custom-call | tf_op jit(solution)/shard_map/pallas_call | solution.py:420
  61.8 1.4 %shard_map.90 = f32[32,8,128]{2,1,0:T(8,128)S(1)} custom-call(f32[16,128]{1,0:T(8,128)S(1)} %get-tuple-element.37.aux_ref, f32[4,16,512]{2,1,0:T(8,128)S(1)} %collective-permute-done.2.odd_ref.x_ref, f32[4,32,512]{2,1,0:T(8,128)S(1)} %collective-permute-done.18.y_ref, f32[8,32,512]{2,1,0:T(8,128)S(1)} %get-tuple-element.39.forward_ref, ...), custom_call_target="tpu_custom_call" | custom-call | tf_op jit(solution)/shard_map/pallas_call | solution.py:420
  63.3 11.1 %all_to_all.5.parts_ref = f32[32,8,128]{2,1,0:T(8,128)S(1)} all-to-all(f32[32,8,128]{2,1,0:T(8,128)S(1)} %shard_map.90), channel_id=1, replica_groups=mesh['row'=8,'col'=4] {'col','row'}, dimensions={0} | all-to-all | bytes 262144 | tf_op jit(solution)/shard_map/all_to_all | solution.py:523
  74.4 4.3 %shard_map.91 = (f32[16,512]{1,0:T(8,128)}, f32[48,48]{1,0:T(8,128)}) custom-call(f32[32,8,128]{2,1,0:T(8,128)S(1)} %all_to_all.5.parts_ref, f32[16,128]{1,0:T(8,128)S(1)} %get-tuple-element.37.aux_ref, f32[32,64]{1,0:T(8,128)S(1)} %get-tuple-element.43.wide_ref, f32[4,16,512]{2,1,0:T(8,128)S(1)} %shard_map.78.even_ref.x_ref, ...), custom_call_target="tpu_custom_call" | custom-call | tf_op jit(solution)/shard_map/pallas_call | solution.py:420
  (33 shorter events, 0.9 us)
Async XLA Ops:
  0.6 5.2 %copy-start.2 = (f32[16,512]{1,0:T(8,128)S(1)}, f32[16,512]{1,0:T(8,128)}, u32[]{:S(2)}) copy-start(f32[16,512]{1,0:T(8,128)} %rest_4_.3) | copy-start | bytes 98308
  0.6 20.1 %copy-start.3 = (s32[32,2]{0,1:T(2,128)S(1)}, s32[32,2]{0,1:T(2,128)}, u32[]{:S(2)}) copy-start(s32[32,2]{0,1:T(2,128)} %param.8) | copy-start | bytes 772
  0.7 20.1 %copy-start.4 = (s32[32,1]{0,1:T(1,128)S(1)}, s32[32,1]{0,1:T(1,128)}, u32[]{:S(2)}) copy-start(s32[32,1]{0,1:T(1,128)} %param.9) | copy-start | bytes 388
  0.7 20.1 %copy-start.1 = (f32[16,512]{1,0:T(8,128)S(1)}, f32[16,512]{1,0:T(8,128)}, u32[]{:S(2)}) copy-start(f32[16,512]{1,0:T(8,128)} %p_ref.3) | copy-start | bytes 98308
  0.7 20.1 %copy-start = (bf16[32,2,128,128]{3,2,1,0:T(8,128)(2,1)S(1)}, bf16[32,2,128,128]{3,2,1,0:T(8,128)(2,1)}, u32[]{:S(2)}) copy-start(bf16[32,2,128,128]{3,2,1,0:T(8,128)(2,1)} %rest_12_.1) | copy-start | bytes 6291460
  0.7 5.1 %collective-permute-start = (f32[16,512]{1,0:T(8,128)}, f32[16,512]{1,0:T(8,128)S(1)}, u32[]{:S(2)}, u32[]{:S(2)}) collective-permute-start(f32[16,512]{1,0:T(8,128)} %rest_4_.3), channel_id=1, source_target_pairs={{0,8},{4,12},{8,0},{12,4},{16,24},{20,28},{24,16},{28,20},{1,9},{5... | collective-permute-start | bytes 98312 | tf_op jit(solution)/shard_map/ppermute | solution.py:431
  5.8 4.4 %collective-permute-start.1 = (f32[2,16,512]{2,1,0:T(8,128)S(1)}, f32[2,16,512]{2,1,0:T(8,128)S(1)}, u32[]{:S(2)}, u32[]{:S(2)}) collective-permute-start(f32[2,16,512]{2,1,0:T(8,128)S(1)} %shard_map.77.refs_0_), channel_id=1, source_target_pairs={{0,16},{4,20},{8,24},{12,28},{16,0},{20,4},{24,8},{28,12},{1,17},{... | collective-permute-start | bytes 196616 | tf_op jit(solution)/shard_map/ppermute | solution.py:431
  10.2 10.5 %collective-permute-start.2 = (f32[4,16,512]{2,1,0:T(8,128)S(1)}, f32[4,16,512]{2,1,0:T(8,128)S(1)}, u32[]{:S(2)}, u32[]{:S(2)}) collective-permute-start(f32[4,16,512]{2,1,0:T(8,128)S(1)} %shard_map.78.even_ref.x_ref), channel_id=1, source_target_pairs={{0,4},{4,0},{8,12},{12,8},{16,20},{20,16},{24,28},{28,24},{1,5},{5... | collective-permute-start | bytes 393224 | tf_op jit(solution)/shard_map/ppermute | solution.py:431
  10.3 4.7 %collective-permute-start.3 = (f32[16,512]{1,0:T(8,128)S(1)}, f32[16,512]{1,0:T(8,128)S(1)}, u32[]{:S(2)}, u32[]{:S(2)}) collective-permute-start(f32[16,512]{1,0:T(8,128)S(1)} %copy-done.2), channel_id=1, source_target_pairs={{0,1},{1,0},{2,3},{3,2},{4,5},{5,4},{6,7},{7,6},{8,9},{9,8},{10,11... | collective-permute-start | bytes 98312 | tf_op jit(solution)/shard_map/ppermute | solution.py:431
  12.4 5.4 %collective-permute-start.4 = (f32[16,512]{1,0:T(8,128)S(1)}, f32[16,512]{1,0:T(8,128)S(1)}, u32[]{:S(2)}, u32[]{:S(2)}) collective-permute-start(f32[16,512]{1,0:T(8,128)S(1)} %copy-done.2), channel_id=1, source_target_pairs={{0,2},{1,3},{2,0},{3,1},{4,6},{5,7},{6,4},{7,5},{8,10},{9,11},{10,... | collective-permute-start | bytes 98312 | tf_op jit(solution)/shard_map/ppermute | solution.py:431
  15.0 5.7 %collective-permute-start.5 = (f32[16,512]{1,0:T(8,128)S(1)}, f32[16,512]{1,0:T(8,128)S(1)}, u32[]{:S(2)}, u32[]{:S(2)}) collective-permute-start(f32[16,512]{1,0:T(8,128)S(1)} %copy-done.2), channel_id=1, source_target_pairs={{0,3},{1,2},{2,1},{3,0},{4,7},{5,6},{6,5},{7,4},{8,11},{9,10},{10,... | collective-permute-start | bytes 98312 | tf_op jit(solution)/shard_map/ppermute | solution.py:431
  23.9 1.4 %collective-permute-start.6 = (f32[4,16,512]{2,1,0:T(8,128)S(1)}, f32[4,16,512]{2,1,0:T(8,128)S(1)}, u32[]{:S(2)}, u32[]{:S(2)}) collective-permute-start(f32[4,16,512]{2,1,0:T(8,128)S(1)} %get-tuple-element.26), channel_id=1, source_target_pairs={{0,4},{4,0},{8,12},{12,8},{16,20},{20,16},{24,28},{28,24},{1,5},{5... | collective-permute-start | bytes 393224 | tf_op jit(solution)/shard_map/ppermute | solution.py:431
  23.9 1.3 %collective-permute-start.7 = (f32[8,128]{1,0:T(8,128)S(1)}, f32[8,128]{1,0:T(8,128)S(1)}, u32[]{:S(2)}, u32[]{:S(2)}) collective-permute-start(f32[8,128]{1,0:T(8,128)S(1)} %get-tuple-element.27.extra_ref), channel_id=1, source_target_pairs={{0,4},{4,0},{8,12},{12,8},{16,20},{20,16},{24,28},{28,24},{1,5},{5... | collective-permute-start | bytes 12296 | tf_op jit(solution)/shard_map/ppermute | solution.py:431
  25.3 8.6 %collective-permute-start.8 = (f32[2,8,1152]{2,1,0:T(8,128)S(1)}, f32[2,8,1152]{2,1,0:T(8,128)S(1)}, u32[]{:S(2)}, u32[]{:S(2)}) collective-permute-start(f32[2,8,1152]{2,1,0:T(8,128)S(1)} %get-tuple-element.29), channel_id=1, source_target_pairs={{0,16},{4,20},{8,24},{12,28},{16,0},{20,4},{24,8},{28,12},{1,17},{... | collective-permute-start | bytes 221192 | tf_op jit(solution)/shard_map/ppermute | solution.py:431
  29.4 6.0 %collective-permute-start.10 = (f32[32,512]{1,0:T(8,128)S(1)}, f32[32,512]{1,0:T(8,128)S(1)}, u32[]{:S(2)}, u32[]{:S(2)}) collective-permute-start(f32[32,512]{1,0:T(8,128)S(1)} %get-tuple-element.33), channel_id=1, source_target_pairs={{0,1},{1,0},{2,3},{3,2},{4,5},{5,4},{6,7},{7,6},{8,9},{9,8},{10,11... | collective-permute-start | bytes 196616 | tf_op jit(solution)/shard_map/ppermute | solution.py:431
  29.5 8.5 %collective-permute-start.11 = (f32[32,512]{1,0:T(8,128)S(1)}, f32[32,512]{1,0:T(8,128)S(1)}, u32[]{:S(2)}, u32[]{:S(2)}) collective-permute-start(f32[32,512]{1,0:T(8,128)S(1)} %get-tuple-element.34), channel_id=1, source_target_pairs={{0,2},{1,3},{2,0},{3,1},{4,6},{5,7},{6,4},{7,5},{8,10},{9,11},{10,... | collective-permute-start | bytes 196616 | tf_op jit(solution)/shard_map/ppermute | solution.py:431
  30.5 7.6 %collective-permute-start.12 = (f32[32,512]{1,0:T(8,128)S(1)}, f32[32,512]{1,0:T(8,128)S(1)}, u32[]{:S(2)}, u32[]{:S(2)}) collective-permute-start(f32[32,512]{1,0:T(8,128)S(1)} %get-tuple-element.35), channel_id=1, source_target_pairs={{0,3},{1,2},{2,1},{3,0},{4,7},{5,6},{6,5},{7,4},{8,11},{9,10},{10,... | collective-permute-start | bytes 196616 | tf_op jit(solution)/shard_map/ppermute | solution.py:431
  33.9 4.1 %collective-permute-start.9 = (f32[1,8,1152]{2,1,0:T(8,128)S(1)}, f32[1,8,1152]{2,1,0:T(8,128)S(1)}, u32[]{:S(2)}, u32[]{:S(2)}) collective-permute-start(f32[1,8,1152]{2,1,0:T(8,128)S(1)} %get-tuple-element.31), channel_id=1, source_target_pairs={{0,8},{4,12},{8,0},{12,4},{16,24},{20,28},{24,16},{28,20},{1,9},{5... | collective-permute-start | bytes 110600 | tf_op jit(solution)/shard_map/ppermute | solution.py:431
  38.1 4.3 %collective-permute-start.16 = (f32[32,512]{1,0:T(8,128)S(1)}, f32[32,512]{1,0:T(8,128)S(1)}, u32[]{:S(2)}, u32[]{:S(2)}) collective-permute-start(f32[32,512]{1,0:T(8,128)S(1)} %get-tuple-element.38.refs_0_.yp_ref), channel_id=1, source_target_pairs={{0,8},{4,12},{8,0},{12,4},{16,24},{20,28},{24,16},{28,20},{1,9},{5... | collective-permute-start | bytes 196616 | tf_op jit(solution)/shard_map/ppermute | solution.py:431
  42.4 5.0 %collective-permute-start.17 = (f32[2,32,512]{2,1,0:T(8,128)S(1)}, f32[2,32,512]{2,1,0:T(8,128)S(1)}, u32[]{:S(2)}, u32[]{:S(2)}) collective-permute-start(f32[2,32,512]{2,1,0:T(8,128)S(1)} %shard_map.86.refs_0_), channel_id=1, source_target_pairs={{0,16},{4,20},{8,24},{12,28},{16,0},{20,4},{24,8},{28,12},{1,17},{... | collective-permute-start | bytes 393224 | tf_op jit(solution)/shard_map/ppermute | solution.py:431
  47.5 14.4 %collective-permute-start.18 = (f32[4,32,512]{2,1,0:T(8,128)S(1)}, f32[4,32,512]{2,1,0:T(8,128)S(1)}, u32[]{:S(2)}, u32[]{:S(2)}) collective-permute-start(f32[4,32,512]{2,1,0:T(8,128)S(1)} %shard_map.87.y_ref), channel_id=1, source_target_pairs={{0,4},{4,0},{8,12},{12,8},{16,20},{20,16},{24,28},{28,24},{1,5},{5... | collective-permute-start | bytes 786440 | tf_op jit(solution)/shard_map/ppermute | solution.py:431
  47.6 4.5 %collective-permute-start.13 = (f32[8,1152]{1,0:T(8,128)S(1)}, f32[8,1152]{1,0:T(8,128)S(1)}, u32[]{:S(2)}, u32[]{:S(2)}) collective-permute-start(f32[8,1152]{1,0:T(8,128)S(1)} %get-tuple-element.36.rest_0_), channel_id=1, source_target_pairs={{0,1},{1,0},{2,3},{3,2},{4,5},{5,4},{6,7},{7,6},{8,9},{9,8},{10,11... | collective-permute-start | bytes 110600 | tf_op jit(solution)/shard_map/ppermute | solution.py:431
  48.9 5.6 %collective-permute-start.14 = (f32[8,1152]{1,0:T(8,128)S(1)}, f32[8,1152]{1,0:T(8,128)S(1)}, u32[]{:S(2)}, u32[]{:S(2)}) collective-permute-start(f32[8,1152]{1,0:T(8,128)S(1)} %get-tuple-element.36.rest_0_), channel_id=1, source_target_pairs={{0,2},{1,3},{2,0},{3,1},{4,6},{5,7},{6,4},{7,5},{8,10},{9,11},{10,... | collective-permute-start | bytes 110600 | tf_op jit(solution)/shard_map/ppermute | solution.py:431
  50.2 5.8 %collective-permute-start.15 = (f32[8,1152]{1,0:T(8,128)S(1)}, f32[8,1152]{1,0:T(8,128)S(1)}, u32[]{:S(2)}, u32[]{:S(2)}) collective-permute-start(f32[8,1152]{1,0:T(8,128)S(1)} %get-tuple-element.36.rest_0_), channel_id=1, source_target_pairs={{0,3},{1,2},{2,1},{3,0},{4,7},{5,6},{6,5},{7,4},{8,11},{9,10},{10,... | collective-permute-start | bytes 110600 | tf_op jit(solution)/shard_map/ppermute | solution.py:431

commit v5 on v4

--- a/solution.py
+++ b/solution.py
@@ -16,6 +16,7 @@
 SMEM = pltpu.MemorySpace.SMEM
 LANES = 128
 VMEM_LIMIT = 16 * 1024 * 1024
+UNROLL = 4
 LOAD_FLOPS = 20_000_000_000
 
 
@@ -139,7 +140,9 @@
             cross = cross + three_pass(dot_nt, rows_ref[h], forward)
         return cross
 
-    cross = lax.fori_loop(0, row_count // 2, two_spans, jnp.zeros((width, width), f32))
+    cross = lax.fori_loop(
+        0, row_count // 2, two_spans, jnp.zeros((width, width), f32), unroll=UNROLL
+    )
     extra_ref[...] = pack([gram[:width, :width], gram[:width, width:], gram[width:, width:], cross])
 
 
@@ -181,7 +184,7 @@
                 spread[at] += back[:, k * bs : (k + 1) * bs] * w
         return carry
 
-    lax.fori_loop(0, row_count // 2, one_span, 0)
+    lax.fori_loop(0, row_count // 2, one_span, 0, unroll=UNROLL)
 
 
 def back_even_kernel(sizes, cols_ref, live_ref, even_ref, blocks_ref, spread_ref):
@@ -246,7 +249,7 @@
 
 def solve_kernel(col_count, width, *rest):
     y_refs = rest[:col_count]
-    aux_ref, wide_ref = rest[col_count:]
+    (aux_ref,) = rest[col_count:]
     w = width
     sums = tree_sum([take(y_ref[...])[1] for y_ref in y_refs])
     gram_x, xp, pp, xbx = (unpack(sums, i) for i in range(4))
@@ -254,13 +257,8 @@
     done = eliminate(jnp.concatenate([gram_x, eye(w), cross_x, xp], axis=1), w)
     inverse_l, below_p = done[:, w : 2 * w], done[:, 3 * w : 4 * w]
     coefficient = dot_tn(inverse_l, done[:, 2 * w : 3 * w])
-    xr = cross_x - dot_nn(gram_x, coefficient)
     aux_ref[...] = jnp.concatenate(
-        [-coefficient.T, coefficient, xr, xp, pp, cross_x, inverse_l, jnp.zeros_like(xp)], axis=1
-    )
-    upper = jnp.concatenate([dot_nn(inverse_l, xr), below_p], axis=1)
-    wide_ref[...] = jnp.concatenate(
-        [dot_tn(upper, upper), -dot_tn(upper, inverse_l), jnp.zeros((2 * w, w), f32)], axis=1
+        [-coefficient.T, coefficient, below_p, xp, pp, cross_x, inverse_l, gram_x], axis=1
     )
 
 
@@ -289,7 +287,7 @@
             )
         return carry
 
-    lax.fori_loop(0, row_count // 2, two_spans, 0)
+    lax.fori_loop(0, row_count // 2, two_spans, 0, unroll=UNROLL)
 
 
 def iota(shape, axis):
@@ -318,12 +316,27 @@
             cross = cross + three_pass(dot_nt, both, forward_ref[2 * h + parity])
         return cross
 
-    return lax.fori_loop(0, x_ref.shape[0] // 2, two_spans, jnp.zeros((2 * w, 2 * w), f32))
+    zero = jnp.zeros((2 * w, 2 * w), f32)
+    return lax.fori_loop(0, x_ref.shape[0] // 2, two_spans, zero, unroll=UNROLL // 2)
 
 
 def gram_even_kernel(
-    width, aux_ref, x_ref, y_ref, forward_ref, p_ref, resid_ref, cross_ref, gram_ref
+    width, aux_ref, x_ref, y_ref, forward_ref, p_ref, resid_ref, cross_ref, gram_ref, wide_ref
 ):
+    w = width
+    coefficient, below_p, cross_x, inverse_l, gram_x = (
+        aux_ref[:, i * w : (i + 1) * w] for i in (1, 2, 5, 6, 7)
+    )
+    xr = cross_x - dot_nn(gram_x, coefficient)
+    upper = jnp.concatenate([dot_nn(inverse_l, xr), below_p], axis=1)
+    wide_ref[...] = jnp.concatenate(
+        [
+            dot_tn(upper, upper),
+            -dot_tn(upper, inverse_l),
+            jnp.concatenate([xr, jnp.zeros((w, w), f32)], axis=0),
+        ],
+        axis=1,
+    )
     mine = resid_ref[...]
     gram_ref[...] = four_pass(dot_nt, mine, jnp.concatenate([mine, p_ref[...]], axis=0))
     cross_ref[...] = gram_spans(width, 0, aux_ref, x_ref, y_ref, forward_ref)
@@ -361,7 +374,10 @@
     rr = jnp.where(row <= lane, first, below)
     rar = jnp.where(row > lane, first, jnp.where(row < lane, below, diagonal))
     pap = jnp.where(row <= lane, second, second.T)
-    coefficient, xr, xp, pp, xax, inverse_x = (aux_ref[:, i * w : (i + 1) * w] for i in range(1, 7))
+    coefficient, xp, pp, xax, inverse_x = (
+        aux_ref[:, i * w : (i + 1) * w] for i in (1, 3, 4, 5, 6)
+    )
+    xr = wide_ref[:w, 3 * w : 4 * w]
     schur = (
         jnp.concatenate(
             [jnp.concatenate([rr, rp], axis=1), jnp.concatenate([rp.T, pp], axis=1)], axis=0
@@ -495,11 +511,11 @@
     )
     image_cols = over_col([message] * col_count)
     image_even, image_odd = gather_rows(image)
-    aux, wide = call(
+    (aux,) = call(
         functools.partial(solve_kernel, col_count, width),
         "v" * col_count,
         image_cols,
-        [shape(width, LANES), shape(2 * width, 4 * width)],
+        [shape(width, 8 * width)],
     )
     forward_rp, resid, resid_out = call(
         functools.partial(forward_rest_kernel, sizes),
@@ -508,11 +524,11 @@
         [shape(row_count, 2 * width, span_rows)] + [shape(width, span_rows)] * 2,
         [pltpu.VMEM((col_blocks, 4 * width, bs), bf16)],
     )
-    cross, gram = call(
+    cross, gram, wide = call(
         functools.partial(gram_even_kernel, width),
         "v" * 6,
         [aux, x_even, image_even, forward_rp, direction, resid],
-        [shape(2 * width, 2 * width), shape(width, 2 * width)],
+        [shape(2 * width, 2 * width), shape(width, 2 * width), shape(2 * width, 4 * width)],
     )
     (part,) = call(
         functools.partial(gram_odd_kernel, width),

time: 78.8 us -> 76.2 us (0.967)
  Pallas kernels: 17.3 us -> 14.8 us
    pallas_call x16, Pallas kernels: 17.3 us -> 14.8 us  [call(): pl.pallas_call(kernel, in_specs=[spec[letter] for letter in ins], out_spe...]
  transfers between devices with their start and end apart: 19 -> 19, of which waited for: 10 -> 10; matrix products, arithmetic and copies ran while one was open for 0% -> 0% of each run, Pallas kernels for 11% -> 9%
where the time goes in v5:
time: 76.2 us; the launch traced here: 76.1 us
  starting transfers between devices  24.7 us (32%)
  waiting for transfers between devices  24.7 us (32%)
  Pallas kernels  14.8 us (19%)
  blocking collectives  11.1 us (15%)
  between operations  0.78 us (1%)
    ppermute x19, starting transfers between devices, swap(): lax.ppermute(array, axis, [(i, i ^ s) for i in range(lax.axis_size(axis))])  24.7 us
    ppermute x19, waiting for transfers between devices, swap(): lax.ppermute(array, axis, [(i, i ^ s) for i in range(lax.axis_size(axis))])  24.7 us
    pallas_call x16, Pallas kernels, call(): pl.pallas_call(kernel, in_specs=[spec[letter] for letter in ins], out_spe...  14.8 us
    all_to_all x1, blocking collectives, per_device(): parts = lax.all_to_all(part, ('col', 'row'), 0, 0)  11.1 us
  transfers between devices with their start and end apart: 19, of which 10 were waited for; matrix products, arithmetic and copies ran while one was open for 0% of the time, Pallas kernels for 9%

profile of v5, /device:TPU:0, one launch (start us, length us, event | category | flops | bytes accessed | tf_op | source)
XLA Modules:
  0.0 76.1 jit_solution(12418956198112183278)
XLA Ops:
  0.7 3.0 %collective-permute-start = (f32[16,512]{1,0:T(8,128)}, f32[16,512]{1,0:T(8,128)S(1)}, u32[]{:S(2)}, u32[]{:S(2)}) collective-permute-start(f32[16,512]{1,0:T(8,128)} %rest_4_.3), channel_id=1, source_target_pairs={{0,8},{4,12},{8,0},{12,4},{16,24},{20,28},{24,16},{28,20},{1,9},{5... | collective-permute-start | bytes 98312 | tf_op jit(solution)/shard_map/ppermute | solution.py:447
  3.7 2.1 %collective-permute-done.refs_1_ = f32[16,512]{1,0:T(8,128)S(1)} collective-permute-done((f32[16,512]{1,0:T(8,128)}, f32[16,512]{1,0:T(8,128)S(1)}, u32[]{:S(2)}, u32[]{:S(2)}) %collective-permute-start) | collective-permute-done | bytes 32800 | tf_op jit(solution)/shard_map/ppermute | solution.py:447
  5.8 2.1 %collective-permute-start.1 = (f32[2,16,512]{2,1,0:T(8,128)S(1)}, f32[2,16,512]{2,1,0:T(8,128)S(1)}, u32[]{:S(2)}, u32[]{:S(2)}) collective-permute-start(f32[2,16,512]{2,1,0:T(8,128)S(1)} %shard_map.77.refs_0_), channel_id=1, source_target_pairs={{0,16},{4,20},{8,24},{12,28},{16,0},{20,4},{24,8},{28,12},{1,17},{... | collective-permute-start | bytes 196616 | tf_op jit(solution)/shard_map/ppermute | solution.py:447
  7.9 2.2 %collective-permute-done.1.refs_1_ = f32[2,16,512]{2,1,0:T(8,128)S(1)} collective-permute-done((f32[2,16,512]{2,1,0:T(8,128)S(1)}, f32[2,16,512]{2,1,0:T(8,128)S(1)}, u32[]{:S(2)}, u32[]{:S(2)}) %collective-permute-start.1) | collective-permute-done | bytes 65568 | tf_op jit(solution)/shard_map/ppermute | solution.py:447
  10.3 2.1 %collective-permute-start.3 = (f32[16,512]{1,0:T(8,128)S(1)}, f32[16,512]{1,0:T(8,128)S(1)}, u32[]{:S(2)}, u32[]{:S(2)}) collective-permute-start(f32[16,512]{1,0:T(8,128)S(1)} %copy-done.2), channel_id=1, source_target_pairs={{0,1},{1,0},{2,3},{3,2},{4,5},{5,4},{6,7},{7,6},{8,9},{9,8},{10,11... | collective-permute-start | bytes 98312 | tf_op jit(solution)/shard_map/ppermute | solution.py:447
  12.4 2.6 %collective-permute-start.4 = (f32[16,512]{1,0:T(8,128)S(1)}, f32[16,512]{1,0:T(8,128)S(1)}, u32[]{:S(2)}, u32[]{:S(2)}) collective-permute-start(f32[16,512]{1,0:T(8,128)S(1)} %copy-done.2), channel_id=1, source_target_pairs={{0,2},{1,3},{2,0},{3,1},{4,6},{5,7},{6,4},{7,5},{8,10},{9,11},{10,... | collective-permute-start | bytes 98312 | tf_op jit(solution)/shard_map/ppermute | solution.py:447
  15.0 2.8 %collective-permute-done.4.rest_2_.rest_6_ = f32[16,512]{1,0:T(8,128)S(1)} collective-permute-done((f32[16,512]{1,0:T(8,128)S(1)}, f32[16,512]{1,0:T(8,128)S(1)}, u32[]{:S(2)}, u32[]{:S(2)}) %collective-permute-start.4) | collective-permute-done | bytes 32800 | tf_op jit(solution)/shard_map/ppermute | solution.py:447
  17.8 2.9 %collective-permute-done.5.rest_3_.rest_7_ = f32[16,512]{1,0:T(8,128)S(1)} collective-permute-done((f32[16,512]{1,0:T(8,128)S(1)}, f32[16,512]{1,0:T(8,128)S(1)}, u32[]{:S(2)}, u32[]{:S(2)}) %collective-permute-start.5) | collective-permute-done | bytes 32800 | tf_op jit(solution)/shard_map/ppermute | solution.py:447
  20.8 2.4 %shard_map.79 = (f32[4,16,512]{2,1,0:T(8,128)S(1)}, f32[4,16,512]{2,1,0:T(8,128)S(1)}, f32[8,128]{1,0:T(8,128)S(1)}) custom-call(s32[2,32]{1,0:T(2,128)S(1)} %bitcast.2, s32[1,32]{1,0:T(1,128)S(1)} %bitcast.6, f32[4,16,512]{2,1,0:T(8,128)S(1)} %shard_map.78.even_ref.x_ref, f32[4,16,512]{2,1,0:T(8,128)S(1)} %collective-permute-done.2.odd_ref.x_ref, ...), custom_call_target="tpu_custom_call" | custom-call | tf_op jit(solution)/shard_map/pallas_call | solution.py:436
  23.7 0.8 %collective-permute-done.7.got_extra_ref = f32[8,128]{1,0:T(8,128)S(1)} collective-permute-done((f32[8,128]{1,0:T(8,128)S(1)}, f32[8,128]{1,0:T(8,128)S(1)}, u32[]{:S(2)}, u32[]{:S(2)}) %collective-permute-start.7) | collective-permute-done | bytes 4128 | tf_op jit(solution)/shard_map/ppermute | solution.py:447
  24.6 1.6 %collective-permute-start.8 = (f32[2,8,1152]{2,1,0:T(8,128)S(1)}, f32[2,8,1152]{2,1,0:T(8,128)S(1)}, u32[]{:S(2)}, u32[]{:S(2)}) collective-permute-start(f32[2,8,1152]{2,1,0:T(8,128)S(1)} %get-tuple-element.28), channel_id=1, source_target_pairs={{0,16},{4,20},{8,24},{12,28},{16,0},{20,4},{24,8},{28,12},{1,17},{... | collective-permute-start | bytes 221192 | tf_op jit(solution)/shard_map/ppermute | solution.py:447
  26.1 0.9 %shard_map.82.begun_ref = f32[16,16,128]{2,1,0:T(8,128)S(1)} custom-call(s32[2,32]{1,0:T(2,128)S(1)} %bitcast.3, s32[1,32]{1,0:T(1,128)S(1)} %bitcast.7, f32[4,16,512]{2,1,0:T(8,128)S(1)} %shard_map.78.even_ref.x_ref, bf16[32,2,128,128]{3,2,1,0:T(8,128)(2,1)S(1)} %copy-done), custom_call_target="tpu_custom_call" | custom-call | tf_op jit(solution)/shard_map/pallas_call | solution.py:436
  27.1 0.9 %shard_map.83 = (f32[32,512]{1,0:T(8,128)S(1)}, f32[32,512]{1,0:T(8,128)S(1)}, f32[32,512]{1,0:T(8,128)S(1)}, f32[32,512]{1,0:T(8,128)S(1)}) custom-call(s32[2,32]{1,0:T(2,128)S(1)} %bitcast.4, s32[1,32]{1,0:T(1,128)S(1)} %bitcast.8, f32[4,16,512]{2,1,0:T(8,128)S(1)} %collective-permute-done.2.odd_ref.x_ref, bf16[32,2,128,128]{3,2,1,0:T(8,128)(2,1)S(1)} %copy-done, ...), custom_call_target="tpu_custom_call" | custom-call | tf_op jit(solution)/shard_map/pallas_call | solution.py:436
  28.1 1.0 %collective-permute-start.11 = (f32[32,512]{1,0:T(8,128)S(1)}, f32[32,512]{1,0:T(8,128)S(1)}, u32[]{:S(2)}, u32[]{:S(2)}) collective-permute-start(f32[32,512]{1,0:T(8,128)S(1)} %get-tuple-element.33), channel_id=1, source_target_pairs={{0,2},{1,3},{2,0},{3,1},{4,6},{5,7},{6,4},{7,5},{8,10},{9,11},{10,... | collective-permute-start | bytes 196616 | tf_op jit(solution)/shard_map/ppermute | solution.py:447
  29.0 3.4 %collective-permute-start.12 = (f32[32,512]{1,0:T(8,128)S(1)}, f32[32,512]{1,0:T(8,128)S(1)}, u32[]{:S(2)}, u32[]{:S(2)}) collective-permute-start(f32[32,512]{1,0:T(8,128)S(1)} %get-tuple-element.34), channel_id=1, source_target_pairs={{0,3},{1,2},{2,1},{3,0},{4,7},{5,6},{6,5},{7,4},{8,11},{9,10},{10,... | collective-permute-start | bytes 196616 | tf_op jit(solution)/shard_map/ppermute | solution.py:447
  32.5 1.6 %collective-permute-start.9 = (f32[1,8,1152]{2,1,0:T(8,128)S(1)}, f32[1,8,1152]{2,1,0:T(8,128)S(1)}, u32[]{:S(2)}, u32[]{:S(2)}) collective-permute-start(f32[1,8,1152]{2,1,0:T(8,128)S(1)} %get-tuple-element.30), channel_id=1, source_target_pairs={{0,8},{4,12},{8,0},{12,4},{16,24},{20,28},{24,16},{28,20},{1,9},{5... | collective-permute-start | bytes 110600 | tf_op jit(solution)/shard_map/ppermute | solution.py:447
  34.0 2.6 %collective-permute-done.11.refs_2_.rest_10_ = f32[32,512]{1,0:T(8,128)S(1)} collective-permute-done((f32[32,512]{1,0:T(8,128)S(1)}, f32[32,512]{1,0:T(8,128)S(1)}, u32[]{:S(2)}, u32[]{:S(2)}) %collective-permute-start.11) | collective-permute-done | bytes 65568 | tf_op jit(solution)/shard_map/ppermute | solution.py:447
  36.6 1.6 %collective-permute-start.16 = (f32[32,512]{1,0:T(8,128)S(1)}, f32[32,512]{1,0:T(8,128)S(1)}, u32[]{:S(2)}, u32[]{:S(2)}) collective-permute-start(f32[32,512]{1,0:T(8,128)S(1)} %get-tuple-element.36.refs_0_.yp_ref), channel_id=1, source_target_pairs={{0,8},{4,12},{8,0},{12,4},{16,24},{20,28},{24,16},{28,20},{1,9},{5... | collective-permute-start | bytes 196616 | tf_op jit(solution)/shard_map/ppermute | solution.py:447
  38.2 2.8 %collective-permute-done.16.refs_1_ = f32[32,512]{1,0:T(8,128)S(1)} collective-permute-done((f32[32,512]{1,0:T(8,128)S(1)}, f32[32,512]{1,0:T(8,128)S(1)}, u32[]{:S(2)}, u32[]{:S(2)}) %collective-permute-start.16) | collective-permute-done | bytes 65568 | tf_op jit(solution)/shard_map/ppermute | solution.py:447
  41.0 0.6 collective-permute-start.17
  41.5 4.5 %collective-permute-done.17.refs_1_ = f32[2,32,512]{2,1,0:T(8,128)S(1)} collective-permute-done((f32[2,32,512]{2,1,0:T(8,128)S(1)}, f32[2,32,512]{2,1,0:T(8,128)S(1)}, u32[]{:S(2)}, u32[]{:S(2)}) %collective-permute-start.17) | collective-permute-done | bytes 131104 | tf_op jit(solution)/shard_map/ppermute | solution.py:447
  46.1 1.3 %collective-permute-start.13 = (f32[8,1152]{1,0:T(8,128)S(1)}, f32[8,1152]{1,0:T(8,128)S(1)}, u32[]{:S(2)}, u32[]{:S(2)}) collective-permute-start(f32[8,1152]{1,0:T(8,128)S(1)} %get-tuple-element.35.rest_0_), channel_id=1, source_target_pairs={{0,1},{1,0},{2,3},{3,2},{4,5},{5,4},{6,7},{7,6},{8,9},{9,8},{10,11... | collective-permute-start | bytes 110600 | tf_op jit(solution)/shard_map/ppermute | solution.py:447
  47.4 1.3 %collective-permute-start.14 = (f32[8,1152]{1,0:T(8,128)S(1)}, f32[8,1152]{1,0:T(8,128)S(1)}, u32[]{:S(2)}, u32[]{:S(2)}) collective-permute-start(f32[8,1152]{1,0:T(8,128)S(1)} %get-tuple-element.35.rest_0_), channel_id=1, source_target_pairs={{0,2},{1,3},{2,0},{3,1},{4,6},{5,7},{6,4},{7,5},{8,10},{9,11},{10,... | collective-permute-start | bytes 110600 | tf_op jit(solution)/shard_map/ppermute | solution.py:447
  48.7 1.8 %collective-permute-start.15 = (f32[8,1152]{1,0:T(8,128)S(1)}, f32[8,1152]{1,0:T(8,128)S(1)}, u32[]{:S(2)}, u32[]{:S(2)}) collective-permute-start(f32[8,1152]{1,0:T(8,128)S(1)} %get-tuple-element.35.rest_0_), channel_id=1, source_target_pairs={{0,3},{1,2},{2,1},{3,0},{4,7},{5,6},{6,5},{7,4},{8,11},{9,10},{10,... | collective-permute-start | bytes 110600 | tf_op jit(solution)/shard_map/ppermute | solution.py:447
  50.5 2.5 %collective-permute-done.14.rest_2_ = f32[8,1152]{1,0:T(8,128)S(1)} collective-permute-done((f32[8,1152]{1,0:T(8,128)S(1)}, f32[8,1152]{1,0:T(8,128)S(1)}, u32[]{:S(2)}, u32[]{:S(2)}) %collective-permute-start.14) | collective-permute-done | bytes 36896 | tf_op jit(solution)/shard_map/ppermute | solution.py:447
  53.0 1.4 %collective-permute-done.15.rest_3_ = f32[8,1152]{1,0:T(8,128)S(1)} collective-permute-done((f32[8,1152]{1,0:T(8,128)S(1)}, f32[8,1152]{1,0:T(8,128)S(1)}, u32[]{:S(2)}, u32[]{:S(2)}) %collective-permute-start.15) | collective-permute-done | bytes 36896 | tf_op jit(solution)/shard_map/ppermute | solution.py:447
  54.5 1.4 %shard_map.85.aux_ref = f32[16,128]{1,0:T(8,128)S(1)} custom-call(f32[8,1152]{1,0:T(8,128)S(1)} %get-tuple-element.35.rest_0_, f32[8,1152]{1,0:T(8,128)S(1)} %collective-permute-done.13.rest_1_, f32[8,1152]{1,0:T(8,128)S(1)} %collective-permute-done.14.rest_2_, f32[8,1152]{1,0:T(8,128)S(1)} %collective-permute-done.15.rest_3_), custom_call_target="tpu_custom_call" | custom-call | tf_op jit(solution)/shard_map/pallas_call | solution.py:436
  55.9 2.3 %shard_map.88 = (f32[8,32,512]{2,1,0:T(8,128)S(1)}, f32[16,512]{1,0:T(8,128)S(1)}, f32[16,512]{1,0:T(8,128)}) custom-call(s32[2,32]{1,0:T(2,128)S(1)} %bitcast.5, s32[1,32]{1,0:T(1,128)S(1)} %bitcast.9, f32[16,128]{1,0:T(8,128)S(1)} %shard_map.85.aux_ref, f32[8,1152]{1,0:T(8,128)S(1)} %get-tuple-element.35.rest_0_, ...), custom_call_target="tpu_custom_call" | custom-call | tf_op jit(solution)/shard_map/pallas_call | solution.py:436
  58.2 1.3 %shard_map.89 = (f32[32,32]{1,0:T(8,128)S(1)}, f32[16,32]{1,0:T(8,128)S(1)}, f32[32,64]{1,0:T(8,128)S(1)}) custom-call(f32[16,128]{1,0:T(8,128)S(1)} %shard_map.85.aux_ref, f32[4,16,512]{2,1,0:T(8,128)S(1)} %shard_map.78.even_ref.x_ref, f32[4,32,512]{2,1,0:T(8,128)S(1)} %shard_map.87.y_ref, f32[8,32,512]{2,1,0:T(8,128)S(1)} %get-tuple-element.37.forward_ref, ...), custom_call_target="tpu_custom_call" | custom-call | tf_op jit(solution)/shard_map/pallas_call | solution.py:436
  59.5 1.2 %shard_map.90 = f32[32,8,128]{2,1,0:T(8,128)S(1)} custom-call(f32[16,128]{1,0:T(8,128)S(1)} %shard_map.85.aux_ref, f32[4,16,512]{2,1,0:T(8,128)S(1)} %collective-permute-done.2.odd_ref.x_ref, f32[4,32,512]{2,1,0:T(8,128)S(1)} %collective-permute-done.18.y_ref, f32[8,32,512]{2,1,0:T(8,128)S(1)} %get-tuple-element.37.forward_ref, ...), custom_call_target="tpu_custom_call" | custom-call | tf_op jit(solution)/shard_map/pallas_call | solution.py:436
  60.7 11.1 %all_to_all.5.parts_ref = f32[32,8,128]{2,1,0:T(8,128)S(1)} all-to-all(f32[32,8,128]{2,1,0:T(8,128)S(1)} %shard_map.90), channel_id=1, replica_groups=mesh['row'=8,'col'=4] {'col','row'}, dimensions={0} | all-to-all | bytes 262144 | tf_op jit(solution)/shard_map/all_to_all | solution.py:539
  71.8 4.3 %shard_map.91 = (f32[16,512]{1,0:T(8,128)}, f32[48,48]{1,0:T(8,128)}) custom-call(f32[32,8,128]{2,1,0:T(8,128)S(1)} %all_to_all.5.parts_ref, f32[16,128]{1,0:T(8,128)S(1)} %shard_map.85.aux_ref, f32[32,64]{1,0:T(8,128)S(1)} %get-tuple-element.41.wide_ref, f32[4,16,512]{2,1,0:T(8,128)S(1)} %shard_map.78.even_ref.x_ref, ...), custom_call_target="tpu_custom_call" | custom-call | tf_op jit(solution)/shard_map/pallas_call | solution.py:436
  (33 shorter events, 0.9 us)
Async XLA Ops:
  0.6 5.2 %copy-start.2 = (f32[16,512]{1,0:T(8,128)S(1)}, f32[16,512]{1,0:T(8,128)}, u32[]{:S(2)}) copy-start(f32[16,512]{1,0:T(8,128)} %rest_4_.3) | copy-start | bytes 98308
  0.6 20.1 %copy-start.3 = (s32[32,2]{0,1:T(2,128)S(1)}, s32[32,2]{0,1:T(2,128)}, u32[]{:S(2)}) copy-start(s32[32,2]{0,1:T(2,128)} %param.8) | copy-start | bytes 772
  0.7 20.1 %copy-start.4 = (s32[32,1]{0,1:T(1,128)S(1)}, s32[32,1]{0,1:T(1,128)}, u32[]{:S(2)}) copy-start(s32[32,1]{0,1:T(1,128)} %param.9) | copy-start | bytes 388
  0.7 20.1 %copy-start.1 = (f32[16,512]{1,0:T(8,128)S(1)}, f32[16,512]{1,0:T(8,128)}, u32[]{:S(2)}) copy-start(f32[16,512]{1,0:T(8,128)} %p_ref.3) | copy-start | bytes 98308
  0.7 20.1 %copy-start = (bf16[32,2,128,128]{3,2,1,0:T(8,128)(2,1)S(1)}, bf16[32,2,128,128]{3,2,1,0:T(8,128)(2,1)}, u32[]{:S(2)}) copy-start(bf16[32,2,128,128]{3,2,1,0:T(8,128)(2,1)} %rest_12_.1) | copy-start | bytes 6291460
  0.7 5.1 %collective-permute-start = (f32[16,512]{1,0:T(8,128)}, f32[16,512]{1,0:T(8,128)S(1)}, u32[]{:S(2)}, u32[]{:S(2)}) collective-permute-start(f32[16,512]{1,0:T(8,128)} %rest_4_.3), channel_id=1, source_target_pairs={{0,8},{4,12},{8,0},{12,4},{16,24},{20,28},{24,16},{28,20},{1,9},{5... | collective-permute-start | bytes 98312 | tf_op jit(solution)/shard_map/ppermute | solution.py:447
  5.8 4.4 %collective-permute-start.1 = (f32[2,16,512]{2,1,0:T(8,128)S(1)}, f32[2,16,512]{2,1,0:T(8,128)S(1)}, u32[]{:S(2)}, u32[]{:S(2)}) collective-permute-start(f32[2,16,512]{2,1,0:T(8,128)S(1)} %shard_map.77.refs_0_), channel_id=1, source_target_pairs={{0,16},{4,20},{8,24},{12,28},{16,0},{20,4},{24,8},{28,12},{1,17},{... | collective-permute-start | bytes 196616 | tf_op jit(solution)/shard_map/ppermute | solution.py:447
  10.2 10.5 %collective-permute-start.2 = (f32[4,16,512]{2,1,0:T(8,128)S(1)}, f32[4,16,512]{2,1,0:T(8,128)S(1)}, u32[]{:S(2)}, u32[]{:S(2)}) collective-permute-start(f32[4,16,512]{2,1,0:T(8,128)S(1)} %shard_map.78.even_ref.x_ref), channel_id=1, source_target_pairs={{0,4},{4,0},{8,12},{12,8},{16,20},{20,16},{24,28},{28,24},{1,5},{5... | collective-permute-start | bytes 393224 | tf_op jit(solution)/shard_map/ppermute | solution.py:447
  10.3 4.7 %collective-permute-start.3 = (f32[16,512]{1,0:T(8,128)S(1)}, f32[16,512]{1,0:T(8,128)S(1)}, u32[]{:S(2)}, u32[]{:S(2)}) collective-permute-start(f32[16,512]{1,0:T(8,128)S(1)} %copy-done.2), channel_id=1, source_target_pairs={{0,1},{1,0},{2,3},{3,2},{4,5},{5,4},{6,7},{7,6},{8,9},{9,8},{10,11... | collective-permute-start | bytes 98312 | tf_op jit(solution)/shard_map/ppermute | solution.py:447
  12.4 5.4 %collective-permute-start.4 = (f32[16,512]{1,0:T(8,128)S(1)}, f32[16,512]{1,0:T(8,128)S(1)}, u32[]{:S(2)}, u32[]{:S(2)}) collective-permute-start(f32[16,512]{1,0:T(8,128)S(1)} %copy-done.2), channel_id=1, source_target_pairs={{0,2},{1,3},{2,0},{3,1},{4,6},{5,7},{6,4},{7,5},{8,10},{9,11},{10,... | collective-permute-start | bytes 98312 | tf_op jit(solution)/shard_map/ppermute | solution.py:447
  15.0 5.7 %collective-permute-start.5 = (f32[16,512]{1,0:T(8,128)S(1)}, f32[16,512]{1,0:T(8,128)S(1)}, u32[]{:S(2)}, u32[]{:S(2)}) collective-permute-start(f32[16,512]{1,0:T(8,128)S(1)} %copy-done.2), channel_id=1, source_target_pairs={{0,3},{1,2},{2,1},{3,0},{4,7},{5,6},{6,5},{7,4},{8,11},{9,10},{10,... | collective-permute-start | bytes 98312 | tf_op jit(solution)/shard_map/ppermute | solution.py:447
  23.2 1.4 %collective-permute-start.6 = (f32[4,16,512]{2,1,0:T(8,128)S(1)}, f32[4,16,512]{2,1,0:T(8,128)S(1)}, u32[]{:S(2)}, u32[]{:S(2)}) collective-permute-start(f32[4,16,512]{2,1,0:T(8,128)S(1)} %get-tuple-element.25), channel_id=1, source_target_pairs={{0,4},{4,0},{8,12},{12,8},{16,20},{20,16},{24,28},{28,24},{1,5},{5... | collective-permute-start | bytes 393224 | tf_op jit(solution)/shard_map/ppermute | solution.py:447
  23.2 1.4 %collective-permute-start.7 = (f32[8,128]{1,0:T(8,128)S(1)}, f32[8,128]{1,0:T(8,128)S(1)}, u32[]{:S(2)}, u32[]{:S(2)}) collective-permute-start(f32[8,128]{1,0:T(8,128)S(1)} %get-tuple-element.26.extra_ref), channel_id=1, source_target_pairs={{0,4},{4,0},{8,12},{12,8},{16,20},{20,16},{24,28},{28,24},{1,5},{5... | collective-permute-start | bytes 12296 | tf_op jit(solution)/shard_map/ppermute | solution.py:447
  24.6 7.9 %collective-permute-start.8 = (f32[2,8,1152]{2,1,0:T(8,128)S(1)}, f32[2,8,1152]{2,1,0:T(8,128)S(1)}, u32[]{:S(2)}, u32[]{:S(2)}) collective-permute-start(f32[2,8,1152]{2,1,0:T(8,128)S(1)} %get-tuple-element.28), channel_id=1, source_target_pairs={{0,16},{4,20},{8,24},{12,28},{16,0},{20,4},{24,8},{28,12},{1,17},{... | collective-permute-start | bytes 221192 | tf_op jit(solution)/shard_map/ppermute | solution.py:447
  28.0 6.0 %collective-permute-start.10 = (f32[32,512]{1,0:T(8,128)S(1)}, f32[32,512]{1,0:T(8,128)S(1)}, u32[]{:S(2)}, u32[]{:S(2)}) collective-permute-start(f32[32,512]{1,0:T(8,128)S(1)} %get-tuple-element.32), channel_id=1, source_target_pairs={{0,1},{1,0},{2,3},{3,2},{4,5},{5,4},{6,7},{7,6},{8,9},{9,8},{10,11... | collective-permute-start | bytes 196616 | tf_op jit(solution)/shard_map/ppermute | solution.py:447
  28.1 8.5 %collective-permute-start.11 = (f32[32,512]{1,0:T(8,128)S(1)}, f32[32,512]{1,0:T(8,128)S(1)}, u32[]{:S(2)}, u32[]{:S(2)}) collective-permute-start(f32[32,512]{1,0:T(8,128)S(1)} %get-tuple-element.33), channel_id=1, source_target_pairs={{0,2},{1,3},{2,0},{3,1},{4,6},{5,7},{6,4},{7,5},{8,10},{9,11},{10,... | collective-permute-start | bytes 196616 | tf_op jit(solution)/shard_map/ppermute | solution.py:447
  29.0 7.6 %collective-permute-start.12 = (f32[32,512]{1,0:T(8,128)S(1)}, f32[32,512]{1,0:T(8,128)S(1)}, u32[]{:S(2)}, u32[]{:S(2)}) collective-permute-start(f32[32,512]{1,0:T(8,128)S(1)} %get-tuple-element.34), channel_id=1, source_target_pairs={{0,3},{1,2},{2,1},{3,0},{4,7},{5,6},{6,5},{7,4},{8,11},{9,10},{10,... | collective-permute-start | bytes 196616 | tf_op jit(solution)/shard_map/ppermute | solution.py:447
  32.5 4.1 %collective-permute-start.9 = (f32[1,8,1152]{2,1,0:T(8,128)S(1)}, f32[1,8,1152]{2,1,0:T(8,128)S(1)}, u32[]{:S(2)}, u32[]{:S(2)}) collective-permute-start(f32[1,8,1152]{2,1,0:T(8,128)S(1)} %get-tuple-element.30), channel_id=1, source_target_pairs={{0,8},{4,12},{8,0},{12,4},{16,24},{20,28},{24,16},{28,20},{1,9},{5... | collective-permute-start | bytes 110600 | tf_op jit(solution)/shard_map/ppermute | solution.py:447
  36.6 4.3 %collective-permute-start.16 = (f32[32,512]{1,0:T(8,128)S(1)}, f32[32,512]{1,0:T(8,128)S(1)}, u32[]{:S(2)}, u32[]{:S(2)}) collective-permute-start(f32[32,512]{1,0:T(8,128)S(1)} %get-tuple-element.36.refs_0_.yp_ref), channel_id=1, source_target_pairs={{0,8},{4,12},{8,0},{12,4},{16,24},{20,28},{24,16},{28,20},{1,9},{5... | collective-permute-start | bytes 196616 | tf_op jit(solution)/shard_map/ppermute | solution.py:447
  41.0 5.0 %collective-permute-start.17 = (f32[2,32,512]{2,1,0:T(8,128)S(1)}, f32[2,32,512]{2,1,0:T(8,128)S(1)}, u32[]{:S(2)}, u32[]{:S(2)}) collective-permute-start(f32[2,32,512]{2,1,0:T(8,128)S(1)} %shard_map.86.refs_0_), channel_id=1, source_target_pairs={{0,16},{4,20},{8,24},{12,28},{16,0},{20,4},{24,8},{28,12},{1,17},{... | collective-permute-start | bytes 393224 | tf_op jit(solution)/shard_map/ppermute | solution.py:447
  46.0 13.5 %collective-permute-start.18 = (f32[4,32,512]{2,1,0:T(8,128)S(1)}, f32[4,32,512]{2,1,0:T(8,128)S(1)}, u32[]{:S(2)}, u32[]{:S(2)}) collective-permute-start(f32[4,32,512]{2,1,0:T(8,128)S(1)} %shard_map.87.y_ref), channel_id=1, source_target_pairs={{0,4},{4,0},{8,12},{12,8},{16,20},{20,16},{24,28},{28,24},{1,5},{5... | collective-permute-start | bytes 786440 | tf_op jit(solution)/shard_map/ppermute | solution.py:447
  46.1 4.5 %collective-permute-start.13 = (f32[8,1152]{1,0:T(8,128)S(1)}, f32[8,1152]{1,0:T(8,128)S(1)}, u32[]{:S(2)}, u32[]{:S(2)}) collective-permute-start(f32[8,1152]{1,0:T(8,128)S(1)} %get-tuple-element.35.rest_0_), channel_id=1, source_target_pairs={{0,1},{1,0},{2,3},{3,2},{4,5},{5,4},{6,7},{7,6},{8,9},{9,8},{10,11... | collective-permute-start | bytes 110600 | tf_op jit(solution)/shard_map/ppermute | solution.py:447
  47.4 5.6 %collective-permute-start.14 = (f32[8,1152]{1,0:T(8,128)S(1)}, f32[8,1152]{1,0:T(8,128)S(1)}, u32[]{:S(2)}, u32[]{:S(2)}) collective-permute-start(f32[8,1152]{1,0:T(8,128)S(1)} %get-tuple-element.35.rest_0_), channel_id=1, source_target_pairs={{0,2},{1,3},{2,0},{3,1},{4,6},{5,7},{6,4},{7,5},{8,10},{9,11},{10,... | collective-permute-start | bytes 110600 | tf_op jit(solution)/shard_map/ppermute | solution.py:447
  48.7 5.8 %collective-permute-start.15 = (f32[8,1152]{1,0:T(8,128)S(1)}, f32[8,1152]{1,0:T(8,128)S(1)}, u32[]{:S(2)}, u32[]{:S(2)}) collective-permute-start(f32[8,1152]{1,0:T(8,128)S(1)} %get-tuple-element.35.rest_0_), channel_id=1, source_target_pairs={{0,3},{1,2},{2,1},{3,0},{4,7},{5,6},{6,5},{7,4},{8,11},{9,10},{10,... | collective-permute-start | bytes 110600 | tf_op jit(solution)/shard_map/ppermute | solution.py:447

commit v6 on v5

--- a/solution.py
+++ b/solution.py
@@ -99,8 +99,13 @@
     return stack / jnp.sqrt(diagonal)
 
 
-def place(block_cols_ref, b, k, me_col, per_span, row_count):
-    g = block_cols_ref[k, b]
+def table_kernel(cols_ref, live_ref, table_ref):
+    slot = lax.broadcasted_iota(jnp.int32, cols_ref.shape, 0)
+    table_ref[...] = 2 * cols_ref[...] + (slot < live_ref[...]).astype(jnp.int32)
+
+
+def place(table_ref, b, k, me_col, per_span, row_count):
+    g = lax.shift_right_logical(table_ref[k, b], 1)
     span = lax.div(g, per_span)
     return (lax.div(span, row_count) ^ me_col) * per_span + lax.rem(g, per_span)
 
@@ -118,23 +123,32 @@
         at += n
 
 
-def forward_kernel(sizes, cols_ref, live_ref, even_ref, odd_ref, *rest):
+def forward_kernel(sizes, table_ref, even_ref, odd_ref, *rest):
     row_count, col_count, _, width, bs = sizes
     x_refs = rest[:col_count]
-    p_ref, blocks_ref, keep_ref, send_ref, extra_ref, picks = rest[col_count:]
+    gram_ref, blocks_ref, begun_ref, p_ref, keep_ref, send_ref, extra_ref = rest[
+        col_count : col_count + 7
+    ]
+    back_refs, picks, spread = rest[col_count + 7 : -2], rest[-2], rest[-1]
     per_span = keep_ref.shape[2] // bs
     me_col = lax.axis_index("col")
     me_row = lax.axis_index("row")
     for s in range(col_count):
         for o in range(per_span):
             picks[s * per_span + o] = split_rows(x_refs[s][:, o * bs : (o + 1) * bs])
-    pair = jnp.concatenate([x_refs[0][...], p_ref[...]], axis=0)
-    gram = four_pass(dot_nt, pair, pair)
+    gram = gram_ref[...]
+    spread[...] = begun_ref[...]
+    n = odd_ref.shape[0]
+    backward_spans(sizes, 1, table_ref, odd_ref, blocks_ref, spread, 0, n)
+    for s, back_ref in enumerate(back_refs):
+        for o in range(per_span):
+            back_ref[:width, o * bs : (o + 1) * bs] = spread[s * per_span + o]
+        back_ref[width:] = p_ref[...]
 
     def two_spans(h, cross):
         for i, (out_ref, rows_ref) in enumerate(((keep_ref, even_ref), (send_ref, odd_ref))):
             forward = forward_span(
-                sizes, 2 * h + i, cols_ref, live_ref, picks, blocks_ref, per_span, me_row, me_col
+                sizes, 2 * h + i, table_ref, picks, blocks_ref, per_span, me_row, me_col
             )
             out_ref[h] = forward
             cross = cross + three_pass(dot_nt, rows_ref[h], forward)
@@ -147,7 +161,7 @@
 
 
 def forward_span(
-    sizes, s, cols_ref, live_ref, picks, blocks_ref, per_span, me_row, me_col
+    sizes, s, table_ref, picks, blocks_ref, per_span, me_row, me_col
 ):
     row_count, _, slots, _, _ = sizes
     n = picks.shape[1] // 2
@@ -156,8 +170,8 @@
         b = (me_row ^ s) * per_span + o
         tiles, chosen = [], []
         for k in range(slots):
-            w = (k < live_ref[0, b]).astype(f32)
-            at = place(cols_ref, b, k, me_col, per_span, row_count)
+            w = (table_ref[k, b] & 1).astype(f32)
+            at = place(table_ref, b, k, me_col, per_span, row_count)
             tiles.append(blocks_ref[b, k])
             chosen.append(picks[at] * w.astype(bf16))
         both = dot_nt(jnp.concatenate(chosen, axis=1), jnp.concatenate(tiles, axis=1), None)
@@ -165,7 +179,7 @@
     return jnp.concatenate(parts, axis=1)
 
 
-def backward_spans(sizes, parity, cols_ref, live_ref, rows_ref, blocks_ref, spread):
+def backward_spans(sizes, parity, table_ref, rows_ref, blocks_ref, spread, begin, end):
     row_count, _, slots, width, bs = sizes
     per_span = rows_ref.shape[2] // bs
     me_col = lax.axis_index("col")
@@ -179,29 +193,30 @@
             back = dot_nn(own[:, o * bs : (o + 1) * bs], tile, None)
             back = back[:width] + back[width:]
             for k in range(slots):
-                at = place(cols_ref, b, k, me_col, per_span, row_count)
-                w = (k < live_ref[0, b]).astype(f32)
+                at = place(table_ref, b, k, me_col, per_span, row_count)
+                w = (table_ref[k, b] & 1).astype(f32)
                 spread[at] += back[:, k * bs : (k + 1) * bs] * w
         return carry
 
-    lax.fori_loop(0, row_count // 2, one_span, 0, unroll=UNROLL)
-
-
-def back_even_kernel(sizes, cols_ref, live_ref, even_ref, blocks_ref, spread_ref):
+    lax.fori_loop(begin, end, one_span, 0, unroll=min(UNROLL, end - begin))
+
+
+def back_near_kernel(
+    sizes, table_ref, near_ref, blocks_ref, p_ref, spread_ref, gram_ref
+):
     spread_ref[...] = jnp.zeros_like(spread_ref)
-    backward_spans(sizes, 0, cols_ref, live_ref, even_ref, blocks_ref, spread_ref)
-
-
-def back_odd_kernel(sizes, cols_ref, live_ref, odd_ref, blocks_ref, begun_ref, p_ref, *rest):
-    width, bs = sizes[3:]
-    out_refs, spread = rest[:-1], rest[-1]
-    spread[...] = begun_ref[...]
-    backward_spans(sizes, 1, cols_ref, live_ref, odd_ref, blocks_ref, spread)
-    per_span = odd_ref.shape[2] // bs
-    for s, out_ref in enumerate(out_refs):
-        for o in range(per_span):
-            out_ref[:width, o * bs : (o + 1) * bs] = spread[s * per_span + o]
-        out_ref[width:] = p_ref[...]
+    pair = jnp.concatenate([near_ref[0], p_ref[...]], axis=0)
+    gram_ref[...] = four_pass(dot_nt, pair, pair)
+    n = near_ref.shape[0]
+    backward_spans(sizes, 0, table_ref, near_ref, blocks_ref, spread_ref, 0, n)
+
+
+def back_even_kernel(
+    sizes, near, table_ref, even_ref, blocks_ref, begun_ref, spread_ref
+):
+    spread_ref[...] = begun_ref[...]
+    n = even_ref.shape[0]
+    backward_spans(sizes, 0, table_ref, even_ref, blocks_ref, spread_ref, near, n)
 
 
 def put(ref, vectors, extra):
@@ -247,30 +262,29 @@
     put(out_ref, y, sums)
 
 
-def solve_kernel(col_count, width, *rest):
-    y_refs = rest[:col_count]
-    (aux_ref,) = rest[col_count:]
-    w = width
+def solve(y_refs, aux_ref, w):
     sums = tree_sum([take(y_ref[...])[1] for y_ref in y_refs])
     gram_x, xp, pp, xbx = (unpack(sums, i) for i in range(4))
     cross_x = 0.5 * (xbx + xbx.T)
     done = eliminate(jnp.concatenate([gram_x, eye(w), cross_x, xp], axis=1), w)
     inverse_l, below_p = done[:, w : 2 * w], done[:, 3 * w : 4 * w]
     coefficient = dot_tn(inverse_l, done[:, 2 * w : 3 * w])
+    minus_c_t = -coefficient.T
     aux_ref[...] = jnp.concatenate(
-        [-coefficient.T, coefficient, below_p, xp, pp, cross_x, inverse_l, gram_x], axis=1
-    )
-
-
-def forward_rest_kernel(sizes, cols_ref, live_ref, aux_ref, *rest):
+        [minus_c_t, coefficient, below_p, xp, pp, cross_x, inverse_l, gram_x], axis=1
+    )
+    return minus_c_t
+
+
+def forward_rest_kernel(sizes, table_ref, *rest):
     row_count, col_count, _, width, bs = sizes
     y_refs, x_refs, p_refs = (rest[i * col_count : (i + 1) * col_count] for i in range(3))
-    blocks_ref, out_ref, resid_ref, resid_out_ref, picks = rest[3 * col_count :]
+    blocks_ref, out_ref, resid_ref, resid_out_ref, aux_ref, picks = rest[3 * col_count :]
     span_rows = out_ref.shape[2]
     per_span = span_rows // bs
     me_col = lax.axis_index("col")
     me_row = lax.axis_index("row")
-    minus_c_t = aux_ref[:, :width]
+    minus_c_t = solve(y_refs, aux_ref, width)
     for s in range(col_count):
         rest_s = take(y_refs[s][...])[0] + dot_nn(minus_c_t, x_refs[s][...])
         if s == 0:
@@ -283,7 +297,7 @@
     def two_spans(h, carry):
         for s in (2 * h, 2 * h + 1):
             out_ref[s] = forward_span(
-                sizes, s, cols_ref, live_ref, picks, blocks_ref, per_span, me_row, me_col
+                sizes, s, table_ref, picks, blocks_ref, per_span, me_row, me_col
             )
         return carry
 
@@ -455,35 +469,47 @@
         for bit in bits:
             got = swap(even, "row", bit)
             (even,) = call(stack_kernel, "vvv", [even, got, mark], [shape(bit, *array.shape)])
-        return even, swap(even, "row", 1)
+            if bit == bits[0]:
+                near = even
+        return near, even, swap(even, "row", 1)
 
     def over_col(arrays):
         got = {s: swap(arrays[s], "col", s) for s in far}
         return [arrays[0]] + [got[s] for s in range(1, col_count)]
 
     (mark,) = call(mark_kernel, "", [], [shape(8, LANES)], cost=window)
-    cols, live = block_cols.T, live_counts.T
+    (table,) = call(
+        table_kernel,
+        "vv",
+        [block_cols.T, live_counts.T],
+        [jax.ShapeDtypeStruct(block_cols.T.shape, jnp.int32)],
+    )
     x_cols = over_col([block_vecs] * col_count)
-    x_even, x_odd = gather_rows(block_vecs)
-    (begun,) = call(
-        functools.partial(back_even_kernel, sizes),
-        "ssvv",
-        [cols, live, x_even, blocks],
-        [shape(col_blocks, width, bs)],
-    )
-    backs = call(
-        functools.partial(back_odd_kernel, sizes),
-        "ssvvvv",
-        [cols, live, x_odd, blocks, begun, direction],
-        [shape(2 * width, span_rows)] * col_count,
-        [pltpu.VMEM((col_blocks, width, bs), f32)],
-    )
-    keep, send, extra = call(
+    x_near, x_even, x_odd = gather_rows(block_vecs)
+    begun, gram = call(
+        functools.partial(back_near_kernel, sizes),
+        "svvv",
+        [table, x_near, blocks, direction],
+        [shape(col_blocks, width, bs), shape(2 * width, 2 * width)],
+    )
+    if half > x_near.shape[0]:
+        (begun,) = call(
+            functools.partial(back_even_kernel, sizes, x_near.shape[0]),
+            "svvv",
+            [table, x_even, blocks, begun],
+            [shape(col_blocks, width, bs)],
+        )
+    keep, send, extra, *backs = call(
         functools.partial(forward_kernel, sizes),
-        "ssvv" + "v" * (col_count + 2),
-        [cols, live, x_even, x_odd, *x_cols, direction, blocks],
-        [shape(half, width, span_rows)] * 2 + [shape(width // 2, LANES)],
-        [pltpu.VMEM((col_blocks, 2 * width, bs), bf16)],
+        "svv" + "v" * (col_count + 4),
+        [table, x_even, x_odd, *x_cols, gram, blocks, begun, direction],
+        [shape(half, width, span_rows)] * 2
+        + [shape(width // 2, LANES)]
+        + [shape(2 * width, span_rows)] * col_count,
+        [
+            pltpu.VMEM((col_blocks, 2 * width, bs), bf16),
+            pltpu.VMEM((col_blocks, width, bs), f32),
+        ],
     )
     got_pair = swap(send, "row", 1)
     got_extra = swap(extra, "row", 1)
@@ -510,18 +536,14 @@
         [shape(width // 2, 2 * span_rows + LANES), shape(2 * width, span_rows)],
     )
     image_cols = over_col([message] * col_count)
-    image_even, image_odd = gather_rows(image)
-    (aux,) = call(
-        functools.partial(solve_kernel, col_count, width),
-        "v" * col_count,
-        image_cols,
-        [shape(width, 8 * width)],
-    )
-    forward_rp, resid, resid_out = call(
+    _, image_even, image_odd = gather_rows(image)
+    forward_rp, resid, resid_out, aux = call(
         functools.partial(forward_rest_kernel, sizes),
-        "ssv" + "v" * (3 * col_count + 1),
-        [cols, live, aux, *image_cols, *x_cols, *got_backs, blocks],
-        [shape(row_count, 2 * width, span_rows)] + [shape(width, span_rows)] * 2,
+        "s" + "v" * (3 * col_count + 1),
+        [table, *image_cols, *x_cols, *got_backs, blocks],
+        [shape(row_count, 2 * width, span_rows)]
+        + [shape(width, span_rows)] * 2
+        + [shape(width, 8 * width)],
         [pltpu.VMEM((col_blocks, 4 * width, bs), bf16)],
     )
     cross, gram, wide = call(

time: 76.2 us -> 74.4 us (0.976)
  waiting for transfers between devices: 24.7 us -> 23 us
    ppermute x19, waiting for transfers between devices: 24.7 us -> 23 us  [swap(): lax.ppermute(array, axis, [(i, i ^ s) for i in range(lax.axis_size(axis))])]
where the time goes in v6:
time: 74.4 us; the launch traced here: 74.3 us
  starting transfers between devices  24.7 us (33%)
  waiting for transfers between devices  23 us (31%)
  Pallas kernels  14.7 us (20%)
  blocking collectives  11 us (15%)
  between operations  0.78 us (1%)
    ppermute x19, starting transfers between devices, swap(): lax.ppermute(array, axis, [(i, i ^ s) for i in range(lax.axis_size(axis))])  24.7 us
    ppermute x19, waiting for transfers between devices, swap(): lax.ppermute(array, axis, [(i, i ^ s) for i in range(lax.axis_size(axis))])  23 us
    pallas_call x16, Pallas kernels, call(): pl.pallas_call(kernel, in_specs=[spec[letter] for letter in ins], out_spe...  14.7 us
    all_to_all x1, blocking collectives, per_device(): parts = lax.all_to_all(part, ('col', 'row'), 0, 0)  11 us
  transfers between devices with their start and end apart: 19, of which 10 were waited for; matrix products, arithmetic and copies ran while one was open for 0% of the time, Pallas kernels for 9%

profile of v6, /device:TPU:0, one launch (start us, length us, event | category | flops | bytes accessed | tf_op | source)
XLA Modules:
  0.0 74.3 jit_solution(2307055018769071655)
XLA Ops:
  0.7 3.0 %collective-permute-start = (f32[16,512]{1,0:T(8,128)}, f32[16,512]{1,0:T(8,128)S(1)}, u32[]{:S(2)}, u32[]{:S(2)}) collective-permute-start(f32[16,512]{1,0:T(8,128)} %rest_4_.1), channel_id=1, source_target_pairs={{0,8},{4,12},{8,0},{12,4},{16,24},{20,28},{24,16},{28,20},{1,9},{5... | collective-permute-start | bytes 98312 | tf_op jit(solution)/shard_map/ppermute | solution.py:461
  3.7 2.1 %collective-permute-done.refs_1_ = f32[16,512]{1,0:T(8,128)S(1)} collective-permute-done((f32[16,512]{1,0:T(8,128)}, f32[16,512]{1,0:T(8,128)S(1)}, u32[]{:S(2)}, u32[]{:S(2)}) %collective-permute-start) | collective-permute-done | bytes 32800 | tf_op jit(solution)/shard_map/ppermute | solution.py:461
  5.8 2.1 %collective-permute-start.1 = (f32[2,16,512]{2,1,0:T(8,128)S(1)}, f32[2,16,512]{2,1,0:T(8,128)S(1)}, u32[]{:S(2)}, u32[]{:S(2)}) collective-permute-start(f32[2,16,512]{2,1,0:T(8,128)S(1)} %shard_map.78.refs_0_.near_ref), channel_id=1, source_target_pairs={{0,16},{4,20},{8,24},{12,28},{16,0},{20,4},{24,8},{28,12},{1,17},{... | collective-permute-start | bytes 196616 | tf_op jit(solution)/shard_map/ppermute | solution.py:461
  7.9 2.2 %collective-permute-done.1.refs_1_ = f32[2,16,512]{2,1,0:T(8,128)S(1)} collective-permute-done((f32[2,16,512]{2,1,0:T(8,128)S(1)}, f32[2,16,512]{2,1,0:T(8,128)S(1)}, u32[]{:S(2)}, u32[]{:S(2)}) %collective-permute-start.1) | collective-permute-done | bytes 65568 | tf_op jit(solution)/shard_map/ppermute | solution.py:461
  10.3 2.1 %collective-permute-start.3 = (f32[16,512]{1,0:T(8,128)S(1)}, f32[16,512]{1,0:T(8,128)S(1)}, u32[]{:S(2)}, u32[]{:S(2)}) collective-permute-start(f32[16,512]{1,0:T(8,128)S(1)} %copy-done.2), channel_id=1, source_target_pairs={{0,1},{1,0},{2,3},{3,2},{4,5},{5,4},{6,7},{7,6},{8,9},{9,8},{10,11... | collective-permute-start | bytes 98312 | tf_op jit(solution)/shard_map/ppermute | solution.py:461
  12.4 2.6 %collective-permute-start.4 = (f32[16,512]{1,0:T(8,128)S(1)}, f32[16,512]{1,0:T(8,128)S(1)}, u32[]{:S(2)}, u32[]{:S(2)}) collective-permute-start(f32[16,512]{1,0:T(8,128)S(1)} %copy-done.2), channel_id=1, source_target_pairs={{0,2},{1,3},{2,0},{3,1},{4,6},{5,7},{6,4},{7,5},{8,10},{9,11},{10,... | collective-permute-start | bytes 98312 | tf_op jit(solution)/shard_map/ppermute | solution.py:461
  15.1 0.8 %shard_map.80 = (f32[16,16,128]{2,1,0:T(8,128)S(1)}, f32[32,32]{1,0:T(8,128)S(1)}) custom-call(s32[2,32]{1,0:T(2,128)S(1)} %shard_map.76.table_ref, f32[2,16,512]{2,1,0:T(8,128)S(1)} %shard_map.78.refs_0_.near_ref, bf16[32,2,128,128]{3,2,1,0:T(8,128)(2,1)S(1)} %copy-done, f32[16,512]{1,0:T(8,128)S(1)} %copy-done.1), custom_call_target="tpu_custom_call" | custom-call | tf_op jit(solution)/shard_map/pallas_call | solution.py:450
  15.9 0.8 %shard_map.81.rest_6_ = f32[16,16,128]{2,1,0:T(8,128)S(1)} custom-call(s32[2,32]{1,0:T(2,128)S(1)} %shard_map.76.table_ref, f32[4,16,512]{2,1,0:T(8,128)S(1)} %shard_map.79.even_ref.x_ref, bf16[32,2,128,128]{3,2,1,0:T(8,128)(2,1)S(1)} %copy-done, f32[16,16,128]{2,1,0:T(8,128)S(1)} %get-tuple-element.28.begun_ref), custom_call_target="tpu_custom_call" | custom-call | tf_op jit(solution)/shard_map/pallas_call | solution.py:450
  16.7 1.2 %collective-permute-done.4.rest_2_.rest_6_ = f32[16,512]{1,0:T(8,128)S(1)} collective-permute-done((f32[16,512]{1,0:T(8,128)S(1)}, f32[16,512]{1,0:T(8,128)S(1)}, u32[]{:S(2)}, u32[]{:S(2)}) %collective-permute-start.4) | collective-permute-done | bytes 32800 | tf_op jit(solution)/shard_map/ppermute | solution.py:461
  17.8 2.9 %collective-permute-done.5.rest_3_.rest_7_ = f32[16,512]{1,0:T(8,128)S(1)} collective-permute-done((f32[16,512]{1,0:T(8,128)S(1)}, f32[16,512]{1,0:T(8,128)S(1)}, u32[]{:S(2)}, u32[]{:S(2)}) %collective-permute-start.5) | collective-permute-done | bytes 32800 | tf_op jit(solution)/shard_map/ppermute | solution.py:461
  20.7 2.7 %shard_map.82 = (f32[4,16,512]{2,1,0:T(8,128)S(1)}, f32[4,16,512]{2,1,0:T(8,128)S(1)}, f32[8,128]{1,0:T(8,128)S(1)}, f32[32,512]{1,0:T(8,128)S(1)}, f32[32,512]{...) custom-call(s32[2,32]{1,0:T(2,128)S(1)} %shard_map.76.table_ref, ...), custom_call_target="tpu_custom_call" | custom-call | tf_op jit(solution)/shard_map/pallas_call | solution.py:450
  23.4 0.5 collective-permute-start.7
  23.9 0.8 %collective-permute-done.7.got_extra_ref = f32[8,128]{1,0:T(8,128)S(1)} collective-permute-done((f32[8,128]{1,0:T(8,128)S(1)}, f32[8,128]{1,0:T(8,128)S(1)}, u32[]{:S(2)}, u32[]{:S(2)}) %collective-permute-start.7) | collective-permute-done | bytes 4128 | tf_op jit(solution)/shard_map/ppermute | solution.py:461
  24.8 1.6 %collective-permute-start.8 = (f32[2,8,1152]{2,1,0:T(8,128)S(1)}, f32[2,8,1152]{2,1,0:T(8,128)S(1)}, u32[]{:S(2)}, u32[]{:S(2)}) collective-permute-start(f32[2,8,1152]{2,1,0:T(8,128)S(1)} %get-tuple-element.33), channel_id=1, source_target_pairs={{0,16},{4,20},{8,24},{12,28},{16,0},{20,4},{24,8},{28,12},{1,17},{... | collective-permute-start | bytes 221192 | tf_op jit(solution)/shard_map/ppermute | solution.py:461
  26.4 1.0 %collective-permute-start.11 = (f32[32,512]{1,0:T(8,128)S(1)}, f32[32,512]{1,0:T(8,128)S(1)}, u32[]{:S(2)}, u32[]{:S(2)}) collective-permute-start(f32[32,512]{1,0:T(8,128)S(1)} %get-tuple-element.38), channel_id=1, source_target_pairs={{0,2},{1,3},{2,0},{3,1},{4,6},{5,7},{6,4},{7,5},{8,10},{9,11},{10,... | collective-permute-start | bytes 196616 | tf_op jit(solution)/shard_map/ppermute | solution.py:461
  27.3 3.4 %collective-permute-start.12 = (f32[32,512]{1,0:T(8,128)S(1)}, f32[32,512]{1,0:T(8,128)S(1)}, u32[]{:S(2)}, u32[]{:S(2)}) collective-permute-start(f32[32,512]{1,0:T(8,128)S(1)} %get-tuple-element.39), channel_id=1, source_target_pairs={{0,3},{1,2},{2,1},{3,0},{4,7},{5,6},{6,5},{7,4},{8,11},{9,10},{10,... | collective-permute-start | bytes 196616 | tf_op jit(solution)/shard_map/ppermute | solution.py:461
  30.8 1.6 %collective-permute-start.9 = (f32[1,8,1152]{2,1,0:T(8,128)S(1)}, f32[1,8,1152]{2,1,0:T(8,128)S(1)}, u32[]{:S(2)}, u32[]{:S(2)}) collective-permute-start(f32[1,8,1152]{2,1,0:T(8,128)S(1)} %get-tuple-element.35), channel_id=1, source_target_pairs={{0,8},{4,12},{8,0},{12,4},{16,24},{20,28},{24,16},{28,20},{1,9},{5... | collective-permute-start | bytes 110600 | tf_op jit(solution)/shard_map/ppermute | solution.py:461
  32.3 2.5 %collective-permute-done.11.refs_2_.rest_10_ = f32[32,512]{1,0:T(8,128)S(1)} collective-permute-done((f32[32,512]{1,0:T(8,128)S(1)}, f32[32,512]{1,0:T(8,128)S(1)}, u32[]{:S(2)}, u32[]{:S(2)}) %collective-permute-start.11) | collective-permute-done | bytes 65568 | tf_op jit(solution)/shard_map/ppermute | solution.py:461
  34.9 1.6 %collective-permute-start.16 = (f32[32,512]{1,0:T(8,128)S(1)}, f32[32,512]{1,0:T(8,128)S(1)}, u32[]{:S(2)}, u32[]{:S(2)}) collective-permute-start(f32[32,512]{1,0:T(8,128)S(1)} %get-tuple-element.42.refs_0_.yp_ref), channel_id=1, source_target_pairs={{0,8},{4,12},{8,0},{12,4},{16,24},{20,28},{24,16},{28,20},{1,9},{5... | collective-permute-start | bytes 196616 | tf_op jit(solution)/shard_map/ppermute | solution.py:461
  36.4 2.8 %collective-permute-done.16.refs_1_ = f32[32,512]{1,0:T(8,128)S(1)} collective-permute-done((f32[32,512]{1,0:T(8,128)S(1)}, f32[32,512]{1,0:T(8,128)S(1)}, u32[]{:S(2)}, u32[]{:S(2)}) %collective-permute-start.16) | collective-permute-done | bytes 65568 | tf_op jit(solution)/shard_map/ppermute | solution.py:461
  39.2 0.6 collective-permute-start.17
  39.8 4.5 %collective-permute-done.17.refs_1_ = f32[2,32,512]{2,1,0:T(8,128)S(1)} collective-permute-done((f32[2,32,512]{2,1,0:T(8,128)S(1)}, f32[2,32,512]{2,1,0:T(8,128)S(1)}, u32[]{:S(2)}, u32[]{:S(2)}) %collective-permute-start.17) | collective-permute-done | bytes 131104 | tf_op jit(solution)/shard_map/ppermute | solution.py:461
  44.3 1.3 %collective-permute-start.13 = (f32[8,1152]{1,0:T(8,128)S(1)}, f32[8,1152]{1,0:T(8,128)S(1)}, u32[]{:S(2)}, u32[]{:S(2)}) collective-permute-start(f32[8,1152]{1,0:T(8,128)S(1)} %get-tuple-element.40.rest_0_), channel_id=1, source_target_pairs={{0,1},{1,0},{2,3},{3,2},{4,5},{5,4},{6,7},{7,6},{8,9},{9,8},{10,11... | collective-permute-start | bytes 110600 | tf_op jit(solution)/shard_map/ppermute | solution.py:461
  45.7 1.4 %collective-permute-start.14 = (f32[8,1152]{1,0:T(8,128)S(1)}, f32[8,1152]{1,0:T(8,128)S(1)}, u32[]{:S(2)}, u32[]{:S(2)}) collective-permute-start(f32[8,1152]{1,0:T(8,128)S(1)} %get-tuple-element.40.rest_0_), channel_id=1, source_target_pairs={{0,2},{1,3},{2,0},{3,1},{4,6},{5,7},{6,4},{7,5},{8,10},{9,11},{10,... | collective-permute-start | bytes 110600 | tf_op jit(solution)/shard_map/ppermute | solution.py:461
  47.1 1.7 %collective-permute-start.15 = (f32[8,1152]{1,0:T(8,128)S(1)}, f32[8,1152]{1,0:T(8,128)S(1)}, u32[]{:S(2)}, u32[]{:S(2)}) collective-permute-start(f32[8,1152]{1,0:T(8,128)S(1)} %get-tuple-element.40.rest_0_), channel_id=1, source_target_pairs={{0,3},{1,2},{2,1},{3,0},{4,7},{5,6},{6,5},{7,4},{8,11},{9,10},{10,... | collective-permute-start | bytes 110600 | tf_op jit(solution)/shard_map/ppermute | solution.py:461
  48.8 2.5 %collective-permute-done.14.rest_2_ = f32[8,1152]{1,0:T(8,128)S(1)} collective-permute-done((f32[8,1152]{1,0:T(8,128)S(1)}, f32[8,1152]{1,0:T(8,128)S(1)}, u32[]{:S(2)}, u32[]{:S(2)}) %collective-permute-start.14) | collective-permute-done | bytes 36896 | tf_op jit(solution)/shard_map/ppermute | solution.py:461
  51.3 1.5 %collective-permute-done.15.rest_3_ = f32[8,1152]{1,0:T(8,128)S(1)} collective-permute-done((f32[8,1152]{1,0:T(8,128)S(1)}, f32[8,1152]{1,0:T(8,128)S(1)}, u32[]{:S(2)}, u32[]{:S(2)}) %collective-permute-start.15) | collective-permute-done | bytes 36896 | tf_op jit(solution)/shard_map/ppermute | solution.py:461
  52.8 3.6 %shard_map.86 = (f32[8,32,512]{2,1,0:T(8,128)S(1)}, f32[16,512]{1,0:T(8,128)S(1)}, f32[16,512]{1,0:T(8,128)}, f32[16,128]{1,0:T(8,128)S(1)}) custom-call(s32[2,32]{1,0:T(2,128)S(1)} %shard_map.76.table_ref, f32[8,1152]{1,0:T(8,128)S(1)} %get-tuple-element.40.rest_0_, f32[8,1152]{1,0:T(8,128)S(1)} %collective-permute-done.13.rest_1_, ...), custom_call_target="tpu_custom_call" | custom-call | tf_op jit(solution)/shard_map/pallas_call | solution.py:450
  56.5 1.3 %shard_map.89 = (f32[32,32]{1,0:T(8,128)S(1)}, f32[16,32]{1,0:T(8,128)S(1)}, f32[32,64]{1,0:T(8,128)S(1)}) custom-call(f32[16,128]{1,0:T(8,128)S(1)} %get-tuple-element.41.aux_ref, f32[4,16,512]{2,1,0:T(8,128)S(1)} %shard_map.79.even_ref.x_ref, f32[4,32,512]{2,1,0:T(8,128)S(1)} %shard_map.88.y_ref, f32[8,32,512]{2,1,0:T(8,128)S(1)} %get-tuple-element.43.forward_ref, ...), custom_call_target="tpu_custom_call" | custom-call | tf_op jit(solution)/shard_map/pallas_call | solution.py:450
  57.7 1.2 %shard_map.90 = f32[32,8,128]{2,1,0:T(8,128)S(1)} custom-call(f32[16,128]{1,0:T(8,128)S(1)} %get-tuple-element.41.aux_ref, f32[4,16,512]{2,1,0:T(8,128)S(1)} %collective-permute-done.2.odd_ref.x_ref, f32[4,32,512]{2,1,0:T(8,128)S(1)} %collective-permute-done.18.y_ref, f32[8,32,512]{2,1,0:T(8,128)S(1)} %get-tuple-element.43.forward_ref, ...), custom_call_target="tpu_custom_call" | custom-call | tf_op jit(solution)/shard_map/pallas_call | solution.py:450
  59.0 11.0 %all_to_all.5.parts_ref = f32[32,8,128]{2,1,0:T(8,128)S(1)} all-to-all(f32[32,8,128]{2,1,0:T(8,128)S(1)} %shard_map.90), channel_id=1, replica_groups=mesh['row'=8,'col'=4] {'col','row'}, dimensions={0} | all-to-all | bytes 262144 | tf_op jit(solution)/shard_map/all_to_all | solution.py:561
  70.0 4.3 %shard_map.91 = (f32[16,512]{1,0:T(8,128)}, f32[48,48]{1,0:T(8,128)}) custom-call(f32[32,8,128]{2,1,0:T(8,128)S(1)} %all_to_all.5.parts_ref, f32[16,128]{1,0:T(8,128)S(1)} %get-tuple-element.41.aux_ref, f32[32,64]{1,0:T(8,128)S(1)} %get-tuple-element.47.wide_ref, f32[4,16,512]{2,1,0:T(8,128)S(1)} %shard_map.79.even_ref.x_ref, ...), custom_call_target="tpu_custom_call" | custom-call | tf_op jit(solution)/shard_map/pallas_call | solution.py:450
  (33 shorter events, 0.3 us)
Async XLA Ops:
  0.6 5.2 %copy-start.2 = (f32[16,512]{1,0:T(8,128)S(1)}, f32[16,512]{1,0:T(8,128)}, u32[]{:S(2)}) copy-start(f32[16,512]{1,0:T(8,128)} %rest_4_.1) | copy-start | bytes 98308
  0.6 14.4 %copy-start.3 = (s32[32,2]{0,1:T(2,128)S(1)}, s32[32,2]{0,1:T(2,128)}, u32[]{:S(2)}) copy-start(s32[32,2]{0,1:T(2,128)} %param.8) | copy-start | bytes 772
  0.7 14.4 %copy-start.4 = (s32[32,1]{0,1:T(1,128)S(1)}, s32[32,1]{0,1:T(1,128)}, u32[]{:S(2)}) copy-start(s32[32,1]{0,1:T(1,128)} %param.9) | copy-start | bytes 388
  0.7 14.4 %copy-start = (bf16[32,2,128,128]{3,2,1,0:T(8,128)(2,1)S(1)}, bf16[32,2,128,128]{3,2,1,0:T(8,128)(2,1)}, u32[]{:S(2)}) copy-start(bf16[32,2,128,128]{3,2,1,0:T(8,128)(2,1)} %rest_12_.1) | copy-start | bytes 6291460
  0.7 14.4 %copy-start.1 = (f32[16,512]{1,0:T(8,128)S(1)}, f32[16,512]{1,0:T(8,128)}, u32[]{:S(2)}) copy-start(f32[16,512]{1,0:T(8,128)} %p_ref.3) | copy-start | bytes 98308
  0.7 5.1 %collective-permute-start = (f32[16,512]{1,0:T(8,128)}, f32[16,512]{1,0:T(8,128)S(1)}, u32[]{:S(2)}, u32[]{:S(2)}) collective-permute-start(f32[16,512]{1,0:T(8,128)} %rest_4_.1), channel_id=1, source_target_pairs={{0,8},{4,12},{8,0},{12,4},{16,24},{20,28},{24,16},{28,20},{1,9},{5... | collective-permute-start | bytes 98312 | tf_op jit(solution)/shard_map/ppermute | solution.py:461
  5.8 4.4 %collective-permute-start.1 = (f32[2,16,512]{2,1,0:T(8,128)S(1)}, f32[2,16,512]{2,1,0:T(8,128)S(1)}, u32[]{:S(2)}, u32[]{:S(2)}) collective-permute-start(f32[2,16,512]{2,1,0:T(8,128)S(1)} %shard_map.78.refs_0_.near_ref), channel_id=1, source_target_pairs={{0,16},{4,20},{8,24},{12,28},{16,0},{20,4},{24,8},{28,12},{1,17},{... | collective-permute-start | bytes 196616 | tf_op jit(solution)/shard_map/ppermute | solution.py:461
  10.2 10.5 %collective-permute-start.2 = (f32[4,16,512]{2,1,0:T(8,128)S(1)}, f32[4,16,512]{2,1,0:T(8,128)S(1)}, u32[]{:S(2)}, u32[]{:S(2)}) collective-permute-start(f32[4,16,512]{2,1,0:T(8,128)S(1)} %shard_map.79.even_ref.x_ref), channel_id=1, source_target_pairs={{0,4},{4,0},{8,12},{12,8},{16,20},{20,16},{24,28},{28,24},{1,5},{5... | collective-permute-start | bytes 393224 | tf_op jit(solution)/shard_map/ppermute | solution.py:461
  10.3 6.4 %collective-permute-start.3 = (f32[16,512]{1,0:T(8,128)S(1)}, f32[16,512]{1,0:T(8,128)S(1)}, u32[]{:S(2)}, u32[]{:S(2)}) collective-permute-start(f32[16,512]{1,0:T(8,128)S(1)} %copy-done.2), channel_id=1, source_target_pairs={{0,1},{1,0},{2,3},{3,2},{4,5},{5,4},{6,7},{7,6},{8,9},{9,8},{10,11... | collective-permute-start | bytes 98312 | tf_op jit(solution)/shard_map/ppermute | solution.py:461
  12.4 5.4 %collective-permute-start.4 = (f32[16,512]{1,0:T(8,128)S(1)}, f32[16,512]{1,0:T(8,128)S(1)}, u32[]{:S(2)}, u32[]{:S(2)}) collective-permute-start(f32[16,512]{1,0:T(8,128)S(1)} %copy-done.2), channel_id=1, source_target_pairs={{0,2},{1,3},{2,0},{3,1},{4,6},{5,7},{6,4},{7,5},{8,10},{9,11},{10,... | collective-permute-start | bytes 98312 | tf_op jit(solution)/shard_map/ppermute | solution.py:461
  15.0 5.7 %collective-permute-start.5 = (f32[16,512]{1,0:T(8,128)S(1)}, f32[16,512]{1,0:T(8,128)S(1)}, u32[]{:S(2)}, u32[]{:S(2)}) collective-permute-start(f32[16,512]{1,0:T(8,128)S(1)} %copy-done.2), channel_id=1, source_target_pairs={{0,3},{1,2},{2,1},{3,0},{4,7},{5,6},{6,5},{7,4},{8,11},{9,10},{10,... | collective-permute-start | bytes 98312 | tf_op jit(solution)/shard_map/ppermute | solution.py:461
  23.4 1.4 %collective-permute-start.6 = (f32[4,16,512]{2,1,0:T(8,128)S(1)}, f32[4,16,512]{2,1,0:T(8,128)S(1)}, u32[]{:S(2)}, u32[]{:S(2)}) collective-permute-start(f32[4,16,512]{2,1,0:T(8,128)S(1)} %get-tuple-element.30), channel_id=1, source_target_pairs={{0,4},{4,0},{8,12},{12,8},{16,20},{20,16},{24,28},{28,24},{1,5},{5... | collective-permute-start | bytes 393224 | tf_op jit(solution)/shard_map/ppermute | solution.py:461
  23.4 1.4 %collective-permute-start.7 = (f32[8,128]{1,0:T(8,128)S(1)}, f32[8,128]{1,0:T(8,128)S(1)}, u32[]{:S(2)}, u32[]{:S(2)}) collective-permute-start(f32[8,128]{1,0:T(8,128)S(1)} %get-tuple-element.31.extra_ref), channel_id=1, source_target_pairs={{0,4},{4,0},{8,12},{12,8},{16,20},{20,16},{24,28},{28,24},{1,5},{5... | collective-permute-start | bytes 12296 | tf_op jit(solution)/shard_map/ppermute | solution.py:461
  24.8 6.0 %collective-permute-start.8 = (f32[2,8,1152]{2,1,0:T(8,128)S(1)}, f32[2,8,1152]{2,1,0:T(8,128)S(1)}, u32[]{:S(2)}, u32[]{:S(2)}) collective-permute-start(f32[2,8,1152]{2,1,0:T(8,128)S(1)} %get-tuple-element.33), channel_id=1, source_target_pairs={{0,16},{4,20},{8,24},{12,28},{16,0},{20,4},{24,8},{28,12},{1,17},{... | collective-permute-start | bytes 221192 | tf_op jit(solution)/shard_map/ppermute | solution.py:461
  26.4 6.0 %collective-permute-start.10 = (f32[32,512]{1,0:T(8,128)S(1)}, f32[32,512]{1,0:T(8,128)S(1)}, u32[]{:S(2)}, u32[]{:S(2)}) collective-permute-start(f32[32,512]{1,0:T(8,128)S(1)} %get-tuple-element.37), channel_id=1, source_target_pairs={{0,1},{1,0},{2,3},{3,2},{4,5},{5,4},{6,7},{7,6},{8,9},{9,8},{10,11... | collective-permute-start | bytes 196616 | tf_op jit(solution)/shard_map/ppermute | solution.py:461
  26.4 8.5 %collective-permute-start.11 = (f32[32,512]{1,0:T(8,128)S(1)}, f32[32,512]{1,0:T(8,128)S(1)}, u32[]{:S(2)}, u32[]{:S(2)}) collective-permute-start(f32[32,512]{1,0:T(8,128)S(1)} %get-tuple-element.38), channel_id=1, source_target_pairs={{0,2},{1,3},{2,0},{3,1},{4,6},{5,7},{6,4},{7,5},{8,10},{9,11},{10,... | collective-permute-start | bytes 196616 | tf_op jit(solution)/shard_map/ppermute | solution.py:461
  27.3 7.5 %collective-permute-start.12 = (f32[32,512]{1,0:T(8,128)S(1)}, f32[32,512]{1,0:T(8,128)S(1)}, u32[]{:S(2)}, u32[]{:S(2)}) collective-permute-start(f32[32,512]{1,0:T(8,128)S(1)} %get-tuple-element.39), channel_id=1, source_target_pairs={{0,3},{1,2},{2,1},{3,0},{4,7},{5,6},{6,5},{7,4},{8,11},{9,10},{10,... | collective-permute-start | bytes 196616 | tf_op jit(solution)/shard_map/ppermute | solution.py:461
  30.8 4.1 %collective-permute-start.9 = (f32[1,8,1152]{2,1,0:T(8,128)S(1)}, f32[1,8,1152]{2,1,0:T(8,128)S(1)}, u32[]{:S(2)}, u32[]{:S(2)}) collective-permute-start(f32[1,8,1152]{2,1,0:T(8,128)S(1)} %get-tuple-element.35), channel_id=1, source_target_pairs={{0,8},{4,12},{8,0},{12,4},{16,24},{20,28},{24,16},{28,20},{1,9},{5... | collective-permute-start | bytes 110600 | tf_op jit(solution)/shard_map/ppermute | solution.py:461
  34.9 4.3 %collective-permute-start.16 = (f32[32,512]{1,0:T(8,128)S(1)}, f32[32,512]{1,0:T(8,128)S(1)}, u32[]{:S(2)}, u32[]{:S(2)}) collective-permute-start(f32[32,512]{1,0:T(8,128)S(1)} %get-tuple-element.42.refs_0_.yp_ref), channel_id=1, source_target_pairs={{0,8},{4,12},{8,0},{12,4},{16,24},{20,28},{24,16},{28,20},{1,9},{5... | collective-permute-start | bytes 196616 | tf_op jit(solution)/shard_map/ppermute | solution.py:461
  39.2 5.0 %collective-permute-start.17 = (f32[2,32,512]{2,1,0:T(8,128)S(1)}, f32[2,32,512]{2,1,0:T(8,128)S(1)}, u32[]{:S(2)}, u32[]{:S(2)}) collective-permute-start(f32[2,32,512]{2,1,0:T(8,128)S(1)} %shard_map.87.refs_0_), channel_id=1, source_target_pairs={{0,16},{4,20},{8,24},{12,28},{16,0},{20,4},{24,8},{28,12},{1,17},{... | collective-permute-start | bytes 393224 | tf_op jit(solution)/shard_map/ppermute | solution.py:461
  44.3 13.5 %collective-permute-start.18 = (f32[4,32,512]{2,1,0:T(8,128)S(1)}, f32[4,32,512]{2,1,0:T(8,128)S(1)}, u32[]{:S(2)}, u32[]{:S(2)}) collective-permute-start(f32[4,32,512]{2,1,0:T(8,128)S(1)} %shard_map.88.y_ref), channel_id=1, source_target_pairs={{0,4},{4,0},{8,12},{12,8},{16,20},{20,16},{24,28},{28,24},{1,5},{5... | collective-permute-start | bytes 786440 | tf_op jit(solution)/shard_map/ppermute | solution.py:461
  44.3 4.5 %collective-permute-start.13 = (f32[8,1152]{1,0:T(8,128)S(1)}, f32[8,1152]{1,0:T(8,128)S(1)}, u32[]{:S(2)}, u32[]{:S(2)}) collective-permute-start(f32[8,1152]{1,0:T(8,128)S(1)} %get-tuple-element.40.rest_0_), channel_id=1, source_target_pairs={{0,1},{1,0},{2,3},{3,2},{4,5},{5,4},{6,7},{7,6},{8,9},{9,8},{10,11... | collective-permute-start | bytes 110600 | tf_op jit(solution)/shard_map/ppermute | solution.py:461
  45.7 5.6 %collective-permute-start.14 = (f32[8,1152]{1,0:T(8,128)S(1)}, f32[8,1152]{1,0:T(8,128)S(1)}, u32[]{:S(2)}, u32[]{:S(2)}) collective-permute-start(f32[8,1152]{1,0:T(8,128)S(1)} %get-tuple-element.40.rest_0_), channel_id=1, source_target_pairs={{0,2},{1,3},{2,0},{3,1},{4,6},{5,7},{6,4},{7,5},{8,10},{9,11},{10,... | collective-permute-start | bytes 110600 | tf_op jit(solution)/shard_map/ppermute | solution.py:461
  47.1 5.8 %collective-permute-start.15 = (f32[8,1152]{1,0:T(8,128)S(1)}, f32[8,1152]{1,0:T(8,128)S(1)}, u32[]{:S(2)}, u32[]{:S(2)}) collective-permute-start(f32[8,1152]{1,0:T(8,128)S(1)} %get-tuple-element.40.rest_0_), channel_id=1, source_target_pairs={{0,3},{1,2},{2,1},{3,0},{4,7},{5,6},{6,5},{7,4},{8,11},{9,10},{10,... | collective-permute-start | bytes 110600 | tf_op jit(solution)/shard_map/ppermute | solution.py:461

commit v7 on v6

--- a/solution.py
+++ b/solution.py
@@ -75,20 +75,30 @@
     m = stack.shape[1]
     row_at = lax.broadcasted_iota(jnp.int32, (n, m), 0)
     lane_at = lax.broadcasted_iota(jnp.int32, (n, m), 1)
-    for j in range(0, n - 2, 2):
-        one = jnp.broadcast_to(stack[:, j : j + 1], (n, m))
-        two = jnp.broadcast_to(stack[:, j + 1 : j + 2], (n, m))
+    spread_column = lambda i: jnp.broadcast_to(stack[:, i : i + 1], (n, m))
+
+    def solve_pair(j, one, two, lines):
         a, b, d = one[j : j + 1], two[j : j + 1], two[j + 1 : j + 2]
-        row_one, row_two = stack[j : j + 1], stack[j + 1 : j + 2]
         over = 1.0 / (a * d - b * b)
-        scaled_one = (d * row_one - b * row_two) * over
-        scaled_two = (a * row_two - b * row_one) * over
+        return [((d * u - b * v) * over, (a * v - b * u) * over) for u, v in lines]
+
+    for j in range(0, n - 2, 4):
+        one, two = spread_column(j), spread_column(j + 1)
+        lines = [(stack[j : j + 1], stack[j + 1 : j + 2])]
+        more = j + 4 < n
+        if more:
+            three, four = spread_column(j + 2), spread_column(j + 3)
+            lines += [(c[j : j + 1], c[j + 1 : j + 2]) for c in (three, four)]
+        (u, v), *at = solve_pair(j, one, two, lines)
         below = row_at > j + 1
-        stack = (
-            stack
-            - jnp.where(below, one, 0.0) * scaled_one
-            - jnp.where(below, two, 0.0) * scaled_two
-        )
+        one, two = jnp.where(below, one, 0.0), jnp.where(below, two, 0.0)
+        stack = stack - one * u - two * v
+        if more:
+            three, four = (c - one * p - two * q for c, (p, q) in zip((three, four), at))
+            k = j + 2
+            ((u, v),) = solve_pair(k, three, four, [(stack[k : k + 1], stack[k + 1 : k + 2])])
+            below = row_at > k + 1
+            stack = stack - jnp.where(below, three, 0.0) * u - jnp.where(below, four, 0.0) * v
     odd = row_at % 2 == 1
     above = jnp.concatenate([stack[n - 1 :], stack[: n - 1]], axis=0)
     pivot = jnp.sum(jnp.where(row_at == lane_at + 1, above, 0.0), axis=1, keepdims=True)

time: 74.4 us -> 73.6 us (0.989)
  Pallas kernels: 14.7 us -> 13.9 us
    pallas_call x16, Pallas kernels: 14.7 us -> 13.9 us  [call(): pl.pallas_call(kernel, in_specs=[spec[letter] for letter in ins], out_spe...]
where the time goes in v7:
time: 73.6 us; the launch traced here: 73.5 us
  starting transfers between devices  24.7 us (34%)
  waiting for transfers between devices  23 us (31%)
  Pallas kernels  13.9 us (19%)
  blocking collectives  11 us (15%)
  between operations  0.78 us (1%)
    ppermute x19, starting transfers between devices, swap(): lax.ppermute(array, axis, [(i, i ^ s) for i in range(lax.axis_size(axis))])  24.7 us
    ppermute x19, waiting for transfers between devices, swap(): lax.ppermute(array, axis, [(i, i ^ s) for i in range(lax.axis_size(axis))])  23 us
    pallas_call x16, Pallas kernels, call(): pl.pallas_call(kernel, in_specs=[spec[letter] for letter in ins], out_spe...  13.9 us
    all_to_all x1, blocking collectives, per_device(): parts = lax.all_to_all(part, ('col', 'row'), 0, 0)  11 us
  transfers between devices with their start and end apart: 19, of which 10 were waited for; matrix products, arithmetic and copies ran while one was open for 0% of the time, Pallas kernels for 9%

profile of v7, /device:TPU:0, one launch (start us, length us, event | category | flops | bytes accessed | tf_op | source)
XLA Modules:
  0.0 73.5 jit_solution(3760629377112080341)
XLA Ops:
  0.7 3.0 %collective-permute-start = (f32[16,512]{1,0:T(8,128)}, f32[16,512]{1,0:T(8,128)S(1)}, u32[]{:S(2)}, u32[]{:S(2)}) collective-permute-start(f32[16,512]{1,0:T(8,128)} %rest_4_.1), channel_id=1, source_target_pairs={{0,8},{4,12},{8,0},{12,4},{16,24},{20,28},{24,16},{28,20},{1,9},{5... | collective-permute-start | bytes 98312 | tf_op jit(solution)/shard_map/ppermute | solution.py:471
  3.7 2.1 %collective-permute-done.refs_1_ = f32[16,512]{1,0:T(8,128)S(1)} collective-permute-done((f32[16,512]{1,0:T(8,128)}, f32[16,512]{1,0:T(8,128)S(1)}, u32[]{:S(2)}, u32[]{:S(2)}) %collective-permute-start) | collective-permute-done | bytes 32800 | tf_op jit(solution)/shard_map/ppermute | solution.py:471
  5.8 2.1 %collective-permute-start.1 = (f32[2,16,512]{2,1,0:T(8,128)S(1)}, f32[2,16,512]{2,1,0:T(8,128)S(1)}, u32[]{:S(2)}, u32[]{:S(2)}) collective-permute-start(f32[2,16,512]{2,1,0:T(8,128)S(1)} %shard_map.78.refs_0_.near_ref), channel_id=1, source_target_pairs={{0,16},{4,20},{8,24},{12,28},{16,0},{20,4},{24,8},{28,12},{1,17},{... | collective-permute-start | bytes 196616 | tf_op jit(solution)/shard_map/ppermute | solution.py:471
  7.9 2.2 %collective-permute-done.1.refs_1_ = f32[2,16,512]{2,1,0:T(8,128)S(1)} collective-permute-done((f32[2,16,512]{2,1,0:T(8,128)S(1)}, f32[2,16,512]{2,1,0:T(8,128)S(1)}, u32[]{:S(2)}, u32[]{:S(2)}) %collective-permute-start.1) | collective-permute-done | bytes 65568 | tf_op jit(solution)/shard_map/ppermute | solution.py:471
  10.3 2.1 %collective-permute-start.3 = (f32[16,512]{1,0:T(8,128)S(1)}, f32[16,512]{1,0:T(8,128)S(1)}, u32[]{:S(2)}, u32[]{:S(2)}) collective-permute-start(f32[16,512]{1,0:T(8,128)S(1)} %copy-done.2), channel_id=1, source_target_pairs={{0,1},{1,0},{2,3},{3,2},{4,5},{5,4},{6,7},{7,6},{8,9},{9,8},{10,11... | collective-permute-start | bytes 98312 | tf_op jit(solution)/shard_map/ppermute | solution.py:471
  12.4 2.6 %collective-permute-start.4 = (f32[16,512]{1,0:T(8,128)S(1)}, f32[16,512]{1,0:T(8,128)S(1)}, u32[]{:S(2)}, u32[]{:S(2)}) collective-permute-start(f32[16,512]{1,0:T(8,128)S(1)} %copy-done.2), channel_id=1, source_target_pairs={{0,2},{1,3},{2,0},{3,1},{4,6},{5,7},{6,4},{7,5},{8,10},{9,11},{10,... | collective-permute-start | bytes 98312 | tf_op jit(solution)/shard_map/ppermute | solution.py:471
  15.1 0.8 %shard_map.80 = (f32[16,16,128]{2,1,0:T(8,128)S(1)}, f32[32,32]{1,0:T(8,128)S(1)}) custom-call(s32[2,32]{1,0:T(2,128)S(1)} %shard_map.76.table_ref, f32[2,16,512]{2,1,0:T(8,128)S(1)} %shard_map.78.refs_0_.near_ref, bf16[32,2,128,128]{3,2,1,0:T(8,128)(2,1)S(1)} %copy-done, f32[16,512]{1,0:T(8,128)S(1)} %copy-done.1), custom_call_target="tpu_custom_call" | custom-call | tf_op jit(solution)/shard_map/pallas_call | solution.py:460
  15.9 0.8 %shard_map.81.rest_6_ = f32[16,16,128]{2,1,0:T(8,128)S(1)} custom-call(s32[2,32]{1,0:T(2,128)S(1)} %shard_map.76.table_ref, f32[4,16,512]{2,1,0:T(8,128)S(1)} %shard_map.79.even_ref.x_ref, bf16[32,2,128,128]{3,2,1,0:T(8,128)(2,1)S(1)} %copy-done, f32[16,16,128]{2,1,0:T(8,128)S(1)} %get-tuple-element.28.begun_ref), custom_call_target="tpu_custom_call" | custom-call | tf_op jit(solution)/shard_map/pallas_call | solution.py:460
  16.7 1.2 %collective-permute-done.4.rest_2_.rest_6_ = f32[16,512]{1,0:T(8,128)S(1)} collective-permute-done((f32[16,512]{1,0:T(8,128)S(1)}, f32[16,512]{1,0:T(8,128)S(1)}, u32[]{:S(2)}, u32[]{:S(2)}) %collective-permute-start.4) | collective-permute-done | bytes 32800 | tf_op jit(solution)/shard_map/ppermute | solution.py:471
  17.8 2.9 %collective-permute-done.5.rest_3_.rest_7_ = f32[16,512]{1,0:T(8,128)S(1)} collective-permute-done((f32[16,512]{1,0:T(8,128)S(1)}, f32[16,512]{1,0:T(8,128)S(1)}, u32[]{:S(2)}, u32[]{:S(2)}) %collective-permute-start.5) | collective-permute-done | bytes 32800 | tf_op jit(solution)/shard_map/ppermute | solution.py:471
  20.7 2.7 %shard_map.82 = (f32[4,16,512]{2,1,0:T(8,128)S(1)}, f32[4,16,512]{2,1,0:T(8,128)S(1)}, f32[8,128]{1,0:T(8,128)S(1)}, f32[32,512]{1,0:T(8,128)S(1)}, f32[32,512]{...) custom-call(s32[2,32]{1,0:T(2,128)S(1)} %shard_map.76.table_ref, ...), custom_call_target="tpu_custom_call" | custom-call | tf_op jit(solution)/shard_map/pallas_call | solution.py:460
  23.4 0.5 collective-permute-start.7
  23.9 0.8 %collective-permute-done.7.got_extra_ref = f32[8,128]{1,0:T(8,128)S(1)} collective-permute-done((f32[8,128]{1,0:T(8,128)S(1)}, f32[8,128]{1,0:T(8,128)S(1)}, u32[]{:S(2)}, u32[]{:S(2)}) %collective-permute-start.7) | collective-permute-done | bytes 4128 | tf_op jit(solution)/shard_map/ppermute | solution.py:471
  24.8 1.6 %collective-permute-start.8 = (f32[2,8,1152]{2,1,0:T(8,128)S(1)}, f32[2,8,1152]{2,1,0:T(8,128)S(1)}, u32[]{:S(2)}, u32[]{:S(2)}) collective-permute-start(f32[2,8,1152]{2,1,0:T(8,128)S(1)} %get-tuple-element.33), channel_id=1, source_target_pairs={{0,16},{4,20},{8,24},{12,28},{16,0},{20,4},{24,8},{28,12},{1,17},{... | collective-permute-start | bytes 221192 | tf_op jit(solution)/shard_map/ppermute | solution.py:471
  26.4 1.0 %collective-permute-start.11 = (f32[32,512]{1,0:T(8,128)S(1)}, f32[32,512]{1,0:T(8,128)S(1)}, u32[]{:S(2)}, u32[]{:S(2)}) collective-permute-start(f32[32,512]{1,0:T(8,128)S(1)} %get-tuple-element.38), channel_id=1, source_target_pairs={{0,2},{1,3},{2,0},{3,1},{4,6},{5,7},{6,4},{7,5},{8,10},{9,11},{10,... | collective-permute-start | bytes 196616 | tf_op jit(solution)/shard_map/ppermute | solution.py:471
  27.3 3.4 %collective-permute-start.12 = (f32[32,512]{1,0:T(8,128)S(1)}, f32[32,512]{1,0:T(8,128)S(1)}, u32[]{:S(2)}, u32[]{:S(2)}) collective-permute-start(f32[32,512]{1,0:T(8,128)S(1)} %get-tuple-element.39), channel_id=1, source_target_pairs={{0,3},{1,2},{2,1},{3,0},{4,7},{5,6},{6,5},{7,4},{8,11},{9,10},{10,... | collective-permute-start | bytes 196616 | tf_op jit(solution)/shard_map/ppermute | solution.py:471
  30.8 1.6 %collective-permute-start.9 = (f32[1,8,1152]{2,1,0:T(8,128)S(1)}, f32[1,8,1152]{2,1,0:T(8,128)S(1)}, u32[]{:S(2)}, u32[]{:S(2)}) collective-permute-start(f32[1,8,1152]{2,1,0:T(8,128)S(1)} %get-tuple-element.35), channel_id=1, source_target_pairs={{0,8},{4,12},{8,0},{12,4},{16,24},{20,28},{24,16},{28,20},{1,9},{5... | collective-permute-start | bytes 110600 | tf_op jit(solution)/shard_map/ppermute | solution.py:471
  32.3 2.5 %collective-permute-done.11.refs_2_.rest_10_ = f32[32,512]{1,0:T(8,128)S(1)} collective-permute-done((f32[32,512]{1,0:T(8,128)S(1)}, f32[32,512]{1,0:T(8,128)S(1)}, u32[]{:S(2)}, u32[]{:S(2)}) %collective-permute-start.11) | collective-permute-done | bytes 65568 | tf_op jit(solution)/shard_map/ppermute | solution.py:471
  34.9 1.6 %collective-permute-start.16 = (f32[32,512]{1,0:T(8,128)S(1)}, f32[32,512]{1,0:T(8,128)S(1)}, u32[]{:S(2)}, u32[]{:S(2)}) collective-permute-start(f32[32,512]{1,0:T(8,128)S(1)} %get-tuple-element.42.refs_0_.yp_ref), channel_id=1, source_target_pairs={{0,8},{4,12},{8,0},{12,4},{16,24},{20,28},{24,16},{28,20},{1,9},{5... | collective-permute-start | bytes 196616 | tf_op jit(solution)/shard_map/ppermute | solution.py:471
  36.4 2.8 %collective-permute-done.16.refs_1_ = f32[32,512]{1,0:T(8,128)S(1)} collective-permute-done((f32[32,512]{1,0:T(8,128)S(1)}, f32[32,512]{1,0:T(8,128)S(1)}, u32[]{:S(2)}, u32[]{:S(2)}) %collective-permute-start.16) | collective-permute-done | bytes 65568 | tf_op jit(solution)/shard_map/ppermute | solution.py:471
  39.2 0.6 collective-permute-start.17
  39.8 4.5 %collective-permute-done.17.refs_1_ = f32[2,32,512]{2,1,0:T(8,128)S(1)} collective-permute-done((f32[2,32,512]{2,1,0:T(8,128)S(1)}, f32[2,32,512]{2,1,0:T(8,128)S(1)}, u32[]{:S(2)}, u32[]{:S(2)}) %collective-permute-start.17) | collective-permute-done | bytes 131104 | tf_op jit(solution)/shard_map/ppermute | solution.py:471
  44.3 1.3 %collective-permute-start.13 = (f32[8,1152]{1,0:T(8,128)S(1)}, f32[8,1152]{1,0:T(8,128)S(1)}, u32[]{:S(2)}, u32[]{:S(2)}) collective-permute-start(f32[8,1152]{1,0:T(8,128)S(1)} %get-tuple-element.40.rest_0_), channel_id=1, source_target_pairs={{0,1},{1,0},{2,3},{3,2},{4,5},{5,4},{6,7},{7,6},{8,9},{9,8},{10,11... | collective-permute-start | bytes 110600 | tf_op jit(solution)/shard_map/ppermute | solution.py:471
  45.7 1.4 %collective-permute-start.14 = (f32[8,1152]{1,0:T(8,128)S(1)}, f32[8,1152]{1,0:T(8,128)S(1)}, u32[]{:S(2)}, u32[]{:S(2)}) collective-permute-start(f32[8,1152]{1,0:T(8,128)S(1)} %get-tuple-element.40.rest_0_), channel_id=1, source_target_pairs={{0,2},{1,3},{2,0},{3,1},{4,6},{5,7},{6,4},{7,5},{8,10},{9,11},{10,... | collective-permute-start | bytes 110600 | tf_op jit(solution)/shard_map/ppermute | solution.py:471
  47.1 1.7 %collective-permute-start.15 = (f32[8,1152]{1,0:T(8,128)S(1)}, f32[8,1152]{1,0:T(8,128)S(1)}, u32[]{:S(2)}, u32[]{:S(2)}) collective-permute-start(f32[8,1152]{1,0:T(8,128)S(1)} %get-tuple-element.40.rest_0_), channel_id=1, source_target_pairs={{0,3},{1,2},{2,1},{3,0},{4,7},{5,6},{6,5},{7,4},{8,11},{9,10},{10,... | collective-permute-start | bytes 110600 | tf_op jit(solution)/shard_map/ppermute | solution.py:471
  48.8 2.5 %collective-permute-done.14.rest_2_ = f32[8,1152]{1,0:T(8,128)S(1)} collective-permute-done((f32[8,1152]{1,0:T(8,128)S(1)}, f32[8,1152]{1,0:T(8,128)S(1)}, u32[]{:S(2)}, u32[]{:S(2)}) %collective-permute-start.14) | collective-permute-done | bytes 36896 | tf_op jit(solution)/shard_map/ppermute | solution.py:471
  51.3 1.5 %collective-permute-done.15.rest_3_ = f32[8,1152]{1,0:T(8,128)S(1)} collective-permute-done((f32[8,1152]{1,0:T(8,128)S(1)}, f32[8,1152]{1,0:T(8,128)S(1)}, u32[]{:S(2)}, u32[]{:S(2)}) %collective-permute-start.15) | collective-permute-done | bytes 36896 | tf_op jit(solution)/shard_map/ppermute | solution.py:471
  52.8 3.4 %shard_map.86 = (f32[8,32,512]{2,1,0:T(8,128)S(1)}, f32[16,512]{1,0:T(8,128)S(1)}, f32[16,512]{1,0:T(8,128)}, f32[16,128]{1,0:T(8,128)S(1)}) custom-call(s32[2,32]{1,0:T(2,128)S(1)} %shard_map.76.table_ref, f32[8,1152]{1,0:T(8,128)S(1)} %get-tuple-element.40.rest_0_, f32[8,1152]{1,0:T(8,128)S(1)} %collective-permute-done.13.rest_1_, ...), custom_call_target="tpu_custom_call" | custom-call | tf_op jit(solution)/shard_map/pallas_call | solution.py:460
  56.2 1.3 %shard_map.89 = (f32[32,32]{1,0:T(8,128)S(1)}, f32[16,32]{1,0:T(8,128)S(1)}, f32[32,64]{1,0:T(8,128)S(1)}) custom-call(f32[16,128]{1,0:T(8,128)S(1)} %get-tuple-element.41.aux_ref, f32[4,16,512]{2,1,0:T(8,128)S(1)} %shard_map.79.even_ref.x_ref, f32[4,32,512]{2,1,0:T(8,128)S(1)} %shard_map.88.y_ref, f32[8,32,512]{2,1,0:T(8,128)S(1)} %get-tuple-element.43.forward_ref, ...), custom_call_target="tpu_custom_call" | custom-call | tf_op jit(solution)/shard_map/pallas_call | solution.py:460
  57.5 1.2 %shard_map.90 = f32[32,8,128]{2,1,0:T(8,128)S(1)} custom-call(f32[16,128]{1,0:T(8,128)S(1)} %get-tuple-element.41.aux_ref, f32[4,16,512]{2,1,0:T(8,128)S(1)} %collective-permute-done.2.odd_ref.x_ref, f32[4,32,512]{2,1,0:T(8,128)S(1)} %collective-permute-done.18.y_ref, f32[8,32,512]{2,1,0:T(8,128)S(1)} %get-tuple-element.43.forward_ref, ...), custom_call_target="tpu_custom_call" | custom-call | tf_op jit(solution)/shard_map/pallas_call | solution.py:460
  58.8 11.0 %all_to_all.5.parts_ref = f32[32,8,128]{2,1,0:T(8,128)S(1)} all-to-all(f32[32,8,128]{2,1,0:T(8,128)S(1)} %shard_map.90), channel_id=1, replica_groups=mesh['row'=8,'col'=4] {'col','row'}, dimensions={0} | all-to-all | bytes 262144 | tf_op jit(solution)/shard_map/all_to_all | solution.py:571
  69.8 3.7 %shard_map.91 = (f32[16,512]{1,0:T(8,128)}, f32[48,48]{1,0:T(8,128)}) custom-call(f32[32,8,128]{2,1,0:T(8,128)S(1)} %all_to_all.5.parts_ref, f32[16,128]{1,0:T(8,128)S(1)} %get-tuple-element.41.aux_ref, f32[32,64]{1,0:T(8,128)S(1)} %get-tuple-element.47.wide_ref, f32[4,16,512]{2,1,0:T(8,128)S(1)} %shard_map.79.even_ref.x_ref, ...), custom_call_target="tpu_custom_call" | custom-call | tf_op jit(solution)/shard_map/pallas_call | solution.py:460
  (33 shorter events, 0.3 us)
Async XLA Ops:
  0.6 5.2 %copy-start.2 = (f32[16,512]{1,0:T(8,128)S(1)}, f32[16,512]{1,0:T(8,128)}, u32[]{:S(2)}) copy-start(f32[16,512]{1,0:T(8,128)} %rest_4_.1) | copy-start | bytes 98308
  0.6 14.4 %copy-start.3 = (s32[32,2]{0,1:T(2,128)S(1)}, s32[32,2]{0,1:T(2,128)}, u32[]{:S(2)}) copy-start(s32[32,2]{0,1:T(2,128)} %param.8) | copy-start | bytes 772
  0.7 14.4 %copy-start.4 = (s32[32,1]{0,1:T(1,128)S(1)}, s32[32,1]{0,1:T(1,128)}, u32[]{:S(2)}) copy-start(s32[32,1]{0,1:T(1,128)} %param.9) | copy-start | bytes 388
  0.7 14.4 %copy-start = (bf16[32,2,128,128]{3,2,1,0:T(8,128)(2,1)S(1)}, bf16[32,2,128,128]{3,2,1,0:T(8,128)(2,1)}, u32[]{:S(2)}) copy-start(bf16[32,2,128,128]{3,2,1,0:T(8,128)(2,1)} %rest_12_.1) | copy-start | bytes 6291460
  0.7 14.4 %copy-start.1 = (f32[16,512]{1,0:T(8,128)S(1)}, f32[16,512]{1,0:T(8,128)}, u32[]{:S(2)}) copy-start(f32[16,512]{1,0:T(8,128)} %p_ref.3) | copy-start | bytes 98308
  0.7 5.1 %collective-permute-start = (f32[16,512]{1,0:T(8,128)}, f32[16,512]{1,0:T(8,128)S(1)}, u32[]{:S(2)}, u32[]{:S(2)}) collective-permute-start(f32[16,512]{1,0:T(8,128)} %rest_4_.1), channel_id=1, source_target_pairs={{0,8},{4,12},{8,0},{12,4},{16,24},{20,28},{24,16},{28,20},{1,9},{5... | collective-permute-start | bytes 98312 | tf_op jit(solution)/shard_map/ppermute | solution.py:471
  5.8 4.4 %collective-permute-start.1 = (f32[2,16,512]{2,1,0:T(8,128)S(1)}, f32[2,16,512]{2,1,0:T(8,128)S(1)}, u32[]{:S(2)}, u32[]{:S(2)}) collective-permute-start(f32[2,16,512]{2,1,0:T(8,128)S(1)} %shard_map.78.refs_0_.near_ref), channel_id=1, source_target_pairs={{0,16},{4,20},{8,24},{12,28},{16,0},{20,4},{24,8},{28,12},{1,17},{... | collective-permute-start | bytes 196616 | tf_op jit(solution)/shard_map/ppermute | solution.py:471
  10.2 10.5 %collective-permute-start.2 = (f32[4,16,512]{2,1,0:T(8,128)S(1)}, f32[4,16,512]{2,1,0:T(8,128)S(1)}, u32[]{:S(2)}, u32[]{:S(2)}) collective-permute-start(f32[4,16,512]{2,1,0:T(8,128)S(1)} %shard_map.79.even_ref.x_ref), channel_id=1, source_target_pairs={{0,4},{4,0},{8,12},{12,8},{16,20},{20,16},{24,28},{28,24},{1,5},{5... | collective-permute-start | bytes 393224 | tf_op jit(solution)/shard_map/ppermute | solution.py:471
  10.3 6.4 %collective-permute-start.3 = (f32[16,512]{1,0:T(8,128)S(1)}, f32[16,512]{1,0:T(8,128)S(1)}, u32[]{:S(2)}, u32[]{:S(2)}) collective-permute-start(f32[16,512]{1,0:T(8,128)S(1)} %copy-done.2), channel_id=1, source_target_pairs={{0,1},{1,0},{2,3},{3,2},{4,5},{5,4},{6,7},{7,6},{8,9},{9,8},{10,11... | collective-permute-start | bytes 98312 | tf_op jit(solution)/shard_map/ppermute | solution.py:471
  12.4 5.4 %collective-permute-start.4 = (f32[16,512]{1,0:T(8,128)S(1)}, f32[16,512]{1,0:T(8,128)S(1)}, u32[]{:S(2)}, u32[]{:S(2)}) collective-permute-start(f32[16,512]{1,0:T(8,128)S(1)} %copy-done.2), channel_id=1, source_target_pairs={{0,2},{1,3},{2,0},{3,1},{4,6},{5,7},{6,4},{7,5},{8,10},{9,11},{10,... | collective-permute-start | bytes 98312 | tf_op jit(solution)/shard_map/ppermute | solution.py:471
  15.0 5.7 %collective-permute-start.5 = (f32[16,512]{1,0:T(8,128)S(1)}, f32[16,512]{1,0:T(8,128)S(1)}, u32[]{:S(2)}, u32[]{:S(2)}) collective-permute-start(f32[16,512]{1,0:T(8,128)S(1)} %copy-done.2), channel_id=1, source_target_pairs={{0,3},{1,2},{2,1},{3,0},{4,7},{5,6},{6,5},{7,4},{8,11},{9,10},{10,... | collective-permute-start | bytes 98312 | tf_op jit(solution)/shard_map/ppermute | solution.py:471
  23.4 1.4 %collective-permute-start.6 = (f32[4,16,512]{2,1,0:T(8,128)S(1)}, f32[4,16,512]{2,1,0:T(8,128)S(1)}, u32[]{:S(2)}, u32[]{:S(2)}) collective-permute-start(f32[4,16,512]{2,1,0:T(8,128)S(1)} %get-tuple-element.30), channel_id=1, source_target_pairs={{0,4},{4,0},{8,12},{12,8},{16,20},{20,16},{24,28},{28,24},{1,5},{5... | collective-permute-start | bytes 393224 | tf_op jit(solution)/shard_map/ppermute | solution.py:471
  23.4 1.4 %collective-permute-start.7 = (f32[8,128]{1,0:T(8,128)S(1)}, f32[8,128]{1,0:T(8,128)S(1)}, u32[]{:S(2)}, u32[]{:S(2)}) collective-permute-start(f32[8,128]{1,0:T(8,128)S(1)} %get-tuple-element.31.extra_ref), channel_id=1, source_target_pairs={{0,4},{4,0},{8,12},{12,8},{16,20},{20,16},{24,28},{28,24},{1,5},{5... | collective-permute-start | bytes 12296 | tf_op jit(solution)/shard_map/ppermute | solution.py:471
  24.8 6.0 %collective-permute-start.8 = (f32[2,8,1152]{2,1,0:T(8,128)S(1)}, f32[2,8,1152]{2,1,0:T(8,128)S(1)}, u32[]{:S(2)}, u32[]{:S(2)}) collective-permute-start(f32[2,8,1152]{2,1,0:T(8,128)S(1)} %get-tuple-element.33), channel_id=1, source_target_pairs={{0,16},{4,20},{8,24},{12,28},{16,0},{20,4},{24,8},{28,12},{1,17},{... | collective-permute-start | bytes 221192 | tf_op jit(solution)/shard_map/ppermute | solution.py:471
  26.4 6.0 %collective-permute-start.10 = (f32[32,512]{1,0:T(8,128)S(1)}, f32[32,512]{1,0:T(8,128)S(1)}, u32[]{:S(2)}, u32[]{:S(2)}) collective-permute-start(f32[32,512]{1,0:T(8,128)S(1)} %get-tuple-element.37), channel_id=1, source_target_pairs={{0,1},{1,0},{2,3},{3,2},{4,5},{5,4},{6,7},{7,6},{8,9},{9,8},{10,11... | collective-permute-start | bytes 196616 | tf_op jit(solution)/shard_map/ppermute | solution.py:471
  26.4 8.5 %collective-permute-start.11 = (f32[32,512]{1,0:T(8,128)S(1)}, f32[32,512]{1,0:T(8,128)S(1)}, u32[]{:S(2)}, u32[]{:S(2)}) collective-permute-start(f32[32,512]{1,0:T(8,128)S(1)} %get-tuple-element.38), channel_id=1, source_target_pairs={{0,2},{1,3},{2,0},{3,1},{4,6},{5,7},{6,4},{7,5},{8,10},{9,11},{10,... | collective-permute-start | bytes 196616 | tf_op jit(solution)/shard_map/ppermute | solution.py:471
  27.3 7.5 %collective-permute-start.12 = (f32[32,512]{1,0:T(8,128)S(1)}, f32[32,512]{1,0:T(8,128)S(1)}, u32[]{:S(2)}, u32[]{:S(2)}) collective-permute-start(f32[32,512]{1,0:T(8,128)S(1)} %get-tuple-element.39), channel_id=1, source_target_pairs={{0,3},{1,2},{2,1},{3,0},{4,7},{5,6},{6,5},{7,4},{8,11},{9,10},{10,... | collective-permute-start | bytes 196616 | tf_op jit(solution)/shard_map/ppermute | solution.py:471
  30.8 4.1 %collective-permute-start.9 = (f32[1,8,1152]{2,1,0:T(8,128)S(1)}, f32[1,8,1152]{2,1,0:T(8,128)S(1)}, u32[]{:S(2)}, u32[]{:S(2)}) collective-permute-start(f32[1,8,1152]{2,1,0:T(8,128)S(1)} %get-tuple-element.35), channel_id=1, source_target_pairs={{0,8},{4,12},{8,0},{12,4},{16,24},{20,28},{24,16},{28,20},{1,9},{5... | collective-permute-start | bytes 110600 | tf_op jit(solution)/shard_map/ppermute | solution.py:471
  34.9 4.3 %collective-permute-start.16 = (f32[32,512]{1,0:T(8,128)S(1)}, f32[32,512]{1,0:T(8,128)S(1)}, u32[]{:S(2)}, u32[]{:S(2)}) collective-permute-start(f32[32,512]{1,0:T(8,128)S(1)} %get-tuple-element.42.refs_0_.yp_ref), channel_id=1, source_target_pairs={{0,8},{4,12},{8,0},{12,4},{16,24},{20,28},{24,16},{28,20},{1,9},{5... | collective-permute-start | bytes 196616 | tf_op jit(solution)/shard_map/ppermute | solution.py:471
  39.2 5.0 %collective-permute-start.17 = (f32[2,32,512]{2,1,0:T(8,128)S(1)}, f32[2,32,512]{2,1,0:T(8,128)S(1)}, u32[]{:S(2)}, u32[]{:S(2)}) collective-permute-start(f32[2,32,512]{2,1,0:T(8,128)S(1)} %shard_map.87.refs_0_), channel_id=1, source_target_pairs={{0,16},{4,20},{8,24},{12,28},{16,0},{20,4},{24,8},{28,12},{1,17},{... | collective-permute-start | bytes 393224 | tf_op jit(solution)/shard_map/ppermute | solution.py:471
  44.3 13.3 %collective-permute-start.18 = (f32[4,32,512]{2,1,0:T(8,128)S(1)}, f32[4,32,512]{2,1,0:T(8,128)S(1)}, u32[]{:S(2)}, u32[]{:S(2)}) collective-permute-start(f32[4,32,512]{2,1,0:T(8,128)S(1)} %shard_map.88.y_ref), channel_id=1, source_target_pairs={{0,4},{4,0},{8,12},{12,8},{16,20},{20,16},{24,28},{28,24},{1,5},{5... | collective-permute-start | bytes 786440 | tf_op jit(solution)/shard_map/ppermute | solution.py:471
  44.3 4.5 %collective-permute-start.13 = (f32[8,1152]{1,0:T(8,128)S(1)}, f32[8,1152]{1,0:T(8,128)S(1)}, u32[]{:S(2)}, u32[]{:S(2)}) collective-permute-start(f32[8,1152]{1,0:T(8,128)S(1)} %get-tuple-element.40.rest_0_), channel_id=1, source_target_pairs={{0,1},{1,0},{2,3},{3,2},{4,5},{5,4},{6,7},{7,6},{8,9},{9,8},{10,11... | collective-permute-start | bytes 110600 | tf_op jit(solution)/shard_map/ppermute | solution.py:471
  45.7 5.6 %collective-permute-start.14 = (f32[8,1152]{1,0:T(8,128)S(1)}, f32[8,1152]{1,0:T(8,128)S(1)}, u32[]{:S(2)}, u32[]{:S(2)}) collective-permute-start(f32[8,1152]{1,0:T(8,128)S(1)} %get-tuple-element.40.rest_0_), channel_id=1, source_target_pairs={{0,2},{1,3},{2,0},{3,1},{4,6},{5,7},{6,4},{7,5},{8,10},{9,11},{10,... | collective-permute-start | bytes 110600 | tf_op jit(solution)/shard_map/ppermute | solution.py:471
  47.1 5.8 %collective-permute-start.15 = (f32[8,1152]{1,0:T(8,128)S(1)}, f32[8,1152]{1,0:T(8,128)S(1)}, u32[]{:S(2)}, u32[]{:S(2)}) collective-permute-start(f32[8,1152]{1,0:T(8,128)S(1)} %get-tuple-element.40.rest_0_), channel_id=1, source_target_pairs={{0,3},{1,2},{2,1},{3,0},{4,7},{5,6},{6,5},{7,4},{8,11},{9,10},{10,... | collective-permute-start | bytes 110600 | tf_op jit(solution)/shard_map/ppermute | solution.py:471

commit v8 on v7

--- a/solution.py
+++ b/solution.py
@@ -294,15 +294,22 @@
     per_span = span_rows // bs
     me_col = lax.axis_index("col")
     me_row = lax.axis_index("row")
+    w = width
+    for s in range(col_count):
+        hi, lo = split(p_refs[s][w:])
+        for o in range(per_span):
+            picks[s * per_span + o, w : 2 * w] = hi[:, o * bs : (o + 1) * bs]
+            picks[s * per_span + o, 3 * w :] = lo[:, o * bs : (o + 1) * bs]
     minus_c_t = solve(y_refs, aux_ref, width)
     for s in range(col_count):
         rest_s = take(y_refs[s][...])[0] + dot_nn(minus_c_t, x_refs[s][...])
         if s == 0:
             resid_ref[...] = rest_s
             resid_out_ref[...] = rest_s
-        both = jnp.concatenate([rest_s, p_refs[s][width:]], axis=0)
+        hi, lo = split(rest_s)
         for o in range(per_span):
-            picks[s * per_span + o] = split_rows(both[:, o * bs : (o + 1) * bs])
+            picks[s * per_span + o, :w] = hi[:, o * bs : (o + 1) * bs]
+            picks[s * per_span + o, 2 * w : 3 * w] = lo[:, o * bs : (o + 1) * bs]
 
     def two_spans(h, carry):
         for s in (2 * h, 2 * h + 1):

time: 73.6 us -> 73.6 us (level)
  no operation moved by 1% of the time
where the time goes in v8:
time: 73.6 us; the launch traced here: 73.5 us
  starting transfers between devices  24.7 us (34%)
  waiting for transfers between devices  23 us (31%)
  Pallas kernels  13.9 us (19%)
  blocking collectives  11 us (15%)
  between operations  0.78 us (1%)
    ppermute x19, starting transfers between devices, swap(): lax.ppermute(array, axis, [(i, i ^ s) for i in range(lax.axis_size(axis))])  24.7 us
    ppermute x19, waiting for transfers between devices, swap(): lax.ppermute(array, axis, [(i, i ^ s) for i in range(lax.axis_size(axis))])  23 us
    pallas_call x16, Pallas kernels, call(): pl.pallas_call(kernel, in_specs=[spec[letter] for letter in ins], out_spe...  13.9 us
    all_to_all x1, blocking collectives, per_device(): parts = lax.all_to_all(part, ('col', 'row'), 0, 0)  11 us
  transfers between devices with their start and end apart: 19, of which 10 were waited for; matrix products, arithmetic and copies ran while one was open for 0% of the time, Pallas kernels for 9%

profile of v8, /device:TPU:0, one launch (start us, length us, event | category | flops | bytes accessed | tf_op | source)
XLA Modules:
  0.0 73.5 jit_solution(17945324726641069021)
XLA Ops:
  0.7 3.0 %collective-permute-start = (f32[16,512]{1,0:T(8,128)}, f32[16,512]{1,0:T(8,128)S(1)}, u32[]{:S(2)}, u32[]{:S(2)}) collective-permute-start(f32[16,512]{1,0:T(8,128)} %rest_4_.1), channel_id=1, source_target_pairs={{0,8},{4,12},{8,0},{12,4},{16,24},{20,28},{24,16},{28,20},{1,9},{5... | collective-permute-start | bytes 98312 | tf_op jit(solution)/shard_map/ppermute | solution.py:478
  3.7 2.1 %collective-permute-done.refs_1_ = f32[16,512]{1,0:T(8,128)S(1)} collective-permute-done((f32[16,512]{1,0:T(8,128)}, f32[16,512]{1,0:T(8,128)S(1)}, u32[]{:S(2)}, u32[]{:S(2)}) %collective-permute-start) | collective-permute-done | bytes 32800 | tf_op jit(solution)/shard_map/ppermute | solution.py:478
  5.8 2.1 %collective-permute-start.1 = (f32[2,16,512]{2,1,0:T(8,128)S(1)}, f32[2,16,512]{2,1,0:T(8,128)S(1)}, u32[]{:S(2)}, u32[]{:S(2)}) collective-permute-start(f32[2,16,512]{2,1,0:T(8,128)S(1)} %shard_map.78.refs_0_.near_ref), channel_id=1, source_target_pairs={{0,16},{4,20},{8,24},{12,28},{16,0},{20,4},{24,8},{28,12},{1,17},{... | collective-permute-start | bytes 196616 | tf_op jit(solution)/shard_map/ppermute | solution.py:478
  7.9 2.2 %collective-permute-done.1.refs_1_ = f32[2,16,512]{2,1,0:T(8,128)S(1)} collective-permute-done((f32[2,16,512]{2,1,0:T(8,128)S(1)}, f32[2,16,512]{2,1,0:T(8,128)S(1)}, u32[]{:S(2)}, u32[]{:S(2)}) %collective-permute-start.1) | collective-permute-done | bytes 65568 | tf_op jit(solution)/shard_map/ppermute | solution.py:478
  10.3 2.1 %collective-permute-start.3 = (f32[16,512]{1,0:T(8,128)S(1)}, f32[16,512]{1,0:T(8,128)S(1)}, u32[]{:S(2)}, u32[]{:S(2)}) collective-permute-start(f32[16,512]{1,0:T(8,128)S(1)} %copy-done.2), channel_id=1, source_target_pairs={{0,1},{1,0},{2,3},{3,2},{4,5},{5,4},{6,7},{7,6},{8,9},{9,8},{10,11... | collective-permute-start | bytes 98312 | tf_op jit(solution)/shard_map/ppermute | solution.py:478
  12.4 2.6 %collective-permute-start.4 = (f32[16,512]{1,0:T(8,128)S(1)}, f32[16,512]{1,0:T(8,128)S(1)}, u32[]{:S(2)}, u32[]{:S(2)}) collective-permute-start(f32[16,512]{1,0:T(8,128)S(1)} %copy-done.2), channel_id=1, source_target_pairs={{0,2},{1,3},{2,0},{3,1},{4,6},{5,7},{6,4},{7,5},{8,10},{9,11},{10,... | collective-permute-start | bytes 98312 | tf_op jit(solution)/shard_map/ppermute | solution.py:478
  15.1 0.8 %shard_map.80 = (f32[16,16,128]{2,1,0:T(8,128)S(1)}, f32[32,32]{1,0:T(8,128)S(1)}) custom-call(s32[2,32]{1,0:T(2,128)S(1)} %shard_map.76.table_ref, f32[2,16,512]{2,1,0:T(8,128)S(1)} %shard_map.78.refs_0_.near_ref, bf16[32,2,128,128]{3,2,1,0:T(8,128)(2,1)S(1)} %copy-done, f32[16,512]{1,0:T(8,128)S(1)} %copy-done.1), custom_call_target="tpu_custom_call" | custom-call | tf_op jit(solution)/shard_map/pallas_call | solution.py:467
  15.9 0.8 %shard_map.81.rest_6_ = f32[16,16,128]{2,1,0:T(8,128)S(1)} custom-call(s32[2,32]{1,0:T(2,128)S(1)} %shard_map.76.table_ref, f32[4,16,512]{2,1,0:T(8,128)S(1)} %shard_map.79.even_ref.x_ref, bf16[32,2,128,128]{3,2,1,0:T(8,128)(2,1)S(1)} %copy-done, f32[16,16,128]{2,1,0:T(8,128)S(1)} %get-tuple-element.28.begun_ref), custom_call_target="tpu_custom_call" | custom-call | tf_op jit(solution)/shard_map/pallas_call | solution.py:467
  16.7 1.2 %collective-permute-done.4.rest_2_.rest_6_ = f32[16,512]{1,0:T(8,128)S(1)} collective-permute-done((f32[16,512]{1,0:T(8,128)S(1)}, f32[16,512]{1,0:T(8,128)S(1)}, u32[]{:S(2)}, u32[]{:S(2)}) %collective-permute-start.4) | collective-permute-done | bytes 32800 | tf_op jit(solution)/shard_map/ppermute | solution.py:478
  17.8 2.9 %collective-permute-done.5.rest_3_.rest_7_ = f32[16,512]{1,0:T(8,128)S(1)} collective-permute-done((f32[16,512]{1,0:T(8,128)S(1)}, f32[16,512]{1,0:T(8,128)S(1)}, u32[]{:S(2)}, u32[]{:S(2)}) %collective-permute-start.5) | collective-permute-done | bytes 32800 | tf_op jit(solution)/shard_map/ppermute | solution.py:478
  20.7 2.7 %shard_map.82 = (f32[4,16,512]{2,1,0:T(8,128)S(1)}, f32[4,16,512]{2,1,0:T(8,128)S(1)}, f32[8,128]{1,0:T(8,128)S(1)}, f32[32,512]{1,0:T(8,128)S(1)}, f32[32,512]{...) custom-call(s32[2,32]{1,0:T(2,128)S(1)} %shard_map.76.table_ref, ...), custom_call_target="tpu_custom_call" | custom-call | tf_op jit(solution)/shard_map/pallas_call | solution.py:467
  23.4 0.5 collective-permute-start.7
  23.9 0.8 %collective-permute-done.7.got_extra_ref = f32[8,128]{1,0:T(8,128)S(1)} collective-permute-done((f32[8,128]{1,0:T(8,128)S(1)}, f32[8,128]{1,0:T(8,128)S(1)}, u32[]{:S(2)}, u32[]{:S(2)}) %collective-permute-start.7) | collective-permute-done | bytes 4128 | tf_op jit(solution)/shard_map/ppermute | solution.py:478
  24.8 1.6 %collective-permute-start.8 = (f32[2,8,1152]{2,1,0:T(8,128)S(1)}, f32[2,8,1152]{2,1,0:T(8,128)S(1)}, u32[]{:S(2)}, u32[]{:S(2)}) collective-permute-start(f32[2,8,1152]{2,1,0:T(8,128)S(1)} %get-tuple-element.33), channel_id=1, source_target_pairs={{0,16},{4,20},{8,24},{12,28},{16,0},{20,4},{24,8},{28,12},{1,17},{... | collective-permute-start | bytes 221192 | tf_op jit(solution)/shard_map/ppermute | solution.py:478
  26.4 1.0 %collective-permute-start.11 = (f32[32,512]{1,0:T(8,128)S(1)}, f32[32,512]{1,0:T(8,128)S(1)}, u32[]{:S(2)}, u32[]{:S(2)}) collective-permute-start(f32[32,512]{1,0:T(8,128)S(1)} %get-tuple-element.38), channel_id=1, source_target_pairs={{0,2},{1,3},{2,0},{3,1},{4,6},{5,7},{6,4},{7,5},{8,10},{9,11},{10,... | collective-permute-start | bytes 196616 | tf_op jit(solution)/shard_map/ppermute | solution.py:478
  27.3 3.4 %collective-permute-start.12 = (f32[32,512]{1,0:T(8,128)S(1)}, f32[32,512]{1,0:T(8,128)S(1)}, u32[]{:S(2)}, u32[]{:S(2)}) collective-permute-start(f32[32,512]{1,0:T(8,128)S(1)} %get-tuple-element.39), channel_id=1, source_target_pairs={{0,3},{1,2},{2,1},{3,0},{4,7},{5,6},{6,5},{7,4},{8,11},{9,10},{10,... | collective-permute-start | bytes 196616 | tf_op jit(solution)/shard_map/ppermute | solution.py:478
  30.8 1.6 %collective-permute-start.9 = (f32[1,8,1152]{2,1,0:T(8,128)S(1)}, f32[1,8,1152]{2,1,0:T(8,128)S(1)}, u32[]{:S(2)}, u32[]{:S(2)}) collective-permute-start(f32[1,8,1152]{2,1,0:T(8,128)S(1)} %get-tuple-element.35), channel_id=1, source_target_pairs={{0,8},{4,12},{8,0},{12,4},{16,24},{20,28},{24,16},{28,20},{1,9},{5... | collective-permute-start | bytes 110600 | tf_op jit(solution)/shard_map/ppermute | solution.py:478
  32.3 2.5 %collective-permute-done.11.refs_2_.rest_10_ = f32[32,512]{1,0:T(8,128)S(1)} collective-permute-done((f32[32,512]{1,0:T(8,128)S(1)}, f32[32,512]{1,0:T(8,128)S(1)}, u32[]{:S(2)}, u32[]{:S(2)}) %collective-permute-start.11) | collective-permute-done | bytes 65568 | tf_op jit(solution)/shard_map/ppermute | solution.py:478
  34.9 1.6 %collective-permute-start.16 = (f32[32,512]{1,0:T(8,128)S(1)}, f32[32,512]{1,0:T(8,128)S(1)}, u32[]{:S(2)}, u32[]{:S(2)}) collective-permute-start(f32[32,512]{1,0:T(8,128)S(1)} %get-tuple-element.42.refs_0_.yp_ref), channel_id=1, source_target_pairs={{0,8},{4,12},{8,0},{12,4},{16,24},{20,28},{24,16},{28,20},{1,9},{5... | collective-permute-start | bytes 196616 | tf_op jit(solution)/shard_map/ppermute | solution.py:478
  36.4 2.8 %collective-permute-done.16.refs_1_ = f32[32,512]{1,0:T(8,128)S(1)} collective-permute-done((f32[32,512]{1,0:T(8,128)S(1)}, f32[32,512]{1,0:T(8,128)S(1)}, u32[]{:S(2)}, u32[]{:S(2)}) %collective-permute-start.16) | collective-permute-done | bytes 65568 | tf_op jit(solution)/shard_map/ppermute | solution.py:478
  39.2 0.6 collective-permute-start.17
  39.8 4.5 %collective-permute-done.17.refs_1_ = f32[2,32,512]{2,1,0:T(8,128)S(1)} collective-permute-done((f32[2,32,512]{2,1,0:T(8,128)S(1)}, f32[2,32,512]{2,1,0:T(8,128)S(1)}, u32[]{:S(2)}, u32[]{:S(2)}) %collective-permute-start.17) | collective-permute-done | bytes 131104 | tf_op jit(solution)/shard_map/ppermute | solution.py:478
  44.3 1.3 %collective-permute-start.13 = (f32[8,1152]{1,0:T(8,128)S(1)}, f32[8,1152]{1,0:T(8,128)S(1)}, u32[]{:S(2)}, u32[]{:S(2)}) collective-permute-start(f32[8,1152]{1,0:T(8,128)S(1)} %get-tuple-element.40.rest_0_), channel_id=1, source_target_pairs={{0,1},{1,0},{2,3},{3,2},{4,5},{5,4},{6,7},{7,6},{8,9},{9,8},{10,11... | collective-permute-start | bytes 110600 | tf_op jit(solution)/shard_map/ppermute | solution.py:478
  45.7 1.4 %collective-permute-start.14 = (f32[8,1152]{1,0:T(8,128)S(1)}, f32[8,1152]{1,0:T(8,128)S(1)}, u32[]{:S(2)}, u32[]{:S(2)}) collective-permute-start(f32[8,1152]{1,0:T(8,128)S(1)} %get-tuple-element.40.rest_0_), channel_id=1, source_target_pairs={{0,2},{1,3},{2,0},{3,1},{4,6},{5,7},{6,4},{7,5},{8,10},{9,11},{10,... | collective-permute-start | bytes 110600 | tf_op jit(solution)/shard_map/ppermute | solution.py:478
  47.1 1.7 %collective-permute-start.15 = (f32[8,1152]{1,0:T(8,128)S(1)}, f32[8,1152]{1,0:T(8,128)S(1)}, u32[]{:S(2)}, u32[]{:S(2)}) collective-permute-start(f32[8,1152]{1,0:T(8,128)S(1)} %get-tuple-element.40.rest_0_), channel_id=1, source_target_pairs={{0,3},{1,2},{2,1},{3,0},{4,7},{5,6},{6,5},{7,4},{8,11},{9,10},{10,... | collective-permute-start | bytes 110600 | tf_op jit(solution)/shard_map/ppermute | solution.py:478
  48.8 2.5 %collective-permute-done.14.rest_2_ = f32[8,1152]{1,0:T(8,128)S(1)} collective-permute-done((f32[8,1152]{1,0:T(8,128)S(1)}, f32[8,1152]{1,0:T(8,128)S(1)}, u32[]{:S(2)}, u32[]{:S(2)}) %collective-permute-start.14) | collective-permute-done | bytes 36896 | tf_op jit(solution)/shard_map/ppermute | solution.py:478
  51.3 1.5 %collective-permute-done.15.rest_3_ = f32[8,1152]{1,0:T(8,128)S(1)} collective-permute-done((f32[8,1152]{1,0:T(8,128)S(1)}, f32[8,1152]{1,0:T(8,128)S(1)}, u32[]{:S(2)}, u32[]{:S(2)}) %collective-permute-start.15) | collective-permute-done | bytes 36896 | tf_op jit(solution)/shard_map/ppermute | solution.py:478
  52.8 3.4 %shard_map.86 = (f32[8,32,512]{2,1,0:T(8,128)S(1)}, f32[16,512]{1,0:T(8,128)S(1)}, f32[16,512]{1,0:T(8,128)}, f32[16,128]{1,0:T(8,128)S(1)}) custom-call(s32[2,32]{1,0:T(2,128)S(1)} %shard_map.76.table_ref, f32[8,1152]{1,0:T(8,128)S(1)} %get-tuple-element.40.rest_0_, f32[8,1152]{1,0:T(8,128)S(1)} %collective-permute-done.13.rest_1_, ...), custom_call_target="tpu_custom_call" | custom-call | tf_op jit(solution)/shard_map/pallas_call | solution.py:467
  56.2 1.3 %shard_map.89 = (f32[32,32]{1,0:T(8,128)S(1)}, f32[16,32]{1,0:T(8,128)S(1)}, f32[32,64]{1,0:T(8,128)S(1)}) custom-call(f32[16,128]{1,0:T(8,128)S(1)} %get-tuple-element.41.aux_ref, f32[4,16,512]{2,1,0:T(8,128)S(1)} %shard_map.79.even_ref.x_ref, f32[4,32,512]{2,1,0:T(8,128)S(1)} %shard_map.88.y_ref, f32[8,32,512]{2,1,0:T(8,128)S(1)} %get-tuple-element.43.forward_ref, ...), custom_call_target="tpu_custom_call" | custom-call | tf_op jit(solution)/shard_map/pallas_call | solution.py:467
  57.5 1.2 %shard_map.90 = f32[32,8,128]{2,1,0:T(8,128)S(1)} custom-call(f32[16,128]{1,0:T(8,128)S(1)} %get-tuple-element.41.aux_ref, f32[4,16,512]{2,1,0:T(8,128)S(1)} %collective-permute-done.2.odd_ref.x_ref, f32[4,32,512]{2,1,0:T(8,128)S(1)} %collective-permute-done.18.y_ref, f32[8,32,512]{2,1,0:T(8,128)S(1)} %get-tuple-element.43.forward_ref, ...), custom_call_target="tpu_custom_call" | custom-call | tf_op jit(solution)/shard_map/pallas_call | solution.py:467
  58.8 11.0 %all_to_all.5.parts_ref = f32[32,8,128]{2,1,0:T(8,128)S(1)} all-to-all(f32[32,8,128]{2,1,0:T(8,128)S(1)} %shard_map.90), channel_id=1, replica_groups=mesh['row'=8,'col'=4] {'col','row'}, dimensions={0} | all-to-all | bytes 262144 | tf_op jit(solution)/shard_map/all_to_all | solution.py:578
  69.8 3.7 %shard_map.91 = (f32[16,512]{1,0:T(8,128)}, f32[48,48]{1,0:T(8,128)}) custom-call(f32[32,8,128]{2,1,0:T(8,128)S(1)} %all_to_all.5.parts_ref, f32[16,128]{1,0:T(8,128)S(1)} %get-tuple-element.41.aux_ref, f32[32,64]{1,0:T(8,128)S(1)} %get-tuple-element.47.wide_ref, f32[4,16,512]{2,1,0:T(8,128)S(1)} %shard_map.79.even_ref.x_ref, ...), custom_call_target="tpu_custom_call" | custom-call | tf_op jit(solution)/shard_map/pallas_call | solution.py:467
  (33 shorter events, 0.3 us)
Async XLA Ops:
  0.6 5.2 %copy-start.2 = (f32[16,512]{1,0:T(8,128)S(1)}, f32[16,512]{1,0:T(8,128)}, u32[]{:S(2)}) copy-start(f32[16,512]{1,0:T(8,128)} %rest_4_.1) | copy-start | bytes 98308
  0.6 14.4 %copy-start.3 = (s32[32,2]{0,1:T(2,128)S(1)}, s32[32,2]{0,1:T(2,128)}, u32[]{:S(2)}) copy-start(s32[32,2]{0,1:T(2,128)} %param.8) | copy-start | bytes 772
  0.7 14.4 %copy-start.4 = (s32[32,1]{0,1:T(1,128)S(1)}, s32[32,1]{0,1:T(1,128)}, u32[]{:S(2)}) copy-start(s32[32,1]{0,1:T(1,128)} %param.9) | copy-start | bytes 388
  0.7 14.4 %copy-start = (bf16[32,2,128,128]{3,2,1,0:T(8,128)(2,1)S(1)}, bf16[32,2,128,128]{3,2,1,0:T(8,128)(2,1)}, u32[]{:S(2)}) copy-start(bf16[32,2,128,128]{3,2,1,0:T(8,128)(2,1)} %rest_12_.1) | copy-start | bytes 6291460
  0.7 14.4 %copy-start.1 = (f32[16,512]{1,0:T(8,128)S(1)}, f32[16,512]{1,0:T(8,128)}, u32[]{:S(2)}) copy-start(f32[16,512]{1,0:T(8,128)} %p_ref.3) | copy-start | bytes 98308
  0.7 5.1 %collective-permute-start = (f32[16,512]{1,0:T(8,128)}, f32[16,512]{1,0:T(8,128)S(1)}, u32[]{:S(2)}, u32[]{:S(2)}) collective-permute-start(f32[16,512]{1,0:T(8,128)} %rest_4_.1), channel_id=1, source_target_pairs={{0,8},{4,12},{8,0},{12,4},{16,24},{20,28},{24,16},{28,20},{1,9},{5... | collective-permute-start | bytes 98312 | tf_op jit(solution)/shard_map/ppermute | solution.py:478
  5.8 4.4 %collective-permute-start.1 = (f32[2,16,512]{2,1,0:T(8,128)S(1)}, f32[2,16,512]{2,1,0:T(8,128)S(1)}, u32[]{:S(2)}, u32[]{:S(2)}) collective-permute-start(f32[2,16,512]{2,1,0:T(8,128)S(1)} %shard_map.78.refs_0_.near_ref), channel_id=1, source_target_pairs={{0,16},{4,20},{8,24},{12,28},{16,0},{20,4},{24,8},{28,12},{1,17},{... | collective-permute-start | bytes 196616 | tf_op jit(solution)/shard_map/ppermute | solution.py:478
  10.2 10.5 %collective-permute-start.2 = (f32[4,16,512]{2,1,0:T(8,128)S(1)}, f32[4,16,512]{2,1,0:T(8,128)S(1)}, u32[]{:S(2)}, u32[]{:S(2)}) collective-permute-start(f32[4,16,512]{2,1,0:T(8,128)S(1)} %shard_map.79.even_ref.x_ref), channel_id=1, source_target_pairs={{0,4},{4,0},{8,12},{12,8},{16,20},{20,16},{24,28},{28,24},{1,5},{5... | collective-permute-start | bytes 393224 | tf_op jit(solution)/shard_map/ppermute | solution.py:478
  10.3 6.4 %collective-permute-start.3 = (f32[16,512]{1,0:T(8,128)S(1)}, f32[16,512]{1,0:T(8,128)S(1)}, u32[]{:S(2)}, u32[]{:S(2)}) collective-permute-start(f32[16,512]{1,0:T(8,128)S(1)} %copy-done.2), channel_id=1, source_target_pairs={{0,1},{1,0},{2,3},{3,2},{4,5},{5,4},{6,7},{7,6},{8,9},{9,8},{10,11... | collective-permute-start | bytes 98312 | tf_op jit(solution)/shard_map/ppermute | solution.py:478
  12.4 5.4 %collective-permute-start.4 = (f32[16,512]{1,0:T(8,128)S(1)}, f32[16,512]{1,0:T(8,128)S(1)}, u32[]{:S(2)}, u32[]{:S(2)}) collective-permute-start(f32[16,512]{1,0:T(8,128)S(1)} %copy-done.2), channel_id=1, source_target_pairs={{0,2},{1,3},{2,0},{3,1},{4,6},{5,7},{6,4},{7,5},{8,10},{9,11},{10,... | collective-permute-start | bytes 98312 | tf_op jit(solution)/shard_map/ppermute | solution.py:478
  15.0 5.7 %collective-permute-start.5 = (f32[16,512]{1,0:T(8,128)S(1)}, f32[16,512]{1,0:T(8,128)S(1)}, u32[]{:S(2)}, u32[]{:S(2)}) collective-permute-start(f32[16,512]{1,0:T(8,128)S(1)} %copy-done.2), channel_id=1, source_target_pairs={{0,3},{1,2},{2,1},{3,0},{4,7},{5,6},{6,5},{7,4},{8,11},{9,10},{10,... | collective-permute-start | bytes 98312 | tf_op jit(solution)/shard_map/ppermute | solution.py:478
  23.4 1.4 %collective-permute-start.6 = (f32[4,16,512]{2,1,0:T(8,128)S(1)}, f32[4,16,512]{2,1,0:T(8,128)S(1)}, u32[]{:S(2)}, u32[]{:S(2)}) collective-permute-start(f32[4,16,512]{2,1,0:T(8,128)S(1)} %get-tuple-element.30), channel_id=1, source_target_pairs={{0,4},{4,0},{8,12},{12,8},{16,20},{20,16},{24,28},{28,24},{1,5},{5... | collective-permute-start | bytes 393224 | tf_op jit(solution)/shard_map/ppermute | solution.py:478
  23.4 1.4 %collective-permute-start.7 = (f32[8,128]{1,0:T(8,128)S(1)}, f32[8,128]{1,0:T(8,128)S(1)}, u32[]{:S(2)}, u32[]{:S(2)}) collective-permute-start(f32[8,128]{1,0:T(8,128)S(1)} %get-tuple-element.31.extra_ref), channel_id=1, source_target_pairs={{0,4},{4,0},{8,12},{12,8},{16,20},{20,16},{24,28},{28,24},{1,5},{5... | collective-permute-start | bytes 12296 | tf_op jit(solution)/shard_map/ppermute | solution.py:478
  24.8 6.0 %collective-permute-start.8 = (f32[2,8,1152]{2,1,0:T(8,128)S(1)}, f32[2,8,1152]{2,1,0:T(8,128)S(1)}, u32[]{:S(2)}, u32[]{:S(2)}) collective-permute-start(f32[2,8,1152]{2,1,0:T(8,128)S(1)} %get-tuple-element.33), channel_id=1, source_target_pairs={{0,16},{4,20},{8,24},{12,28},{16,0},{20,4},{24,8},{28,12},{1,17},{... | collective-permute-start | bytes 221192 | tf_op jit(solution)/shard_map/ppermute | solution.py:478
  26.4 6.0 %collective-permute-start.10 = (f32[32,512]{1,0:T(8,128)S(1)}, f32[32,512]{1,0:T(8,128)S(1)}, u32[]{:S(2)}, u32[]{:S(2)}) collective-permute-start(f32[32,512]{1,0:T(8,128)S(1)} %get-tuple-element.37), channel_id=1, source_target_pairs={{0,1},{1,0},{2,3},{3,2},{4,5},{5,4},{6,7},{7,6},{8,9},{9,8},{10,11... | collective-permute-start | bytes 196616 | tf_op jit(solution)/shard_map/ppermute | solution.py:478
  26.4 8.5 %collective-permute-start.11 = (f32[32,512]{1,0:T(8,128)S(1)}, f32[32,512]{1,0:T(8,128)S(1)}, u32[]{:S(2)}, u32[]{:S(2)}) collective-permute-start(f32[32,512]{1,0:T(8,128)S(1)} %get-tuple-element.38), channel_id=1, source_target_pairs={{0,2},{1,3},{2,0},{3,1},{4,6},{5,7},{6,4},{7,5},{8,10},{9,11},{10,... | collective-permute-start | bytes 196616 | tf_op jit(solution)/shard_map/ppermute | solution.py:478
  27.3 7.5 %collective-permute-start.12 = (f32[32,512]{1,0:T(8,128)S(1)}, f32[32,512]{1,0:T(8,128)S(1)}, u32[]{:S(2)}, u32[]{:S(2)}) collective-permute-start(f32[32,512]{1,0:T(8,128)S(1)} %get-tuple-element.39), channel_id=1, source_target_pairs={{0,3},{1,2},{2,1},{3,0},{4,7},{5,6},{6,5},{7,4},{8,11},{9,10},{10,... | collective-permute-start | bytes 196616 | tf_op jit(solution)/shard_map/ppermute | solution.py:478
  30.8 4.1 %collective-permute-start.9 = (f32[1,8,1152]{2,1,0:T(8,128)S(1)}, f32[1,8,1152]{2,1,0:T(8,128)S(1)}, u32[]{:S(2)}, u32[]{:S(2)}) collective-permute-start(f32[1,8,1152]{2,1,0:T(8,128)S(1)} %get-tuple-element.35), channel_id=1, source_target_pairs={{0,8},{4,12},{8,0},{12,4},{16,24},{20,28},{24,16},{28,20},{1,9},{5... | collective-permute-start | bytes 110600 | tf_op jit(solution)/shard_map/ppermute | solution.py:478
  34.9 4.3 %collective-permute-start.16 = (f32[32,512]{1,0:T(8,128)S(1)}, f32[32,512]{1,0:T(8,128)S(1)}, u32[]{:S(2)}, u32[]{:S(2)}) collective-permute-start(f32[32,512]{1,0:T(8,128)S(1)} %get-tuple-element.42.refs_0_.yp_ref), channel_id=1, source_target_pairs={{0,8},{4,12},{8,0},{12,4},{16,24},{20,28},{24,16},{28,20},{1,9},{5... | collective-permute-start | bytes 196616 | tf_op jit(solution)/shard_map/ppermute | solution.py:478
  39.2 5.0 %collective-permute-start.17 = (f32[2,32,512]{2,1,0:T(8,128)S(1)}, f32[2,32,512]{2,1,0:T(8,128)S(1)}, u32[]{:S(2)}, u32[]{:S(2)}) collective-permute-start(f32[2,32,512]{2,1,0:T(8,128)S(1)} %shard_map.87.refs_0_), channel_id=1, source_target_pairs={{0,16},{4,20},{8,24},{12,28},{16,0},{20,4},{24,8},{28,12},{1,17},{... | collective-permute-start | bytes 393224 | tf_op jit(solution)/shard_map/ppermute | solution.py:478
  44.3 13.3 %collective-permute-start.18 = (f32[4,32,512]{2,1,0:T(8,128)S(1)}, f32[4,32,512]{2,1,0:T(8,128)S(1)}, u32[]{:S(2)}, u32[]{:S(2)}) collective-permute-start(f32[4,32,512]{2,1,0:T(8,128)S(1)} %shard_map.88.y_ref), channel_id=1, source_target_pairs={{0,4},{4,0},{8,12},{12,8},{16,20},{20,16},{24,28},{28,24},{1,5},{5... | collective-permute-start | bytes 786440 | tf_op jit(solution)/shard_map/ppermute | solution.py:478
  44.3 4.5 %collective-permute-start.13 = (f32[8,1152]{1,0:T(8,128)S(1)}, f32[8,1152]{1,0:T(8,128)S(1)}, u32[]{:S(2)}, u32[]{:S(2)}) collective-permute-start(f32[8,1152]{1,0:T(8,128)S(1)} %get-tuple-element.40.rest_0_), channel_id=1, source_target_pairs={{0,1},{1,0},{2,3},{3,2},{4,5},{5,4},{6,7},{7,6},{8,9},{9,8},{10,11... | collective-permute-start | bytes 110600 | tf_op jit(solution)/shard_map/ppermute | solution.py:478
  45.7 5.6 %collective-permute-start.14 = (f32[8,1152]{1,0:T(8,128)S(1)}, f32[8,1152]{1,0:T(8,128)S(1)}, u32[]{:S(2)}, u32[]{:S(2)}) collective-permute-start(f32[8,1152]{1,0:T(8,128)S(1)} %get-tuple-element.40.rest_0_), channel_id=1, source_target_pairs={{0,2},{1,3},{2,0},{3,1},{4,6},{5,7},{6,4},{7,5},{8,10},{9,11},{10,... | collective-permute-start | bytes 110600 | tf_op jit(solution)/shard_map/ppermute | solution.py:478
  47.1 5.8 %collective-permute-start.15 = (f32[8,1152]{1,0:T(8,128)S(1)}, f32[8,1152]{1,0:T(8,128)S(1)}, u32[]{:S(2)}, u32[]{:S(2)}) collective-permute-start(f32[8,1152]{1,0:T(8,128)S(1)} %get-tuple-element.40.rest_0_), channel_id=1, source_target_pairs={{0,3},{1,2},{2,1},{3,0},{4,7},{5,6},{6,5},{7,4},{8,11},{9,10},{10,... | collective-permute-start | bytes 110600 | tf_op jit(solution)/shard_map/ppermute | solution.py:478
